TPU v7x, 32 devices: a whole 2x2x4 slice. The times are simulated.
32 devices in a mesh: groups: 2 (over x), expert: 16 (over z, y, core).
Axes of the slice: x: 2, y: 2, z: 4, core: 2. Of those that a mesh axis runs over, the one named last changes fastest.
Arguments:
- tokens: bfloat16 [4096, 2048], P(('groups', 'expert')), parts along dimension 0, may hold values from -6 to 6
- out_grad: bfloat16 [4096, 2048], P(('groups', 'expert')), parts along dimension 0, may hold values from -6 to 6
- gate_probs: float32 [4096, 8], P(('groups', 'expert')), parts along dimension 0, may hold values from 0.05 to 0.2
- routes: int32 [4096, 8], P(('groups', 'expert')), parts along dimension 0, may hold values from 0 to 15, all different within a row; in each aligned block of 128 rows (0 to 127, 128 to 255, ...) at most 80 rows name the same one
- w_gate: bfloat16 [16, 2048, 384], P('expert'), may hold values from -0.125 to 0.125
- w_up: bfloat16 [16, 2048, 384], P('expert'), may hold values from -0.125 to 0.125
- w_down: bfloat16 [16, 384, 2048], P('expert'), may hold values from -0.3125 to 0.3125
Outputs:
- tokens_grad: bfloat16 [4096, 2048], P(('groups', 'expert')), parts along dimension 0
- gate_wgrad: bfloat16 [32, 2048, 384], P(('groups', 'expert')), parts along dimension 0
- up_wgrad: bfloat16 [32, 2048, 384], P(('groups', 'expert')), parts along dimension 0
- down_wgrad: bfloat16 [32, 384, 2048], P(('groups', 'expert')), parts along dimension 0
There are 2 independent parts, one for each index of `groups`. A program takes and returns all parts, laid end to end along the dimension named above; an argument that names none is the same for every part. Nothing has to cross between parts.
Inputs may be any that keep to these rules, and one draw needn't show every extreme that they name: A token's 8 experts differ. Among the 128 tokens of one block no expert is named by more than 80 routes, and in some block one expert is named by exactly 80.
All inputs are finite; a program needn't handle non-finite values.
Results may differ from a plain program's by a relative error of at most 0.0064.
Values may be sent and summed in bfloat16 or wider, within the bound.
No kernel may reach another device: no remote copies, remote signals or barrier semaphores. Data moves between devices by JAX's collectives and lax.ppermute only.
A program may use at most 128 MiB of HBM per device.

v0:
```python
import jax
import jax.numpy as jnp
from jax import lax
from jax.sharding import PartitionSpec as P


def expert_rows(inputs, grads_in, weight_gate, weight_up, weight_down):
    gate_pre = jnp.dot(inputs, weight_gate, preferred_element_type=jnp.float32)
    up_pre = jnp.dot(inputs, weight_up, preferred_element_type=jnp.float32)
    sigmoid_gate = jax.nn.sigmoid(gate_pre)
    activated = gate_pre * sigmoid_gate
    hidden = (activated * up_pre).astype(jnp.bfloat16)
    hidden_grad = jnp.dot(grads_in, weight_down.T, preferred_element_type=jnp.float32)
    up_grad = (hidden_grad * activated).astype(jnp.bfloat16)
    gate_grad = (
        hidden_grad * up_pre * sigmoid_gate * (1.0 + gate_pre * (1.0 - sigmoid_gate))
    ).astype(jnp.bfloat16)
    row_grad = (
        jnp.dot(gate_grad, weight_gate.T, preferred_element_type=jnp.float32)
        + jnp.dot(up_grad, weight_up.T, preferred_element_type=jnp.float32)
    ).astype(jnp.bfloat16)
    return (hidden, gate_grad, up_grad, row_grad)


def slot_numbers(expert_ids, experts):
    onehot = (expert_ids[:, None] == jnp.arange(experts, dtype=jnp.int32)[None, :]).astype(
        jnp.int32
    )
    running = jnp.cumsum(onehot, axis=0, dtype=jnp.int32)
    return (
        jnp.sum(running * onehot, axis=1, dtype=jnp.int32) - 1,
        jnp.sum(onehot, axis=0, dtype=jnp.int32),
    )


def local(tokens, out_grad, gate_probs, routes, w_gate, w_up, w_down):
    experts = lax.axis_size("expert")
    tok_count = tokens.shape[0]
    width = tokens.shape[1]
    top_count = routes.shape[1]
    capacity = tok_count * top_count * 5 // (4 * experts)
    row_total = experts * capacity
    weight_gate = w_gate[0]
    weight_up = w_up[0]
    weight_down = w_down[0]
    expert_ids = routes.reshape(-1)
    slots, counts = slot_numbers(expert_ids, experts)
    places = expert_ids * capacity + slots
    route_inputs = jnp.repeat(tokens, top_count, axis=0)
    route_grads = (
        (gate_probs[:, :, None] * out_grad[:, None, :].astype(jnp.float32))
        .astype(jnp.bfloat16)
        .reshape(-1, width)
    )
    send_inputs = (
        jnp.zeros((row_total, width), jnp.bfloat16)
        .at[places]
        .set(route_inputs)
        .reshape(experts, capacity, width)
    )
    send_grads = (
        jnp.zeros((row_total, width), jnp.bfloat16)
        .at[places]
        .set(route_grads)
        .reshape(experts, capacity, width)
    )
    got_inputs, got_grads = (
        lax.all_to_all(send_inputs, "expert", split_axis=0, concat_axis=0, tiled=True),
        lax.all_to_all(send_grads, "expert", split_axis=0, concat_axis=0, tiled=True),
    )
    flat_in = got_inputs.reshape(row_total, width)
    flat_grad = got_grads.reshape(row_total, width)
    hidden, gate_grad, up_grad, row_grad = expert_rows(
        flat_in, flat_grad, weight_gate, weight_up, weight_down
    )
    returned = lax.all_to_all(
        row_grad.reshape(experts, capacity, width),
        "expert",
        split_axis=0,
        concat_axis=0,
        tiled=True,
    )
    gate_acc = jnp.dot(flat_in.T, gate_grad, preferred_element_type=jnp.float32)
    up_acc = jnp.dot(flat_in.T, up_grad, preferred_element_type=jnp.float32)
    down_acc = jnp.dot(hidden.T, flat_grad, preferred_element_type=jnp.float32)
    gathered = returned.reshape(row_total, width)[places].reshape(tok_count, top_count, width)
    tokens_grad = jnp.sum(gathered, axis=1, dtype=jnp.float32).astype(jnp.bfloat16)
    gate_wgrad = gate_acc.astype(jnp.bfloat16)[None]
    up_wgrad = up_acc.astype(jnp.bfloat16)[None]
    down_wgrad = down_acc.astype(jnp.bfloat16)[None]
    return (tokens_grad, gate_wgrad, up_wgrad, down_wgrad)


def solution(mesh):
    return jax.shard_map(
        local,
        mesh=mesh,
        in_specs=(
            P(("groups", "expert"), None),
            P(("groups", "expert"), None),
            P(("groups", "expert"), None),
            P(("groups", "expert"), None),
            P("expert", None, None),
            P("expert", None, None),
            P("expert", None, None),
        ),
        out_specs=(
            P(("groups", "expert"), None),
            P(("groups", "expert"), None, None),
            P(("groups", "expert"), None, None),
            P(("groups", "expert"), None, None),
        ),
        check_vma=False,
    )
```

profile of v0, /device:TPU:13, one launch (start us, length us, event | category | flops | bytes accessed | tf_op | source)
XLA Modules:
  0.0 412.5 jit_solution(14100621843344244033)
XLA Ops:
  0.6 0.0 copy-start
  0.6 0.8 broadcast_multiply_fusion
  1.5 0.8 copy.14
  2.2 0.1 eq.29
  2.3 0.1 eq.25
  2.4 0.1 copy.13
  2.5 0.1 mul.60
  2.6 4.5 %reduce-window.6 = s32[16,8,128]{2,1,0:T(8,128)S(1)} reduce-window(s32[16,8,128]{2,1,0:T(8,128)S(1)} %fusion.26, s32[]{:T(128)} %constant.8.clone.1), window={size=1x1x128 pad=0_0x0_0x127_0}, to_apply=%region_0.0 | reduce-window | flops 2080768 | bytes 131076 | tf_op jit(solution)/shard_map/reduce-window
  7.2 0.1 slice.10
  7.2 0.1 copy.16
  7.4 0.1 copy.17
  7.5 0.1 broadcast_add_fusion
  7.6 10.1 %scatter_custom_fusion.1 = bf16[1280,2048]{1,0:T(8,128)(2,1)} fusion(s32[1024]{0:T(1024)S(1)} %bitcast.70, bf16[]{:T(256)} %constant.6.clone.1, bf16[128,2048]{1,0:T(8,128)(2,1)} %param.7), kind=kCustom, calls=%fused_computation.8 | custom fusion | bytes 5767170 | tf_op jit(solution)/shard_map/scatter | solution.py:58
  17.7 0.0 copy-start.7
  17.7 0.0 copy-start.6
  17.7 6.7 %all-to-all-start.1 = ((bf16[16,80,2048]{2,1,0:T(8,128)(2,1)}), bf16[16,80,2048]{2,1,0:T(8,128)(2,1)}, u32[]{:S(2)}, u32[]{:S(2)}) async-start(bf16[16,80,2048]{2,1,0:T(8,128)(2,1)} %bitcast.66), calls=%async_computation.1 | async-start | bytes 10485760 | tf_op jit(solution)/shard_map/all_to_all | solution.py:68
  24.4 0.0 copy-done.7
  24.4 0.1 copy.18
  24.5 0.1 mul.62
  24.6 0.0 copy-done.6
  24.6 0.1 convert_element_type.37
  24.7 10.1 %scatter_custom_fusion = bf16[1280,2048]{1,0:T(8,128)(2,1)} fusion(s32[1024]{0:T(1024)S(1)} %bitcast.71, f32[128,2048]{1,0:T(8,128)S(1)} %convert_element_type.37, f32[1024]{0:T(1024)S(1)} %mul.62, bf16[]{:T(256)} %constant.6.clone.1), kind=kCustom, calls=%fused_computation.6 | custom fusion | flops 4194304 | bytes 6295554 | tf_op jit(solution)/shard_map/scatter | solution.py:64
  34.8 104.5 %all-to-all-done.1 = bf16[16,80,2048]{2,1,0:T(8,128)(2,1)} async-done(((bf16[16,80,2048]{2,1,0:T(8,128)(2,1)}), bf16[16,80,2048]{2,1,0:T(8,128)(2,1)}, u32[]{:S(2)}, u32[]{:S(2)}) %all-to-all-start.1) | async-done | bytes 5242912 | tf_op jit(solution)/shard_map/all_to_all | solution.py:68
  139.3 4.9 %all-to-all-start = ((bf16[16,80,2048]{2,1,0:T(8,128)(2,1)}), bf16[16,80,2048]{2,1,0:T(8,128)(2,1)}, u32[]{:S(2)}, u32[]{:S(2)}) async-start(bf16[16,80,2048]{2,1,0:T(8,128)(2,1)} %bitcast.65), calls=%async_computation | async-start | bytes 10485760 | tf_op jit(solution)/shard_map/all_to_all | solution.py:69
  144.2 0.0 copy-done
  144.2 0.0 copy-start.1
  144.3 6.8 %fusion.16 = f32[1280,384]{1,0:T(8,128)} fusion(bf16[1280,2048]{1,0:T(8,128)(2,1)} %bitcast.10, bf16[1,2048,384]{2,1,0:T(8,128)(2,1)S(1)} %copy-done), kind=kOutput, calls=%fused_computation.28 | convolution fusion | flops 2013265920 | bytes 8781824 | tf_op jit(solution)/shard_map/dot_general | solution.py:8
  151.0 0.0 copy-done.1
  151.0 6.6 %fusion.19 = f32[1280,384]{1,0:T(8,128)} fusion(bf16[1280,2048]{1,0:T(8,128)(2,1)} %bitcast.10, bf16[1,2048,384]{2,1,0:T(8,128)(2,1)S(1)} %copy-done.1), kind=kOutput, calls=%fused_computation.31 | convolution fusion | flops 2013265920 | bytes 8781824 | tf_op jit(solution)/shard_map/dot_general | solution.py:9
  157.7 101.5 %all-to-all-done = bf16[16,80,2048]{2,1,0:T(8,128)(2,1)} async-done(((bf16[16,80,2048]{2,1,0:T(8,128)(2,1)}), bf16[16,80,2048]{2,1,0:T(8,128)(2,1)}, u32[]{:S(2)}, u32[]{:S(2)}) %all-to-all-start) | async-done | bytes 5242912 | tf_op jit(solution)/shard_map/all_to_all | solution.py:69
  259.2 7.5 %multiply_convert_fusion.1 = (bf16[1280,384]{1,0:T(8,128)(2,1)S(1)}, bf16[1280,384]{1,0:T(8,128)(2,1)S(1)}) fusion(f32[1280,384]{1,0:T(8,128)} %fusion.16, f32[1280,384]{1,0:T(8,128)} %fusion.19, bf16[1280,2048]{1,0:T(8,128)(2,1)} %bitcast.6, bf16[1,384,2048]{2,1,0:T(8,128)(2,1)} %param.13), kind=kOutput, calls=%fused_computation.22 | convolution fusion | flops 2019655680 | bytes 12713984 | tf_op jit(solution)/shard_map/dot_general | solution.py:13
  266.7 0.0 copy-start.2
  266.7 0.0 copy-start.4
  266.7 2.9 fusion.14
  269.7 0.0 copy-done.2
  269.7 0.0 copy-done.4
  269.7 4.7 %add_convert_fusion = bf16[1280,2048]{1,0:T(8,128)(2,1)} fusion(f32[1280,2048]{1,0:T(8,128)S(1)} %fusion.14, bf16[1280,384]{1,0:T(8,128)(2,1)S(1)} %get-tuple-element.4, bf16[1,2048,384]{2,1,0:T(8,128)(2,1)S(1)} %copy-done.1), kind=kOutput, calls=%fused_computation.3 | convolution fusion | flops 2018508800 | bytes 18284544 | tf_op jit(solution)/shard_map/dot_general | solution.py:20
  274.4 0.0 copy-start.5
  274.4 5.3 %all-to-all-start.2 = ((bf16[16,80,2048]{2,1,0:T(8,128)(2,1)}), bf16[16,80,2048]{2,1,0:T(8,128)(2,1)}, u32[]{:S(2)}, u32[]{:S(2)}) async-start(bf16[16,80,2048]{2,1,0:T(8,128)(2,1)} %bitcast.67), calls=%async_computation.2 | async-start | bytes 10485760 | tf_op jit(solution)/shard_map/all_to_all | solution.py:76
  279.7 0.0 copy-done.5
  279.7 0.0 copy-start.3
  279.7 6.6 %fusion.10 = bf16[1,2048,384]{2,1,0:T(8,128)(2,1)} fusion(bf16[1280,2048]{1,0:T(8,128)(2,1)} %bitcast.10, bf16[1280,384]{1,0:T(8,128)(2,1)S(1)} %copy-done.5), kind=kOutput, calls=%fused_computation.18 | convolution fusion | flops 2014052352 | bytes 7798784 | tf_op jit(solution)/shard_map/dot_general | solution.py:84
  286.4 0.0 copy-done.3
  286.4 0.0 copy-start.8
  286.4 0.0 copy-start.9
  286.4 6.7 %fusion.9 = bf16[1,2048,384]{2,1,0:T(8,128)(2,1)} fusion(bf16[1280,2048]{1,0:T(8,128)(2,1)} %bitcast.10, bf16[1280,384]{1,0:T(8,128)(2,1)S(1)} %copy-done.3), kind=kOutput, calls=%fused_computation.17 | convolution fusion | flops 2014052352 | bytes 7798784 | tf_op jit(solution)/shard_map/dot_general | solution.py:83
  293.1 0.0 copy-done.8
  293.1 0.0 copy-done.9
  293.1 6.0 %fusion.11 = bf16[1,384,2048]{2,1,0:T(8,128)(2,1)} fusion(bf16[1280,2048]{1,0:T(8,128)(2,1)} %bitcast.6, f32[1280,384]{1,0:T(8,128)S(1)} %copy-done.9, f32[1280,384]{1,0:T(8,128)S(1)} %copy-done.8), kind=kOutput, calls=%fused_computation.19 | convolution fusion | flops 2017001472 | bytes 10747904 | tf_op jit(solution)/shard_map/dot_general | solution.py:85
  299.1 95.5 %all-to-all-done.2 = bf16[16,80,2048]{2,1,0:T(8,128)(2,1)} async-done(((bf16[16,80,2048]{2,1,0:T(8,128)(2,1)}), bf16[16,80,2048]{2,1,0:T(8,128)(2,1)}, u32[]{:S(2)}, u32[]{:S(2)}) %all-to-all-start.2) | async-done | bytes 5242912 | tf_op jit(solution)/shard_map/all_to_all | solution.py:76
  394.6 12.0 %gather_fusion = bf16[1024,2048]{1,0:T(8,128)(2,1)} fusion(bf16[1280,2048]{1,0:T(8,128)(2,1)} %bitcast.14, s32[1024]{0:T(1024)S(1)} %broadcast_clamp_fusion), kind=kCustom, calls=%fused_computation | custom fusion | bytes 8392704 | tf_op jit(solution)/shard_map/gather | solution.py:86
  406.6 5.9 %bitcast_reduce_fusion = bf16[128,2048]{1,0:T(8,128)(2,1)} fusion(bf16[1024,2048]{1,0:T(8,128)(2,1)} %gather_fusion), kind=kLoop, calls=%fused_computation.7 | loop fusion | flops 1835008 | bytes 4718592 | tf_op jit(solution)/shard_map/reduce_sum | solution.py:87
  (7 shorter events, 0.1 us)
Async XLA Ops:
  0.6 143.6 %copy-start = (bf16[1,2048,384]{2,1,0:T(8,128)(2,1)S(1)}, bf16[1,2048,384]{2,1,0:T(8,128)(2,1)}, u32[]{:S(2)}) copy-start(bf16[1,2048,384]{2,1,0:T(8,128)(2,1)} %param.11) | copy-start | bytes 4718596
  17.7 6.7 %copy-start.7 = (f32[128,8]{0,1:T(8,128)S(1)}, f32[128,8]{0,1:T(8,128)}, u32[]{:S(2)}) copy-start(f32[128,8]{0,1:T(8,128)} %param.9) | copy-start | bytes 12292
  17.7 6.9 %copy-start.6 = (bf16[128,2048]{1,0:T(8,128)(2,1)S(1)}, bf16[128,2048]{1,0:T(8,128)(2,1)}, u32[]{:S(2)}) copy-start(bf16[128,2048]{1,0:T(8,128)(2,1)} %param.8) | copy-start | bytes 1572868
  17.7 121.6 %all-to-all-start.1 = ((bf16[16,80,2048]{2,1,0:T(8,128)(2,1)}), bf16[16,80,2048]{2,1,0:T(8,128)(2,1)}, u32[]{:S(2)}, u32[]{:S(2)}) async-start(bf16[16,80,2048]{2,1,0:T(8,128)(2,1)} %bitcast.66), calls=%async_computation.1 | async-start | bytes 10485760 | tf_op jit(solution)/shard_map/all_to_all | solution.py:68
  139.3 119.8 %all-to-all-start = ((bf16[16,80,2048]{2,1,0:T(8,128)(2,1)}), bf16[16,80,2048]{2,1,0:T(8,128)(2,1)}, u32[]{:S(2)}, u32[]{:S(2)}) async-start(bf16[16,80,2048]{2,1,0:T(8,128)(2,1)} %bitcast.65), calls=%async_computation | async-start | bytes 10485760 | tf_op jit(solution)/shard_map/all_to_all | solution.py:69
  144.2 6.8 %copy-start.1 = (bf16[1,2048,384]{2,1,0:T(8,128)(2,1)S(1)}, bf16[1,2048,384]{2,1,0:T(8,128)(2,1)}, u32[]{:S(2)}) copy-start(bf16[1,2048,384]{2,1,0:T(8,128)(2,1)} %param.12) | copy-start | bytes 4718596
  266.7 3.0 copy-start.2
  266.7 3.0 copy-start.4
  274.4 5.3 %copy-start.5 = (bf16[1280,384]{1,0:T(8,128)(2,1)S(1)}, bf16[1280,384]{1,0:T(8,128)(2,1)}, u32[]{:S(2)}) copy-start(bf16[1280,384]{1,0:T(8,128)(2,1)} %copy-done.4) | copy-start | bytes 2949124
  274.4 120.2 %all-to-all-start.2 = ((bf16[16,80,2048]{2,1,0:T(8,128)(2,1)}), bf16[16,80,2048]{2,1,0:T(8,128)(2,1)}, u32[]{:S(2)}, u32[]{:S(2)}) async-start(bf16[16,80,2048]{2,1,0:T(8,128)(2,1)} %bitcast.67), calls=%async_computation.2 | async-start | bytes 10485760 | tf_op jit(solution)/shard_map/all_to_all | solution.py:76
  279.7 6.7 %copy-start.3 = (bf16[1280,384]{1,0:T(8,128)(2,1)S(1)}, bf16[1280,384]{1,0:T(8,128)(2,1)}, u32[]{:S(2)}) copy-start(bf16[1280,384]{1,0:T(8,128)(2,1)} %copy-done.2) | copy-start | bytes 2949124
  286.4 6.7 %copy-start.8 = (f32[1280,384]{1,0:T(8,128)S(1)}, f32[1280,384]{1,0:T(8,128)}, u32[]{:S(2)}) copy-start(f32[1280,384]{1,0:T(8,128)} %fusion.16) | copy-start | bytes 5898244
  286.4 6.7 %copy-start.9 = (f32[1280,384]{1,0:T(8,128)S(1)}, f32[1280,384]{1,0:T(8,128)}, u32[]{:S(2)}) copy-start(f32[1280,384]{1,0:T(8,128)} %fusion.19) | copy-start | bytes 5898244
where the time goes:
time: 413 us; the launch traced here: 412 us
  waiting for transfers between devices  302 us (73%)
  matrix products  47.9 us (12%)
  local copies, waits for them, and re-layouts  23.7 us (6%)
  other arithmetic  21.6 us (5%)
  starting transfers between devices  16.9 us (4%)
    all_to_all x1, waiting for transfers between devices, local(): lax.all_to_all(send_inputs, 'expert', split_axis=0, concat_axis=0, tiled=...  105 us
    all_to_all x1, waiting for transfers between devices, local(): lax.all_to_all(send_grads, 'expert', split_axis=0, concat_axis=0, tiled=T...  102 us
    all_to_all x1, waiting for transfers between devices, local(): lax.all_to_all(row_grad.reshape(experts, capacity, width), 'expert', spli...  95.5 us
    gather x1, local copies, waits for them, and re-layouts, local(): returned.reshape(row_total, width)[places]  12 us
    scatter x1, other arithmetic, local(): send_grads = jnp.zeros((row_total, width), jnp.bfloat16).at[places].set(r...  10.1 us
    scatter x1, local copies, waits for them, and re-layouts, local(): send_inputs = jnp.zeros((row_total, width), jnp.bfloat16).at[places].set(...  10.1 us
  transfers between devices with their start and end apart: 3, of which 3 were waited for; matrix products, arithmetic and copies ran while one was open for 10% of the time, Pallas kernels for 0%

commit v1 on v0

v1 whole, which is shorter than its diff:
```python
import functools

import jax
import jax.numpy as jnp
from jax import lax
from jax.experimental import pallas as pl
from jax.experimental.pallas import tpu as pltpu
from jax.sharding import PartitionSpec as P

F32 = jnp.float32
BF16 = jnp.bfloat16
NN = (((1,), (0,)), ((), ()))
NT = (((1,), (1,)), ((), ()))
TN = (((0,), (0,)), ((), ()))
GROUP = 4
PARTS = 3
BLOCK_VMEM = 16 << 20
WGRAD_VMEM = 24 << 20


def mm(a, b, dims):
    return lax.dot_general(a, b, dims, preferred_element_type=F32)


def near(v):
    return pltpu.with_memory_space_constraint(v, pltpu.VMEM)


def encode(probs):
    parts = []
    rest = probs
    for _ in range(PARTS):
        top = lax.reduce_precision(rest, 8, 7)
        parts.append(top.astype(BF16))
        rest = rest - top
    coded = jnp.concatenate(parts, axis=1)
    return jnp.pad(coded, ((0, 0), (0, -coded.shape[1] % 128)))


def block_pair(me, devices, xa, xb, oa, ob, wgu, wd):
    rows, width = oa.shape
    ff = wd.shape[0]

    def body(me, xa, xb, oa, ob, wgu, wd, row_a, row_b, grads, hidden):
        x = jnp.concatenate([xa[:, :width], xb[:, :width]], axis=0)
        o = jnp.concatenate([oa[...], ob[...]], axis=0)
        coded = jnp.concatenate([xa[:, width:], xb[:, width:]], axis=0).astype(F32)
        lane = lax.broadcasted_iota(jnp.int32, coded.shape, 1)
        mine = (lane % devices == me[0]) & (lane < PARTS * devices)
        p = jnp.sum(jnp.where(mine, coded, 0.0), axis=1, keepdims=True)
        pre = mm(x, wgu[...], NN)
        gate, up = pre[:, :ff], pre[:, ff:]
        hid = p * mm(o, wd[...], NT)
        sig = jax.nn.sigmoid(gate)
        act = gate * sig
        hidden[...] = (p * (act * up)).astype(BF16)
        grads[:, :ff] = (hid * up * sig * (1.0 + gate * (1.0 - sig))).astype(BF16)
        grads[:, ff:] = (hid * act).astype(BF16)
        back = mm(grads[...], wgu[...], NT).astype(BF16)
        row_a[...] = back[:rows]
        row_b[...] = back[rows:]

    return pl.pallas_call(
        body,
        in_specs=[pl.BlockSpec(memory_space=pltpu.SMEM)]
        + [pl.BlockSpec(memory_space=pltpu.VMEM)] * 6,
        out_shape=[
            jax.ShapeDtypeStruct((rows, width), BF16),
            jax.ShapeDtypeStruct((rows, width), BF16),
            jax.ShapeDtypeStruct((2 * rows, 2 * ff), BF16),
            jax.ShapeDtypeStruct((2 * rows, ff), BF16),
        ],
        compiler_params=pltpu.CompilerParams(vmem_limit_bytes=BLOCK_VMEM),
        cost_estimate=pl.CostEstimate(
            flops=2 * (2 * rows) * width * ff * 5,
            bytes_accessed=2 * (6 * rows * width + 3 * width * ff),
            transcendentals=2 * rows * ff,
        ),
        name="block_pair",
    )(me, near(xa), near(xb), near(oa), near(ob), near(wgu), near(wd))


def wgrad_group(xs, os, grads, hiddens, acc, last, resident):
    count, pairs = len(xs), len(grads)
    rows, width = os[0].shape
    ff = hiddens[0].shape[1]
    chunk = 512 if resident else 256
    has = acc is not None

    def body(*refs):
        start = pl.multiple_of(pl.program_id(0) * chunk, chunk)
        columns = pl.ds(start, chunk) if resident else slice(None)
        x = jnp.concatenate([r[:, columns] for r in refs[:count]], axis=0)
        o = jnp.concatenate([r[:, columns] for r in refs[count : 2 * count]], axis=0)
        rest = refs[2 * count :]
        g = jnp.concatenate([r[...] for r in rest[:pairs]], axis=0)
        h = jnp.concatenate([r[...] for r in rest[pairs : 2 * pairs]], axis=0)
        rest = rest[2 * pairs :]
        gu = mm(x, g, TN)
        dn = mm(h, o, TN)
        parts = [gu[:, :ff], gu[:, ff:], dn]
        if has:
            parts = [a[...] + b for a, b in zip(rest[:3], parts)]
            rest = rest[3:]
        for r, v in zip(rest, parts):
            r[...] = v.astype(r.dtype)

    tall = pl.BlockSpec((chunk, ff), lambda j: (j, 0))
    wide = pl.BlockSpec((ff, chunk), lambda j: (0, j))
    kind = BF16 if last else F32
    acc_specs = [tall, tall, wide]
    if resident:
        inputs = [near(v) for v in (*xs, *os, *grads, *hiddens)]
        specs = [pl.BlockSpec(memory_space=pltpu.VMEM)] * len(inputs)
    else:
        inputs = [*xs, *os, *grads, *hiddens]
        specs = [pl.BlockSpec((rows, chunk), lambda j: (0, j))] * (2 * count)
        specs += [pl.BlockSpec(v.shape, lambda j: (0, 0)) for v in (*grads, *hiddens)]
    alias = {len(inputs) + i: i for i in range(3)} if has and not last else {}
    return pl.pallas_call(
        body,
        grid=(width // chunk,),
        in_specs=specs + (acc_specs if has else []),
        out_specs=acc_specs,
        out_shape=[
            jax.ShapeDtypeStruct((width, ff), kind),
            jax.ShapeDtypeStruct((width, ff), kind),
            jax.ShapeDtypeStruct((ff, width), kind),
        ],
        input_output_aliases=alias,
        compiler_params=pltpu.CompilerParams(vmem_limit_bytes=WGRAD_VMEM),
        cost_estimate=pl.CostEstimate(
            flops=2 * count * rows * width * ff * 3,
            bytes_accessed=2 * 2 * count * rows * width + 4 * 3 * width * ff,
            transcendentals=0,
        ),
        name="wgrad_group",
    )(*inputs, *(acc if has else ()))


def chip_ring(chips, ladder):
    if ladder:
        return list(range(0, chips, 2)) + list(range(chips - 1, 0, -2))
    return list(range(chips))


def local(ladder, tokens, out_grad, gate_probs, routes, w_gate, w_up, w_down):
    devices = lax.axis_size("expert")
    chips = devices // 2
    resident = chips <= 8
    ring = chip_ring(chips, ladder)
    hop = [(2 * ring[i], 2 * ring[(i + 1) % chips]) for i in range(chips)]
    hop += [(2 * ring[(i + 1) % chips] + 1, 2 * ring[i] + 1) for i in range(chips)]
    swap = [(i, i ^ 1) for i in range(devices)]

    def forward(v):
        return lax.ppermute(v, "expert", hop)

    def other(v):
        return lax.ppermute(v, "expert", swap)

    me = lax.axis_index("expert").reshape(1)
    expert_ids = jnp.arange(devices, dtype=jnp.int32)
    named = routes[:, :, None] == expert_ids[None, None, :]
    probs = jnp.sum(jnp.where(named, gate_probs[:, :, None], 0.0), axis=1)
    x = jnp.concatenate([tokens, encode(probs)], axis=1)
    o = out_grad
    wgu = jnp.concatenate([w_gate[0], w_up[0]], axis=1)
    wd = w_down[0]

    acc, total, own = None, None, None
    held = []
    for s in range(chips):
        if s:
            x, o = forward(x), forward(o)
        xo, oo = other(x), other(o)
        row_a, row_b, grads, hidden = block_pair(me, devices, x, xo, o, oo, wgu, wd)
        partial = row_a.astype(F32) + other(row_b).astype(F32)
        if s == 0:
            own = partial
        else:
            if total is not None:
                partial = forward(total).astype(F32) + partial
            total = partial.astype(BF16)
        held.append((x, xo, o, oo, grads, hidden))
        if len(held) == GROUP or s == chips - 1:
            acc = wgrad_group(
                [v for h in held for v in h[:2]],
                [v for h in held for v in h[2:4]],
                [h[4] for h in held],
                [h[5] for h in held],
                acc,
                s == chips - 1,
                resident,
            )
            held = []
            if not resident:
                x, o, acc = lax.optimization_barrier((x, o, acc))
    total = forward(total).astype(F32) + own if chips > 1 else own
    gate_wgrad, up_wgrad, down_wgrad = acc
    return (
        total.astype(BF16),
        gate_wgrad[None],
        up_wgrad[None],
        down_wgrad[None],
    )


def solution(mesh):
    ladder = mesh.shape["groups"] == 2
    rows = P(("groups", "expert"), None)
    weights = P("expert", None, None)
    wgrads = P(("groups", "expert"), None, None)
    return jax.shard_map(
        functools.partial(local, ladder),
        mesh=mesh,
        in_specs=(rows, rows, rows, rows, weights, weights, weights),
        out_specs=(rows, wgrads, wgrads, wgrads),
        check_vma=False,
    )
```

time: 413 us -> 153 us (0.37)
  the two profiles are of different devices: /device:TPU:13 before, /device:TPU:0 now
where the time goes in v1:
time: 153 us
  waiting for transfers between devices  63.8 us (42%)
  starting transfers between devices  45.4 us (30%)
  Pallas kernels  35.7 us (23%)
  other arithmetic  6.74 us (4%)
    ppermute x21, waiting for transfers between devices, forward(): return lax.ppermute(v, 'expert', hop)  63.7 us
    ppermute x21, starting transfers between devices, forward(): return lax.ppermute(v, 'expert', hop)  41.3 us
    pallas_call x8, Pallas kernels, block_pair(): pl.pallas_call(body, in_specs=[pl.BlockSpec(memory_space=pltpu.SMEM)] + [...  22.6 us
    pallas_call x2, Pallas kernels, wgrad_group(): pl.pallas_call(body, grid=(width // chunk,), in_specs=specs + (acc_specs...  13.1 us
    ppermute x24, starting transfers between devices, other(): return lax.ppermute(v, 'expert', swap)  4.14 us
  transfers between devices with their start and end apart: 45, of which 14 were waited for; matrix products, arithmetic and copies ran while one was open for 3% of the time, Pallas kernels for 23%

profile of v1, /device:TPU:0, one launch (start us, length us, event | category | flops | bytes accessed | tf_op | source)
XLA Modules:
  0.0 152.5 jit_solution(14170436415030867853)
XLA Ops:
  0.6 0.7 select_reduce_fusion
  1.5 1.1 fusion.1.xa.refs_0_
  2.6 3.1 %collective-permute-start = (bf16[128,2176]{1,0:T(8,128)(2,1)S(1)}, bf16[128,2176]{1,0:T(8,128)(2,1)S(1)}, u32[]{:S(2)}, u32[]{:S(2)}) collective-permute-start(bf16[128,2176]{1,0:T(8,128)(2,1)S(1)} %fusion.1.xa.refs_0_), channel_id=1, source_target_pairs={{0,4},{4,8},{8,12},{12,14},{14,10},{10,6},{6,2},{2,0},{5,1},{9,5},... | collective-permute-start | bytes 1671176 | tf_op jit(solution)/shard_map/ppermute | solution.py:157
  5.7 1.6 %collective-permute-start.2 = (bf16[128,2048]{1,0:T(8,128)(2,1)}, bf16[128,2048]{1,0:T(8,128)(2,1)S(1)}, u32[]{:S(2)}, u32[]{:S(2)}) collective-permute-start(bf16[128,2048]{1,0:T(8,128)(2,1)} %refs_8_.1), channel_id=1, source_target_pairs={{0,4},{4,8},{8,12},{12,14},{14,10},{10,6},{6,2},{2,0},{5,1},{9,5},... | collective-permute-start | bytes 1572872 | tf_op jit(solution)/shard_map/ppermute | solution.py:157
  7.2 5.9 %collective-permute-done.xa.refs_2_ = bf16[128,2176]{1,0:T(8,128)(2,1)S(1)} collective-permute-done((bf16[128,2176]{1,0:T(8,128)(2,1)S(1)}, bf16[128,2176]{1,0:T(8,128)(2,1)S(1)}, u32[]{:S(2)}, u32[]{:S(2)}) %collective-permute-start) | collective-permute-done | bytes 557088 | tf_op jit(solution)/shard_map/ppermute | solution.py:157
  13.1 5.6 %collective-permute-done.2.oa.refs_10_ = bf16[128,2048]{1,0:T(8,128)(2,1)S(1)} collective-permute-done((bf16[128,2048]{1,0:T(8,128)(2,1)}, bf16[128,2048]{1,0:T(8,128)(2,1)S(1)}, u32[]{:S(2)}, u32[]{:S(2)}) %collective-permute-start.2) | collective-permute-done | bytes 524320 | tf_op jit(solution)/shard_map/ppermute | solution.py:157
  18.7 2.2 %pad_maximum_fusion.wgu = bf16[2048,768]{1,0:T(8,128)(2,1)S(1)} fusion(bf16[2048,384]{1,0:T(8,128)(2,1)} %bitcast.15, bf16[2048,384]{1,0:T(8,128)(2,1)} %bitcast.16), kind=kLoop, calls=%fused_computation | loop fusion | flops 6291456 | bytes 6291456 | tf_op jit(solution)/shard_map/concatenate | solution.py:168
  21.0 2.1 %collective-permute-start.8 = (bf16[128,2048]{1,0:T(8,128)(2,1)S(1)}, bf16[128,2048]{1,0:T(8,128)(2,1)S(1)}, u32[]{:S(2)}, u32[]{:S(2)}) collective-permute-start(bf16[128,2048]{1,0:T(8,128)(2,1)S(1)} %collective-permute-done.2.oa.refs_10_), channel_id=1, source_target_pairs={{0,4},{4,8},{8,12},{12,14},{14,10},{10,6},{6,2},{2,0},{5,1},{9,5},... | collective-permute-start | bytes 1572872 | tf_op jit(solution)/shard_map/ppermute | solution.py:157
  23.1 1.6 %collective-permute-start.6 = (bf16[128,2176]{1,0:T(8,128)(2,1)S(1)}, bf16[128,2176]{1,0:T(8,128)(2,1)S(1)}, u32[]{:S(2)}, u32[]{:S(2)}) collective-permute-start(bf16[128,2176]{1,0:T(8,128)(2,1)S(1)} %collective-permute-done.xa.refs_2_), channel_id=1, source_target_pairs={{0,4},{4,8},{8,12},{12,14},{14,10},{10,6},{6,2},{2,0},{5,1},{9,5},... | collective-permute-start | bytes 1671176 | tf_op jit(solution)/shard_map/ppermute | solution.py:157
  24.7 2.8 %block_pair.8 = (bf16[128,2048]{1,0:T(8,128)(2,1)S(1)}, bf16[128,2048]{1,0:T(8,128)(2,1)S(1)}, bf16[256,768]{1,0:T(8,128)(2,1)S(1)}, bf16[256,384]{1,0:T(8,128)(2,1)S(1)}) custom-call(s32[1]{0:T(128)} %bitcast.me, bf16[128,2176]{1,0:T(8,128)(2,1)S(1)} %collective-permute-done.xa.refs_2_, bf16[128,2176]{1,0:T(8,128)(2,1)S(1)} %collective-permute-done.1.xb.refs_3_, ...), custom_call_target="tpu_custom_call" | custom-call | flops 2013265920 | bytes 7864320 | tf_op jit(solution)/shard_map/block_pair/pallas_call | solution.py:63
  27.6 8.6 %collective-permute-done.6.xa.refs_4_ = bf16[128,2176]{1,0:T(8,128)(2,1)S(1)} collective-permute-done((bf16[128,2176]{1,0:T(8,128)(2,1)S(1)}, bf16[128,2176]{1,0:T(8,128)(2,1)S(1)}, u32[]{:S(2)}, u32[]{:S(2)}) %collective-permute-start.6) | collective-permute-done | bytes 557088 | tf_op jit(solution)/shard_map/ppermute | solution.py:157
  36.2 0.5 collective-permute-start.9
  36.7 2.1 %collective-permute-start.14 = (bf16[128,2048]{1,0:T(8,128)(2,1)S(1)}, bf16[128,2048]{1,0:T(8,128)(2,1)S(1)}, u32[]{:S(2)}, u32[]{:S(2)}) collective-permute-start(bf16[128,2048]{1,0:T(8,128)(2,1)S(1)} %collective-permute-done.8.oa.refs_12_), channel_id=1, source_target_pairs={{0,4},{4,8},{8,12},{12,14},{14,10},{10,6},{6,2},{2,0},{5,1},{9,5},... | collective-permute-start | bytes 1572872 | tf_op jit(solution)/shard_map/ppermute | solution.py:157
  38.8 1.6 %collective-permute-start.12 = (bf16[128,2176]{1,0:T(8,128)(2,1)S(1)}, bf16[128,2176]{1,0:T(8,128)(2,1)S(1)}, u32[]{:S(2)}, u32[]{:S(2)}) collective-permute-start(bf16[128,2176]{1,0:T(8,128)(2,1)S(1)} %collective-permute-done.6.xa.refs_4_), channel_id=1, source_target_pairs={{0,4},{4,8},{8,12},{12,14},{14,10},{10,6},{6,2},{2,0},{5,1},{9,5},... | collective-permute-start | bytes 1671176 | tf_op jit(solution)/shard_map/ppermute | solution.py:157
  40.4 0.1 add_convert_fusion.7
  40.5 1.6 %collective-permute-start.5 = (bf16[128,2048]{1,0:T(8,128)(2,1)S(1)}, bf16[128,2048]{1,0:T(8,128)(2,1)S(1)}, u32[]{:S(2)}, u32[]{:S(2)}) collective-permute-start(bf16[128,2048]{1,0:T(8,128)(2,1)S(1)} %add_convert_fusion.7), channel_id=1, source_target_pairs={{0,4},{4,8},{8,12},{12,14},{14,10},{10,6},{6,2},{2,0},{5,1},{9,5},... | collective-permute-start | bytes 1572872 | tf_op jit(solution)/shard_map/ppermute | solution.py:157
  42.1 2.8 %block_pair.9 = (bf16[128,2048]{1,0:T(8,128)(2,1)S(1)}, bf16[128,2048]{1,0:T(8,128)(2,1)S(1)}, bf16[256,768]{1,0:T(8,128)(2,1)S(1)}, bf16[256,384]{1,0:T(8,128)(2,1)S(1)}) custom-call(s32[1]{0:T(128)} %bitcast.me, bf16[128,2176]{1,0:T(8,128)(2,1)S(1)} %collective-permute-done.6.xa.refs_4_, bf16[128,2176]{1,0:T(8,128)(2,1)S(1)} %collective-permute-done.7.xb.refs_5_, ...), custom_call_target="tpu_custom_call" | custom-call | flops 2013265920 | bytes 7864320 | tf_op jit(solution)/shard_map/block_pair/pallas_call | solution.py:63
  45.1 6.8 %collective-permute-done.12.xa.refs_6_ = bf16[128,2176]{1,0:T(8,128)(2,1)S(1)} collective-permute-done((bf16[128,2176]{1,0:T(8,128)(2,1)S(1)}, bf16[128,2176]{1,0:T(8,128)(2,1)S(1)}, u32[]{:S(2)}, u32[]{:S(2)}) %collective-permute-start.12) | collective-permute-done | bytes 557088 | tf_op jit(solution)/shard_map/ppermute | solution.py:157
  51.9 0.5 collective-permute-start.15
  52.4 2.1 %collective-permute-start.20 = (bf16[128,2048]{1,0:T(8,128)(2,1)S(1)}, bf16[128,2048]{1,0:T(8,128)(2,1)S(1)}, u32[]{:S(2)}, u32[]{:S(2)}) collective-permute-start(bf16[128,2048]{1,0:T(8,128)(2,1)S(1)} %collective-permute-done.14.oa.refs_14_), channel_id=1, source_target_pairs={{0,4},{4,8},{8,12},{12,14},{14,10},{10,6},{6,2},{2,0},{5,1},{9,5},... | collective-permute-start | bytes 1572872 | tf_op jit(solution)/shard_map/ppermute | solution.py:157
  54.5 3.0 %collective-permute-done.5 = bf16[128,2048]{1,0:T(8,128)(2,1)S(1)} collective-permute-done((bf16[128,2048]{1,0:T(8,128)(2,1)S(1)}, bf16[128,2048]{1,0:T(8,128)(2,1)S(1)}, u32[]{:S(2)}, u32[]{:S(2)}) %collective-permute-start.5) | collective-permute-done | bytes 524320 | tf_op jit(solution)/shard_map/ppermute | solution.py:157
  57.5 2.1 %collective-permute-start.18 = (bf16[128,2176]{1,0:T(8,128)(2,1)S(1)}, bf16[128,2176]{1,0:T(8,128)(2,1)S(1)}, u32[]{:S(2)}, u32[]{:S(2)}) collective-permute-start(bf16[128,2176]{1,0:T(8,128)(2,1)S(1)} %collective-permute-done.12.xa.refs_6_), channel_id=1, source_target_pairs={{0,4},{4,8},{8,12},{12,14},{14,10},{10,6},{6,2},{2,0},{5,1},{9,5},... | collective-permute-start | bytes 1671176 | tf_op jit(solution)/shard_map/ppermute | solution.py:157
  59.6 0.2 add_convert_fusion.6
  59.8 1.6 %collective-permute-start.11 = (bf16[128,2048]{1,0:T(8,128)(2,1)S(1)}, bf16[128,2048]{1,0:T(8,128)(2,1)S(1)}, u32[]{:S(2)}, u32[]{:S(2)}) collective-permute-start(bf16[128,2048]{1,0:T(8,128)(2,1)S(1)} %add_convert_fusion.6), channel_id=1, source_target_pairs={{0,4},{4,8},{8,12},{12,14},{14,10},{10,6},{6,2},{2,0},{5,1},{9,5},... | collective-permute-start | bytes 1572872 | tf_op jit(solution)/shard_map/ppermute | solution.py:157
  61.5 2.8 %block_pair.10 = (bf16[128,2048]{1,0:T(8,128)(2,1)S(1)}, bf16[128,2048]{1,0:T(8,128)(2,1)S(1)}, bf16[256,768]{1,0:T(8,128)(2,1)S(1)}, bf16[256,384]{1,0:T(8,128)(2,1)S(1)}) custom-call(s32[1]{0:T(128)} %bitcast.me, bf16[128,2176]{1,0:T(8,128)(2,1)S(1)} %collective-permute-done.12.xa.refs_6_, bf16[128,2176]{1,0:T(8,128)(2,1)S(1)} %collective-permute-done.13.xb.refs_7_, ...), custom_call_target="tpu_custom_call" | custom-call | flops 2013265920 | bytes 7864320 | tf_op jit(solution)/shard_map/block_pair/pallas_call | solution.py:63
  64.4 4.7 %collective-permute-done.18.xa.refs_0_ = bf16[128,2176]{1,0:T(8,128)(2,1)S(1)} collective-permute-done((bf16[128,2176]{1,0:T(8,128)(2,1)S(1)}, bf16[128,2176]{1,0:T(8,128)(2,1)S(1)}, u32[]{:S(2)}, u32[]{:S(2)}) %collective-permute-start.18) | collective-permute-done | bytes 557088 | tf_op jit(solution)/shard_map/ppermute | solution.py:157
  69.1 0.5 collective-permute-start.21
  69.6 2.1 %collective-permute-start.26 = (bf16[128,2048]{1,0:T(8,128)(2,1)S(1)}, bf16[128,2048]{1,0:T(8,128)(2,1)S(1)}, u32[]{:S(2)}, u32[]{:S(2)}) collective-permute-start(bf16[128,2048]{1,0:T(8,128)(2,1)S(1)} %collective-permute-done.20.oa.refs_8_), channel_id=1, source_target_pairs={{0,4},{4,8},{8,12},{12,14},{14,10},{10,6},{6,2},{2,0},{5,1},{9,5},... | collective-permute-start | bytes 1572872 | tf_op jit(solution)/shard_map/ppermute | solution.py:157
  71.7 3.0 %collective-permute-done.11 = bf16[128,2048]{1,0:T(8,128)(2,1)S(1)} collective-permute-done((bf16[128,2048]{1,0:T(8,128)(2,1)S(1)}, bf16[128,2048]{1,0:T(8,128)(2,1)S(1)}, u32[]{:S(2)}, u32[]{:S(2)}) %collective-permute-start.11) | collective-permute-done | bytes 524320 | tf_op jit(solution)/shard_map/ppermute | solution.py:157
  74.7 2.1 %collective-permute-start.24 = (bf16[128,2176]{1,0:T(8,128)(2,1)S(1)}, bf16[128,2176]{1,0:T(8,128)(2,1)S(1)}, u32[]{:S(2)}, u32[]{:S(2)}) collective-permute-start(bf16[128,2176]{1,0:T(8,128)(2,1)S(1)} %collective-permute-done.18.xa.refs_0_), channel_id=1, source_target_pairs={{0,4},{4,8},{8,12},{12,14},{14,10},{10,6},{6,2},{2,0},{5,1},{9,5},... | collective-permute-start | bytes 1671176 | tf_op jit(solution)/shard_map/ppermute | solution.py:157
  76.8 0.2 add_convert_fusion.5
  77.0 1.6 %collective-permute-start.17 = (bf16[128,2048]{1,0:T(8,128)(2,1)S(1)}, bf16[128,2048]{1,0:T(8,128)(2,1)S(1)}, u32[]{:S(2)}, u32[]{:S(2)}) collective-permute-start(bf16[128,2048]{1,0:T(8,128)(2,1)S(1)} %add_convert_fusion.5), channel_id=1, source_target_pairs={{0,4},{4,8},{8,12},{12,14},{14,10},{10,6},{6,2},{2,0},{5,1},{9,5},... | collective-permute-start | bytes 1572872 | tf_op jit(solution)/shard_map/ppermute | solution.py:157
  78.7 2.8 %block_pair.11 = (bf16[128,2048]{1,0:T(8,128)(2,1)S(1)}, bf16[128,2048]{1,0:T(8,128)(2,1)S(1)}, bf16[256,768]{1,0:T(8,128)(2,1)S(1)}, bf16[256,384]{1,0:T(8,128)(2,1)S(1)}) custom-call(s32[1]{0:T(128)} %bitcast.me, bf16[128,2176]{1,0:T(8,128)(2,1)S(1)} %collective-permute-done.18.xa.refs_0_, bf16[128,2176]{1,0:T(8,128)(2,1)S(1)} %collective-permute-done.19.xb.refs_1_, ...), custom_call_target="tpu_custom_call" | custom-call | flops 2013265920 | bytes 7864320 | tf_op jit(solution)/shard_map/block_pair/pallas_call | solution.py:63
  81.6 4.7 %collective-permute-done.24.xa.refs_2_ = bf16[128,2176]{1,0:T(8,128)(2,1)S(1)} collective-permute-done((bf16[128,2176]{1,0:T(8,128)(2,1)S(1)}, bf16[128,2176]{1,0:T(8,128)(2,1)S(1)}, u32[]{:S(2)}, u32[]{:S(2)}) %collective-permute-start.24) | collective-permute-done | bytes 557088 | tf_op jit(solution)/shard_map/ppermute | solution.py:157
  86.3 0.5 collective-permute-start.27
  86.8 2.1 %collective-permute-start.32 = (bf16[128,2048]{1,0:T(8,128)(2,1)S(1)}, bf16[128,2048]{1,0:T(8,128)(2,1)S(1)}, u32[]{:S(2)}, u32[]{:S(2)}) collective-permute-start(bf16[128,2048]{1,0:T(8,128)(2,1)S(1)} %collective-permute-done.26.oa.refs_10_), channel_id=1, source_target_pairs={{0,4},{4,8},{8,12},{12,14},{14,10},{10,6},{6,2},{2,0},{5,1},{9,5},... | collective-permute-start | bytes 1572872 | tf_op jit(solution)/shard_map/ppermute | solution.py:157
  88.9 3.0 %collective-permute-done.17 = bf16[128,2048]{1,0:T(8,128)(2,1)S(1)} collective-permute-done((bf16[128,2048]{1,0:T(8,128)(2,1)S(1)}, bf16[128,2048]{1,0:T(8,128)(2,1)S(1)}, u32[]{:S(2)}, u32[]{:S(2)}) %collective-permute-start.17) | collective-permute-done | bytes 524320 | tf_op jit(solution)/shard_map/ppermute | solution.py:157
  91.9 2.1 %collective-permute-start.30 = (bf16[128,2176]{1,0:T(8,128)(2,1)S(1)}, bf16[128,2176]{1,0:T(8,128)(2,1)S(1)}, u32[]{:S(2)}, u32[]{:S(2)}) collective-permute-start(bf16[128,2176]{1,0:T(8,128)(2,1)S(1)} %collective-permute-done.24.xa.refs_2_), channel_id=1, source_target_pairs={{0,4},{4,8},{8,12},{12,14},{14,10},{10,6},{6,2},{2,0},{5,1},{9,5},... | collective-permute-start | bytes 1671176 | tf_op jit(solution)/shard_map/ppermute | solution.py:157
  94.0 0.2 add_convert_fusion.4
  94.2 1.6 %collective-permute-start.23 = (bf16[128,2048]{1,0:T(8,128)(2,1)S(1)}, bf16[128,2048]{1,0:T(8,128)(2,1)S(1)}, u32[]{:S(2)}, u32[]{:S(2)}) collective-permute-start(bf16[128,2048]{1,0:T(8,128)(2,1)S(1)} %add_convert_fusion.4), channel_id=1, source_target_pairs={{0,4},{4,8},{8,12},{12,14},{14,10},{10,6},{6,2},{2,0},{5,1},{9,5},... | collective-permute-start | bytes 1572872 | tf_op jit(solution)/shard_map/ppermute | solution.py:157
  95.9 2.8 %block_pair.12 = (bf16[128,2048]{1,0:T(8,128)(2,1)S(1)}, bf16[128,2048]{1,0:T(8,128)(2,1)S(1)}, bf16[256,768]{1,0:T(8,128)(2,1)S(1)}, bf16[256,384]{1,0:T(8,128)(2,1)S(1)}) custom-call(s32[1]{0:T(128)} %bitcast.me, bf16[128,2176]{1,0:T(8,128)(2,1)S(1)} %collective-permute-done.24.xa.refs_2_, bf16[128,2176]{1,0:T(8,128)(2,1)S(1)} %collective-permute-done.25.xb.refs_3_, ...), custom_call_target="tpu_custom_call" | custom-call | flops 2013265920 | bytes 7864320 | tf_op jit(solution)/shard_map/block_pair/pallas_call | solution.py:63
  98.8 4.7 %collective-permute-done.30.xa.refs_4_ = bf16[128,2176]{1,0:T(8,128)(2,1)S(1)} collective-permute-done((bf16[128,2176]{1,0:T(8,128)(2,1)S(1)}, bf16[128,2176]{1,0:T(8,128)(2,1)S(1)}, u32[]{:S(2)}, u32[]{:S(2)}) %collective-permute-start.30) | collective-permute-done | bytes 557088 | tf_op jit(solution)/shard_map/ppermute | solution.py:157
  103.5 0.5 collective-permute-start.33
  104.0 2.1 %collective-permute-start.38 = (bf16[128,2048]{1,0:T(8,128)(2,1)S(1)}, bf16[128,2048]{1,0:T(8,128)(2,1)S(1)}, u32[]{:S(2)}, u32[]{:S(2)}) collective-permute-start(bf16[128,2048]{1,0:T(8,128)(2,1)S(1)} %collective-permute-done.32.oa.refs_12_), channel_id=1, source_target_pairs={{0,4},{4,8},{8,12},{12,14},{14,10},{10,6},{6,2},{2,0},{5,1},{9,5},... | collective-permute-start | bytes 1572872 | tf_op jit(solution)/shard_map/ppermute | solution.py:157
  106.1 3.0 %collective-permute-done.23 = bf16[128,2048]{1,0:T(8,128)(2,1)S(1)} collective-permute-done((bf16[128,2048]{1,0:T(8,128)(2,1)S(1)}, bf16[128,2048]{1,0:T(8,128)(2,1)S(1)}, u32[]{:S(2)}, u32[]{:S(2)}) %collective-permute-start.23) | collective-permute-done | bytes 524320 | tf_op jit(solution)/shard_map/ppermute | solution.py:157
  109.1 2.1 %collective-permute-start.36 = (bf16[128,2176]{1,0:T(8,128)(2,1)S(1)}, bf16[128,2176]{1,0:T(8,128)(2,1)S(1)}, u32[]{:S(2)}, u32[]{:S(2)}) collective-permute-start(bf16[128,2176]{1,0:T(8,128)(2,1)S(1)} %collective-permute-done.30.xa.refs_4_), channel_id=1, source_target_pairs={{0,4},{4,8},{8,12},{12,14},{14,10},{10,6},{6,2},{2,0},{5,1},{9,5},... | collective-permute-start | bytes 1671176 | tf_op jit(solution)/shard_map/ppermute | solution.py:157
  111.2 0.3 add_convert_fusion.3
  111.5 1.6 %collective-permute-start.29 = (bf16[128,2048]{1,0:T(8,128)(2,1)S(1)}, bf16[128,2048]{1,0:T(8,128)(2,1)S(1)}, u32[]{:S(2)}, u32[]{:S(2)}) collective-permute-start(bf16[128,2048]{1,0:T(8,128)(2,1)S(1)} %add_convert_fusion.3), channel_id=1, source_target_pairs={{0,4},{4,8},{8,12},{12,14},{14,10},{10,6},{6,2},{2,0},{5,1},{9,5},... | collective-permute-start | bytes 1572872 | tf_op jit(solution)/shard_map/ppermute | solution.py:157
  113.1 2.8 %block_pair.13 = (bf16[128,2048]{1,0:T(8,128)(2,1)S(1)}, bf16[128,2048]{1,0:T(8,128)(2,1)S(1)}, bf16[256,768]{1,0:T(8,128)(2,1)S(1)}, bf16[256,384]{1,0:T(8,128)(2,1)S(1)}) custom-call(s32[1]{0:T(128)} %bitcast.me, bf16[128,2176]{1,0:T(8,128)(2,1)S(1)} %collective-permute-done.30.xa.refs_4_, bf16[128,2176]{1,0:T(8,128)(2,1)S(1)} %collective-permute-done.31.xb.refs_5_, ...), custom_call_target="tpu_custom_call" | custom-call | flops 2013265920 | bytes 7864320 | tf_op jit(solution)/shard_map/block_pair/pallas_call | solution.py:63
  116.0 4.7 %collective-permute-done.36.xa.refs_6_ = bf16[128,2176]{1,0:T(8,128)(2,1)S(1)} collective-permute-done((bf16[128,2176]{1,0:T(8,128)(2,1)S(1)}, bf16[128,2176]{1,0:T(8,128)(2,1)S(1)}, u32[]{:S(2)}, u32[]{:S(2)}) %collective-permute-start.36) | collective-permute-done | bytes 557088 | tf_op jit(solution)/shard_map/ppermute | solution.py:157
  120.7 0.5 collective-permute-start.39
  121.2 5.1 %collective-permute-done.29 = bf16[128,2048]{1,0:T(8,128)(2,1)S(1)} collective-permute-done((bf16[128,2048]{1,0:T(8,128)(2,1)S(1)}, bf16[128,2048]{1,0:T(8,128)(2,1)S(1)}, u32[]{:S(2)}, u32[]{:S(2)}) %collective-permute-start.29) | collective-permute-done | bytes 524320 | tf_op jit(solution)/shard_map/ppermute | solution.py:157
  126.3 0.2 add_convert_fusion.2
  126.6 2.1 %collective-permute-start.35 = (bf16[128,2048]{1,0:T(8,128)(2,1)S(1)}, bf16[128,2048]{1,0:T(8,128)(2,1)S(1)}, u32[]{:S(2)}, u32[]{:S(2)}) collective-permute-start(bf16[128,2048]{1,0:T(8,128)(2,1)S(1)} %add_convert_fusion.2), channel_id=1, source_target_pairs={{0,4},{4,8},{8,12},{12,14},{14,10},{10,6},{6,2},{2,0},{5,1},{9,5},... | collective-permute-start | bytes 1572872 | tf_op jit(solution)/shard_map/ppermute | solution.py:157
  128.7 2.8 %block_pair.14 = (bf16[128,2048]{1,0:T(8,128)(2,1)S(1)}, bf16[128,2048]{1,0:T(8,128)(2,1)S(1)}, bf16[256,768]{1,0:T(8,128)(2,1)S(1)}, bf16[256,384]{1,0:T(8,128)(2,1)S(1)}) custom-call(s32[1]{0:T(128)} %bitcast.me, bf16[128,2176]{1,0:T(8,128)(2,1)S(1)} %collective-permute-done.36.xa.refs_6_, bf16[128,2176]{1,0:T(8,128)(2,1)S(1)} %collective-permute-done.37.xb.refs_7_, ...), custom_call_target="tpu_custom_call" | custom-call | flops 2013265920 | bytes 7864320 | tf_op jit(solution)/shard_map/block_pair/pallas_call | solution.py:63
  131.5 0.2 collective-permute-start.40
  131.8 2.8 %block_pair.15 = (bf16[128,2048]{1,0:T(8,128)(2,1)S(1)}, bf16[128,2048]{1,0:T(8,128)(2,1)S(1)}, bf16[256,768]{1,0:T(8,128)(2,1)S(1)}, bf16[256,384]{1,0:T(8,128)(2,1)S(1)}) custom-call(s32[1]{0:T(128)} %bitcast.me, bf16[128,2176]{1,0:T(8,128)(2,1)S(1)} %fusion.1.xa.refs_0_, bf16[128,2176]{1,0:T(8,128)(2,1)S(1)} %collective-permute-done.42.xb.refs_1_, ...), custom_call_target="tpu_custom_call" | custom-call | flops 2013265920 | bytes 7864320 | tf_op jit(solution)/shard_map/block_pair/pallas_call | solution.py:63
  134.6 0.4 collective-permute-start.44
  135.0 0.8 collective-permute-done.35
  135.8 0.2 add_convert_fusion.1
  136.1 2.3 %collective-permute-start.41 = (bf16[128,2048]{1,0:T(8,128)(2,1)S(1)}, bf16[128,2048]{1,0:T(8,128)(2,1)S(1)}, u32[]{:S(2)}, u32[]{:S(2)}) collective-permute-start(bf16[128,2048]{1,0:T(8,128)(2,1)S(1)} %add_convert_fusion.1), channel_id=1, source_target_pairs={{0,4},{4,8},{8,12},{12,14},{14,10},{10,6},{6,2},{2,0},{5,1},{9,5},... | collective-permute-start | bytes 1572872 | tf_op jit(solution)/shard_map/ppermute | solution.py:157
  138.4 6.1 %wgrad_group.2 = (f32[2048,384]{1,0:T(8,128)S(1)}, f32[2048,384]{1,0:T(8,128)S(1)}, f32[384,2048]{1,0:T(8,128)S(1)}) custom-call(bf16[128,2176]{1,0:T(8,128)(2,1)S(1)} %fusion.1.xa.refs_0_, bf16[128,2176]{1,0:T(8,128)(2,1)S(1)} %collective-permute-done.42.xb.refs_1_, bf16[128,2176]{1,0:T(8,128)(2,1)S(1)} %collective-permute-done.xa.refs_2_, ...), custom_call_target="tpu_custom_call" | custom-call | flops 4831838208 | bytes 17825792 | tf_op jit(solution)/shard_map/wgrad_group/pallas_call | solution.py:120
  144.5 7.0 %wgrad_group.3 = (bf16[2048,384]{1,0:T(8,128)(2,1)}, bf16[2048,384]{1,0:T(8,128)(2,1)}, bf16[384,2048]{1,0:T(8,128)(2,1)}) custom-call(bf16[128,2176]{1,0:T(8,128)(2,1)S(1)} %collective-permute-done.18.xa.refs_0_, bf16[128,2176]{1,0:T(8,128)(2,1)S(1)} %collective-permute-done.19.xb.refs_1_, bf16[128,2176]{1,0:T(8,128)(2,1)S(1)} %collective-permute-done.24.xa.refs_2_, ...), custom_call_target="tpu_custom_call" | custom-call | flops 4831838208 | bytes 17825792 | tf_op jit(solution)/shard_map/wgrad_group/pallas_call | solution.py:120
  151.5 1.0 add_convert_fusion
  (54 shorter events, 0.7 us)
Async XLA Ops:
  2.6 10.5 %collective-permute-start = (bf16[128,2176]{1,0:T(8,128)(2,1)S(1)}, bf16[128,2176]{1,0:T(8,128)(2,1)S(1)}, u32[]{:S(2)}, u32[]{:S(2)}) collective-permute-start(bf16[128,2176]{1,0:T(8,128)(2,1)S(1)} %fusion.1.xa.refs_0_), channel_id=1, source_target_pairs={{0,4},{4,8},{8,12},{12,14},{14,10},{10,6},{6,2},{2,0},{5,1},{9,5},... | collective-permute-start | bytes 1671176 | tf_op jit(solution)/shard_map/ppermute | solution.py:157
  5.7 13.1 %collective-permute-start.2 = (bf16[128,2048]{1,0:T(8,128)(2,1)}, bf16[128,2048]{1,0:T(8,128)(2,1)S(1)}, u32[]{:S(2)}, u32[]{:S(2)}) collective-permute-start(bf16[128,2048]{1,0:T(8,128)(2,1)} %refs_8_.1), channel_id=1, source_target_pairs={{0,4},{4,8},{8,12},{12,14},{14,10},{10,6},{6,2},{2,0},{5,1},{9,5},... | collective-permute-start | bytes 1572872 | tf_op jit(solution)/shard_map/ppermute | solution.py:157
  13.1 11.6 %collective-permute-start.1 = (bf16[128,2176]{1,0:T(8,128)(2,1)S(1)}, bf16[128,2176]{1,0:T(8,128)(2,1)S(1)}, u32[]{:S(2)}, u32[]{:S(2)}) collective-permute-start(bf16[128,2176]{1,0:T(8,128)(2,1)S(1)} %collective-permute-done.xa.refs_2_), channel_id=1, source_target_pairs={{0,1},{1,0},{2,3},{3,2},{4,5},{5,4},{6,7},{7,6},{8,9},{9,8},{10,11... | collective-permute-start | bytes 1671176 | tf_op jit(solution)/shard_map/ppermute | solution.py:160
  18.7 6.0 %collective-permute-start.3 = (bf16[128,2048]{1,0:T(8,128)(2,1)S(1)}, bf16[128,2048]{1,0:T(8,128)(2,1)S(1)}, u32[]{:S(2)}, u32[]{:S(2)}) collective-permute-start(bf16[128,2048]{1,0:T(8,128)(2,1)S(1)} %collective-permute-done.2.oa.refs_10_), channel_id=1, source_target_pairs={{0,1},{1,0},{2,3},{3,2},{4,5},{5,4},{6,7},{7,6},{8,9},{9,8},{10,11... | collective-permute-start | bytes 1572872 | tf_op jit(solution)/shard_map/ppermute | solution.py:160
  18.7 6.0 %copy-start = (bf16[1,384,2048]{2,1,0:T(8,128)(2,1)S(1)}, bf16[1,384,2048]{2,1,0:T(8,128)(2,1)}, u32[]{:S(2)}) copy-start(bf16[1,384,2048]{2,1,0:T(8,128)(2,1)} %param.13) | copy-start | bytes 4718596
  21.0 15.2 %collective-permute-start.8 = (bf16[128,2048]{1,0:T(8,128)(2,1)S(1)}, bf16[128,2048]{1,0:T(8,128)(2,1)S(1)}, u32[]{:S(2)}, u32[]{:S(2)}) collective-permute-start(bf16[128,2048]{1,0:T(8,128)(2,1)S(1)} %collective-permute-done.2.oa.refs_10_), channel_id=1, source_target_pairs={{0,4},{4,8},{8,12},{12,14},{14,10},{10,6},{6,2},{2,0},{5,1},{9,5},... | collective-permute-start | bytes 1572872 | tf_op jit(solution)/shard_map/ppermute | solution.py:157
  23.1 13.1 %collective-permute-start.6 = (bf16[128,2176]{1,0:T(8,128)(2,1)S(1)}, bf16[128,2176]{1,0:T(8,128)(2,1)S(1)}, u32[]{:S(2)}, u32[]{:S(2)}) collective-permute-start(bf16[128,2176]{1,0:T(8,128)(2,1)S(1)} %collective-permute-done.xa.refs_2_), channel_id=1, source_target_pairs={{0,4},{4,8},{8,12},{12,14},{14,10},{10,6},{6,2},{2,0},{5,1},{9,5},... | collective-permute-start | bytes 1671176 | tf_op jit(solution)/shard_map/ppermute | solution.py:157
  27.5 12.8 %collective-permute-start.4 = (bf16[128,2048]{1,0:T(8,128)(2,1)S(1)}, bf16[128,2048]{1,0:T(8,128)(2,1)S(1)}, u32[]{:S(2)}, u32[]{:S(2)}) collective-permute-start(bf16[128,2048]{1,0:T(8,128)(2,1)S(1)} %get-tuple-element.43), channel_id=1, source_target_pairs={{0,1},{1,0},{2,3},{3,2},{4,5},{5,4},{6,7},{7,6},{8,9},{9,8},{10,11... | collective-permute-start | bytes 1572872 | tf_op jit(solution)/shard_map/ppermute | solution.py:160
  36.2 5.9 %collective-permute-start.7 = (bf16[128,2176]{1,0:T(8,128)(2,1)S(1)}, bf16[128,2176]{1,0:T(8,128)(2,1)S(1)}, u32[]{:S(2)}, u32[]{:S(2)}) collective-permute-start(bf16[128,2176]{1,0:T(8,128)(2,1)S(1)} %collective-permute-done.6.xa.refs_4_), channel_id=1, source_target_pairs={{0,1},{1,0},{2,3},{3,2},{4,5},{5,4},{6,7},{7,6},{8,9},{9,8},{10,11... | collective-permute-start | bytes 1671176 | tf_op jit(solution)/shard_map/ppermute | solution.py:160
  36.2 5.9 %collective-permute-start.9 = (bf16[128,2048]{1,0:T(8,128)(2,1)S(1)}, bf16[128,2048]{1,0:T(8,128)(2,1)S(1)}, u32[]{:S(2)}, u32[]{:S(2)}) collective-permute-start(bf16[128,2048]{1,0:T(8,128)(2,1)S(1)} %collective-permute-done.8.oa.refs_12_), channel_id=1, source_target_pairs={{0,1},{1,0},{2,3},{3,2},{4,5},{5,4},{6,7},{7,6},{8,9},{9,8},{10,11... | collective-permute-start | bytes 1572872 | tf_op jit(solution)/shard_map/ppermute | solution.py:160
  36.7 15.2 %collective-permute-start.14 = (bf16[128,2048]{1,0:T(8,128)(2,1)S(1)}, bf16[128,2048]{1,0:T(8,128)(2,1)S(1)}, u32[]{:S(2)}, u32[]{:S(2)}) collective-permute-start(bf16[128,2048]{1,0:T(8,128)(2,1)S(1)} %collective-permute-done.8.oa.refs_12_), channel_id=1, source_target_pairs={{0,4},{4,8},{8,12},{12,14},{14,10},{10,6},{6,2},{2,0},{5,1},{9,5},... | collective-permute-start | bytes 1572872 | tf_op jit(solution)/shard_map/ppermute | solution.py:157
  38.8 13.1 %collective-permute-start.12 = (bf16[128,2176]{1,0:T(8,128)(2,1)S(1)}, bf16[128,2176]{1,0:T(8,128)(2,1)S(1)}, u32[]{:S(2)}, u32[]{:S(2)}) collective-permute-start(bf16[128,2176]{1,0:T(8,128)(2,1)S(1)} %collective-permute-done.6.xa.refs_4_), channel_id=1, source_target_pairs={{0,4},{4,8},{8,12},{12,14},{14,10},{10,6},{6,2},{2,0},{5,1},{9,5},... | collective-permute-start | bytes 1671176 | tf_op jit(solution)/shard_map/ppermute | solution.py:157
  40.5 17.0 %collective-permute-start.5 = (bf16[128,2048]{1,0:T(8,128)(2,1)S(1)}, bf16[128,2048]{1,0:T(8,128)(2,1)S(1)}, u32[]{:S(2)}, u32[]{:S(2)}) collective-permute-start(bf16[128,2048]{1,0:T(8,128)(2,1)S(1)} %add_convert_fusion.7), channel_id=1, source_target_pairs={{0,4},{4,8},{8,12},{12,14},{14,10},{10,6},{6,2},{2,0},{5,1},{9,5},... | collective-permute-start | bytes 1572872 | tf_op jit(solution)/shard_map/ppermute | solution.py:157
  45.0 14.6 %collective-permute-start.10 = (bf16[128,2048]{1,0:T(8,128)(2,1)S(1)}, bf16[128,2048]{1,0:T(8,128)(2,1)S(1)}, u32[]{:S(2)}, u32[]{:S(2)}) collective-permute-start(bf16[128,2048]{1,0:T(8,128)(2,1)S(1)} %get-tuple-element.45), channel_id=1, source_target_pairs={{0,1},{1,0},{2,3},{3,2},{4,5},{5,4},{6,7},{7,6},{8,9},{9,8},{10,11... | collective-permute-start | bytes 1572872 | tf_op jit(solution)/shard_map/ppermute | solution.py:160
  51.9 9.6 %collective-permute-start.13 = (bf16[128,2176]{1,0:T(8,128)(2,1)S(1)}, bf16[128,2176]{1,0:T(8,128)(2,1)S(1)}, u32[]{:S(2)}, u32[]{:S(2)}) collective-permute-start(bf16[128,2176]{1,0:T(8,128)(2,1)S(1)} %collective-permute-done.12.xa.refs_6_), channel_id=1, source_target_pairs={{0,1},{1,0},{2,3},{3,2},{4,5},{5,4},{6,7},{7,6},{8,9},{9,8},{10,11... | collective-permute-start | bytes 1671176 | tf_op jit(solution)/shard_map/ppermute | solution.py:160
  51.9 9.6 %collective-permute-start.15 = (bf16[128,2048]{1,0:T(8,128)(2,1)S(1)}, bf16[128,2048]{1,0:T(8,128)(2,1)S(1)}, u32[]{:S(2)}, u32[]{:S(2)}) collective-permute-start(bf16[128,2048]{1,0:T(8,128)(2,1)S(1)} %collective-permute-done.14.oa.refs_14_), channel_id=1, source_target_pairs={{0,1},{1,0},{2,3},{3,2},{4,5},{5,4},{6,7},{7,6},{8,9},{9,8},{10,11... | collective-permute-start | bytes 1572872 | tf_op jit(solution)/shard_map/ppermute | solution.py:160
  52.4 16.7 %collective-permute-start.20 = (bf16[128,2048]{1,0:T(8,128)(2,1)S(1)}, bf16[128,2048]{1,0:T(8,128)(2,1)S(1)}, u32[]{:S(2)}, u32[]{:S(2)}) collective-permute-start(bf16[128,2048]{1,0:T(8,128)(2,1)S(1)} %collective-permute-done.14.oa.refs_14_), channel_id=1, source_target_pairs={{0,4},{4,8},{8,12},{12,14},{14,10},{10,6},{6,2},{2,0},{5,1},{9,5},... | collective-permute-start | bytes 1572872 | tf_op jit(solution)/shard_map/ppermute | solution.py:157
  57.5 11.6 %collective-permute-start.18 = (bf16[128,2176]{1,0:T(8,128)(2,1)S(1)}, bf16[128,2176]{1,0:T(8,128)(2,1)S(1)}, u32[]{:S(2)}, u32[]{:S(2)}) collective-permute-start(bf16[128,2176]{1,0:T(8,128)(2,1)S(1)} %collective-permute-done.12.xa.refs_6_), channel_id=1, source_target_pairs={{0,4},{4,8},{8,12},{12,14},{14,10},{10,6},{6,2},{2,0},{5,1},{9,5},... | collective-permute-start | bytes 1671176 | tf_op jit(solution)/shard_map/ppermute | solution.py:157
  59.8 14.9 %collective-permute-start.11 = (bf16[128,2048]{1,0:T(8,128)(2,1)S(1)}, bf16[128,2048]{1,0:T(8,128)(2,1)S(1)}, u32[]{:S(2)}, u32[]{:S(2)}) collective-permute-start(bf16[128,2048]{1,0:T(8,128)(2,1)S(1)} %add_convert_fusion.6), channel_id=1, source_target_pairs={{0,4},{4,8},{8,12},{12,14},{14,10},{10,6},{6,2},{2,0},{5,1},{9,5},... | collective-permute-start | bytes 1572872 | tf_op jit(solution)/shard_map/ppermute | solution.py:157
  64.3 12.5 %collective-permute-start.16 = (bf16[128,2048]{1,0:T(8,128)(2,1)S(1)}, bf16[128,2048]{1,0:T(8,128)(2,1)S(1)}, u32[]{:S(2)}, u32[]{:S(2)}) collective-permute-start(bf16[128,2048]{1,0:T(8,128)(2,1)S(1)} %get-tuple-element.47), channel_id=1, source_target_pairs={{0,1},{1,0},{2,3},{3,2},{4,5},{5,4},{6,7},{7,6},{8,9},{9,8},{10,11... | collective-permute-start | bytes 1572872 | tf_op jit(solution)/shard_map/ppermute | solution.py:160
  69.1 9.6 %collective-permute-start.19 = (bf16[128,2176]{1,0:T(8,128)(2,1)S(1)}, bf16[128,2176]{1,0:T(8,128)(2,1)S(1)}, u32[]{:S(2)}, u32[]{:S(2)}) collective-permute-start(bf16[128,2176]{1,0:T(8,128)(2,1)S(1)} %collective-permute-done.18.xa.refs_0_), channel_id=1, source_target_pairs={{0,1},{1,0},{2,3},{3,2},{4,5},{5,4},{6,7},{7,6},{8,9},{9,8},{10,11... | collective-permute-start | bytes 1671176 | tf_op jit(solution)/shard_map/ppermute | solution.py:160
  69.1 9.6 %collective-permute-start.21 = (bf16[128,2048]{1,0:T(8,128)(2,1)S(1)}, bf16[128,2048]{1,0:T(8,128)(2,1)S(1)}, u32[]{:S(2)}, u32[]{:S(2)}) collective-permute-start(bf16[128,2048]{1,0:T(8,128)(2,1)S(1)} %collective-permute-done.20.oa.refs_8_), channel_id=1, source_target_pairs={{0,1},{1,0},{2,3},{3,2},{4,5},{5,4},{6,7},{7,6},{8,9},{9,8},{10,11... | collective-permute-start | bytes 1572872 | tf_op jit(solution)/shard_map/ppermute | solution.py:160
  69.6 16.7 %collective-permute-start.26 = (bf16[128,2048]{1,0:T(8,128)(2,1)S(1)}, bf16[128,2048]{1,0:T(8,128)(2,1)S(1)}, u32[]{:S(2)}, u32[]{:S(2)}) collective-permute-start(bf16[128,2048]{1,0:T(8,128)(2,1)S(1)} %collective-permute-done.20.oa.refs_8_), channel_id=1, source_target_pairs={{0,4},{4,8},{8,12},{12,14},{14,10},{10,6},{6,2},{2,0},{5,1},{9,5},... | collective-permute-start | bytes 1572872 | tf_op jit(solution)/shard_map/ppermute | solution.py:157
  74.7 11.6 %collective-permute-start.24 = (bf16[128,2176]{1,0:T(8,128)(2,1)S(1)}, bf16[128,2176]{1,0:T(8,128)(2,1)S(1)}, u32[]{:S(2)}, u32[]{:S(2)}) collective-permute-start(bf16[128,2176]{1,0:T(8,128)(2,1)S(1)} %collective-permute-done.18.xa.refs_0_), channel_id=1, source_target_pairs={{0,4},{4,8},{8,12},{12,14},{14,10},{10,6},{6,2},{2,0},{5,1},{9,5},... | collective-permute-start | bytes 1671176 | tf_op jit(solution)/shard_map/ppermute | solution.py:157
  77.0 14.9 %collective-permute-start.17 = (bf16[128,2048]{1,0:T(8,128)(2,1)S(1)}, bf16[128,2048]{1,0:T(8,128)(2,1)S(1)}, u32[]{:S(2)}, u32[]{:S(2)}) collective-permute-start(bf16[128,2048]{1,0:T(8,128)(2,1)S(1)} %add_convert_fusion.5), channel_id=1, source_target_pairs={{0,4},{4,8},{8,12},{12,14},{14,10},{10,6},{6,2},{2,0},{5,1},{9,5},... | collective-permute-start | bytes 1572872 | tf_op jit(solution)/shard_map/ppermute | solution.py:157
  81.5 12.5 %collective-permute-start.22 = (bf16[128,2048]{1,0:T(8,128)(2,1)S(1)}, bf16[128,2048]{1,0:T(8,128)(2,1)S(1)}, u32[]{:S(2)}, u32[]{:S(2)}) collective-permute-start(bf16[128,2048]{1,0:T(8,128)(2,1)S(1)} %get-tuple-element.49), channel_id=1, source_target_pairs={{0,1},{1,0},{2,3},{3,2},{4,5},{5,4},{6,7},{7,6},{8,9},{9,8},{10,11... | collective-permute-start | bytes 1572872 | tf_op jit(solution)/shard_map/ppermute | solution.py:160
  86.3 9.6 %collective-permute-start.25 = (bf16[128,2176]{1,0:T(8,128)(2,1)S(1)}, bf16[128,2176]{1,0:T(8,128)(2,1)S(1)}, u32[]{:S(2)}, u32[]{:S(2)}) collective-permute-start(bf16[128,2176]{1,0:T(8,128)(2,1)S(1)} %collective-permute-done.24.xa.refs_2_), channel_id=1, source_target_pairs={{0,1},{1,0},{2,3},{3,2},{4,5},{5,4},{6,7},{7,6},{8,9},{9,8},{10,11... | collective-permute-start | bytes 1671176 | tf_op jit(solution)/shard_map/ppermute | solution.py:160
  86.3 9.6 %collective-permute-start.27 = (bf16[128,2048]{1,0:T(8,128)(2,1)S(1)}, bf16[128,2048]{1,0:T(8,128)(2,1)S(1)}, u32[]{:S(2)}, u32[]{:S(2)}) collective-permute-start(bf16[128,2048]{1,0:T(8,128)(2,1)S(1)} %collective-permute-done.26.oa.refs_10_), channel_id=1, source_target_pairs={{0,1},{1,0},{2,3},{3,2},{4,5},{5,4},{6,7},{7,6},{8,9},{9,8},{10,11... | collective-permute-start | bytes 1572872 | tf_op jit(solution)/shard_map/ppermute | solution.py:160
  86.8 16.7 %collective-permute-start.32 = (bf16[128,2048]{1,0:T(8,128)(2,1)S(1)}, bf16[128,2048]{1,0:T(8,128)(2,1)S(1)}, u32[]{:S(2)}, u32[]{:S(2)}) collective-permute-start(bf16[128,2048]{1,0:T(8,128)(2,1)S(1)} %collective-permute-done.26.oa.refs_10_), channel_id=1, source_target_pairs={{0,4},{4,8},{8,12},{12,14},{14,10},{10,6},{6,2},{2,0},{5,1},{9,5},... | collective-permute-start | bytes 1572872 | tf_op jit(solution)/shard_map/ppermute | solution.py:157
  91.9 11.6 %collective-permute-start.30 = (bf16[128,2176]{1,0:T(8,128)(2,1)S(1)}, bf16[128,2176]{1,0:T(8,128)(2,1)S(1)}, u32[]{:S(2)}, u32[]{:S(2)}) collective-permute-start(bf16[128,2176]{1,0:T(8,128)(2,1)S(1)} %collective-permute-done.24.xa.refs_2_), channel_id=1, source_target_pairs={{0,4},{4,8},{8,12},{12,14},{14,10},{10,6},{6,2},{2,0},{5,1},{9,5},... | collective-permute-start | bytes 1671176 | tf_op jit(solution)/shard_map/ppermute | solution.py:157
  94.2 14.9 %collective-permute-start.23 = (bf16[128,2048]{1,0:T(8,128)(2,1)S(1)}, bf16[128,2048]{1,0:T(8,128)(2,1)S(1)}, u32[]{:S(2)}, u32[]{:S(2)}) collective-permute-start(bf16[128,2048]{1,0:T(8,128)(2,1)S(1)} %add_convert_fusion.4), channel_id=1, source_target_pairs={{0,4},{4,8},{8,12},{12,14},{14,10},{10,6},{6,2},{2,0},{5,1},{9,5},... | collective-permute-start | bytes 1572872 | tf_op jit(solution)/shard_map/ppermute | solution.py:157
  98.7 12.5 %collective-permute-start.28 = (bf16[128,2048]{1,0:T(8,128)(2,1)S(1)}, bf16[128,2048]{1,0:T(8,128)(2,1)S(1)}, u32[]{:S(2)}, u32[]{:S(2)}) collective-permute-start(bf16[128,2048]{1,0:T(8,128)(2,1)S(1)} %get-tuple-element.51), channel_id=1, source_target_pairs={{0,1},{1,0},{2,3},{3,2},{4,5},{5,4},{6,7},{7,6},{8,9},{9,8},{10,11... | collective-permute-start | bytes 1572872 | tf_op jit(solution)/shard_map/ppermute | solution.py:160
  103.5 9.6 %collective-permute-start.31 = (bf16[128,2176]{1,0:T(8,128)(2,1)S(1)}, bf16[128,2176]{1,0:T(8,128)(2,1)S(1)}, u32[]{:S(2)}, u32[]{:S(2)}) collective-permute-start(bf16[128,2176]{1,0:T(8,128)(2,1)S(1)} %collective-permute-done.30.xa.refs_4_), channel_id=1, source_target_pairs={{0,1},{1,0},{2,3},{3,2},{4,5},{5,4},{6,7},{7,6},{8,9},{9,8},{10,11... | collective-permute-start | bytes 1671176 | tf_op jit(solution)/shard_map/ppermute | solution.py:160
  103.5 9.6 %collective-permute-start.33 = (bf16[128,2048]{1,0:T(8,128)(2,1)S(1)}, bf16[128,2048]{1,0:T(8,128)(2,1)S(1)}, u32[]{:S(2)}, u32[]{:S(2)}) collective-permute-start(bf16[128,2048]{1,0:T(8,128)(2,1)S(1)} %collective-permute-done.32.oa.refs_12_), channel_id=1, source_target_pairs={{0,1},{1,0},{2,3},{3,2},{4,5},{5,4},{6,7},{7,6},{8,9},{9,8},{10,11... | collective-permute-start | bytes 1572872 | tf_op jit(solution)/shard_map/ppermute | solution.py:160
  104.0 16.7 %collective-permute-start.38 = (bf16[128,2048]{1,0:T(8,128)(2,1)S(1)}, bf16[128,2048]{1,0:T(8,128)(2,1)S(1)}, u32[]{:S(2)}, u32[]{:S(2)}) collective-permute-start(bf16[128,2048]{1,0:T(8,128)(2,1)S(1)} %collective-permute-done.32.oa.refs_12_), channel_id=1, source_target_pairs={{0,4},{4,8},{8,12},{12,14},{14,10},{10,6},{6,2},{2,0},{5,1},{9,5},... | collective-permute-start | bytes 1572872 | tf_op jit(solution)/shard_map/ppermute | solution.py:157
  109.1 11.6 %collective-permute-start.36 = (bf16[128,2176]{1,0:T(8,128)(2,1)S(1)}, bf16[128,2176]{1,0:T(8,128)(2,1)S(1)}, u32[]{:S(2)}, u32[]{:S(2)}) collective-permute-start(bf16[128,2176]{1,0:T(8,128)(2,1)S(1)} %collective-permute-done.30.xa.refs_4_), channel_id=1, source_target_pairs={{0,4},{4,8},{8,12},{12,14},{14,10},{10,6},{6,2},{2,0},{5,1},{9,5},... | collective-permute-start | bytes 1671176 | tf_op jit(solution)/shard_map/ppermute | solution.py:157
  111.5 14.8 %copy-start.1 = (bf16[128,2048]{1,0:T(8,128)(2,1)S(1)}, bf16[128,2048]{1,0:T(8,128)(2,1)}, u32[]{:S(2)}) copy-start(bf16[128,2048]{1,0:T(8,128)(2,1)} %refs_8_.1) | copy-start | bytes 1572868
  111.5 14.8 %collective-permute-start.29 = (bf16[128,2048]{1,0:T(8,128)(2,1)S(1)}, bf16[128,2048]{1,0:T(8,128)(2,1)S(1)}, u32[]{:S(2)}, u32[]{:S(2)}) collective-permute-start(bf16[128,2048]{1,0:T(8,128)(2,1)S(1)} %add_convert_fusion.3), channel_id=1, source_target_pairs={{0,4},{4,8},{8,12},{12,14},{14,10},{10,6},{6,2},{2,0},{5,1},{9,5},... | collective-permute-start | bytes 1572872 | tf_op jit(solution)/shard_map/ppermute | solution.py:157
  115.9 10.4 %collective-permute-start.34 = (bf16[128,2048]{1,0:T(8,128)(2,1)S(1)}, bf16[128,2048]{1,0:T(8,128)(2,1)S(1)}, u32[]{:S(2)}, u32[]{:S(2)}) collective-permute-start(bf16[128,2048]{1,0:T(8,128)(2,1)S(1)} %get-tuple-element.53), channel_id=1, source_target_pairs={{0,1},{1,0},{2,3},{3,2},{4,5},{5,4},{6,7},{7,6},{8,9},{9,8},{10,11... | collective-permute-start | bytes 1572872 | tf_op jit(solution)/shard_map/ppermute | solution.py:160
  120.7 8.0 %collective-permute-start.37 = (bf16[128,2176]{1,0:T(8,128)(2,1)S(1)}, bf16[128,2176]{1,0:T(8,128)(2,1)S(1)}, u32[]{:S(2)}, u32[]{:S(2)}) collective-permute-start(bf16[128,2176]{1,0:T(8,128)(2,1)S(1)} %collective-permute-done.36.xa.refs_6_), channel_id=1, source_target_pairs={{0,1},{1,0},{2,3},{3,2},{4,5},{5,4},{6,7},{7,6},{8,9},{9,8},{10,11... | collective-permute-start | bytes 1671176 | tf_op jit(solution)/shard_map/ppermute | solution.py:160
  120.7 8.0 %collective-permute-start.39 = (bf16[128,2048]{1,0:T(8,128)(2,1)S(1)}, bf16[128,2048]{1,0:T(8,128)(2,1)S(1)}, u32[]{:S(2)}, u32[]{:S(2)}) collective-permute-start(bf16[128,2048]{1,0:T(8,128)(2,1)S(1)} %collective-permute-done.38.oa.refs_14_), channel_id=1, source_target_pairs={{0,1},{1,0},{2,3},{3,2},{4,5},{5,4},{6,7},{7,6},{8,9},{9,8},{10,11... | collective-permute-start | bytes 1572872 | tf_op jit(solution)/shard_map/ppermute | solution.py:160
  121.2 10.6 %collective-permute-start.42 = (bf16[128,2176]{1,0:T(8,128)(2,1)S(1)}, bf16[128,2176]{1,0:T(8,128)(2,1)S(1)}, u32[]{:S(2)}, u32[]{:S(2)}) collective-permute-start(bf16[128,2176]{1,0:T(8,128)(2,1)S(1)} %fusion.1.xa.refs_0_), channel_id=1, source_target_pairs={{0,1},{1,0},{2,3},{3,2},{4,5},{5,4},{6,7},{7,6},{8,9},{9,8},{10,11... | collective-permute-start | bytes 1671176 | tf_op jit(solution)/shard_map/ppermute | solution.py:160
  126.3 5.5 %collective-permute-start.43 = (bf16[128,2048]{1,0:T(8,128)(2,1)S(1)}, bf16[128,2048]{1,0:T(8,128)(2,1)S(1)}, u32[]{:S(2)}, u32[]{:S(2)}) collective-permute-start(bf16[128,2048]{1,0:T(8,128)(2,1)S(1)} %copy-done.1), channel_id=1, source_target_pairs={{0,1},{1,0},{2,3},{3,2},{4,5},{5,4},{6,7},{7,6},{8,9},{9,8},{10,11... | collective-permute-start | bytes 1572872 | tf_op jit(solution)/shard_map/ppermute | solution.py:160
  126.6 9.2 %collective-permute-start.35 = (bf16[128,2048]{1,0:T(8,128)(2,1)S(1)}, bf16[128,2048]{1,0:T(8,128)(2,1)S(1)}, u32[]{:S(2)}, u32[]{:S(2)}) collective-permute-start(bf16[128,2048]{1,0:T(8,128)(2,1)S(1)} %add_convert_fusion.2), channel_id=1, source_target_pairs={{0,4},{4,8},{8,12},{12,14},{14,10},{10,6},{6,2},{2,0},{5,1},{9,5},... | collective-permute-start | bytes 1572872 | tf_op jit(solution)/shard_map/ppermute | solution.py:157
  131.5 4.3 %collective-permute-start.40 = (bf16[128,2048]{1,0:T(8,128)(2,1)S(1)}, bf16[128,2048]{1,0:T(8,128)(2,1)S(1)}, u32[]{:S(2)}, u32[]{:S(2)}) collective-permute-start(bf16[128,2048]{1,0:T(8,128)(2,1)S(1)} %get-tuple-element.55), channel_id=1, source_target_pairs={{0,1},{1,0},{2,3},{3,2},{4,5},{5,4},{6,7},{7,6},{8,9},{9,8},{10,11... | collective-permute-start | bytes 1572872 | tf_op jit(solution)/shard_map/ppermute | solution.py:160
  134.6 16.9 %collective-permute-start.44 = (bf16[128,2048]{1,0:T(8,128)(2,1)S(1)}, bf16[128,2048]{1,0:T(8,128)(2,1)S(1)}, u32[]{:S(2)}, u32[]{:S(2)}) collective-permute-start(bf16[128,2048]{1,0:T(8,128)(2,1)S(1)} %get-tuple-element.57), channel_id=1, source_target_pairs={{0,1},{1,0},{2,3},{3,2},{4,5},{5,4},{6,7},{7,6},{8,9},{9,8},{10,11... | collective-permute-start | bytes 1572872 | tf_op jit(solution)/shard_map/ppermute | solution.py:160
  136.1 15.5 %collective-permute-start.41 = (bf16[128,2048]{1,0:T(8,128)(2,1)S(1)}, bf16[128,2048]{1,0:T(8,128)(2,1)S(1)}, u32[]{:S(2)}, u32[]{:S(2)}) collective-permute-start(bf16[128,2048]{1,0:T(8,128)(2,1)S(1)} %add_convert_fusion.1), channel_id=1, source_target_pairs={{0,4},{4,8},{8,12},{12,14},{14,10},{10,6},{6,2},{2,0},{5,1},{9,5},... | collective-permute-start | bytes 1572872 | tf_op jit(solution)/shard_map/ppermute | solution.py:157

commit v2 on v1

--- a/solution.py
+++ b/solution.py
@@ -50,7 +50,7 @@
         p = jnp.sum(jnp.where(mine, coded, 0.0), axis=1, keepdims=True)
         pre = mm(x, wgu[...], NN)
         gate, up = pre[:, :ff], pre[:, ff:]
-        hid = p * mm(o, wd[...], NT)
+        hid = mm((p * o.astype(F32)).astype(BF16), wd[...], NT)
         sig = jax.nn.sigmoid(gate)
         act = gate * sig
         hidden[...] = (p * (act * up)).astype(BF16)
@@ -72,7 +72,7 @@
         ],
         compiler_params=pltpu.CompilerParams(vmem_limit_bytes=BLOCK_VMEM),
         cost_estimate=pl.CostEstimate(
-            flops=2 * (2 * rows) * width * ff * 5,
+            flops=2 * (2 * rows) * width * ff * 20,
             bytes_accessed=2 * (6 * rows * width + 3 * width * ff),
             transcendentals=2 * rows * ff,
         ),
@@ -165,16 +165,30 @@
     probs = jnp.sum(jnp.where(named, gate_probs[:, :, None], 0.0), axis=1)
     x = jnp.concatenate([tokens, encode(probs)], axis=1)
     o = out_grad
-    wgu = jnp.concatenate([w_gate[0], w_up[0]], axis=1)
     wd = w_down[0]
 
-    acc, total, own = None, None, None
-    held = []
+    def after(v, *others):
+        return lax.optimization_barrier((v, *others))[0]
+
+    acc, total, own, back = None, None, None, None
+    sums, backs, held = [], [], []
     for s in range(chips):
         if s:
-            x, o = forward(x), forward(o)
-        xo, oo = other(x), other(o)
+            x = forward(x)
+            o = forward(o)
+        ties = [o] if s else []
+        if s == 1:
+            ties += [backs[0]]
+        if resident and s == chips - 1 and acc:
+            ties += acc
+        xo = other(after(x, *ties))
+        oo = other(o)
+        if s == 0:
+            pair = lax.optimization_barrier((w_gate[0], w_up[0], xo))[:2]
+            wgu = jnp.concatenate(pair, axis=1)
+            o, wgu = lax.optimization_barrier((o, wgu))
         row_a, row_b, grads, hidden = block_pair(me, devices, x, xo, o, oo, wgu, wd)
+        backs.append(row_b)
         partial = row_a.astype(F32) + other(row_b).astype(F32)
         if s == 0:
             own = partial
@@ -182,6 +196,7 @@
             if total is not None:
                 partial = forward(total).astype(F32) + partial
             total = partial.astype(BF16)
+            sums.append(total)
         held.append((x, xo, o, oo, grads, hidden))
         if len(held) == GROUP or s == chips - 1:
             acc = wgrad_group(

time: 153 us -> 141 us (0.922)
  waiting for transfers between devices: 63.8 us -> 50.8 us
    ppermute x21, waiting for transfers between devices: 63.7 us -> 50.7 us  [forward(): return lax.ppermute(v, 'expert', hop)]
  transfers between devices with their start and end apart: 45 -> 45, of which waited for: 14 -> 17; matrix products, arithmetic and copies ran while one was open for 3% -> 3% of each run, Pallas kernels for 23% -> 25%
where the time goes in v2:
time: 141 us; the launch traced here: 140 us
  waiting for transfers between devices  50.8 us (36%)
  starting transfers between devices  46.5 us (33%)
  Pallas kernels  35.3 us (25%)
  other arithmetic  6.76 us (5%)
    ppermute x21, waiting for transfers between devices, forward(): return lax.ppermute(v, 'expert', hop)  50.7 us
    ppermute x21, starting transfers between devices, forward(): return lax.ppermute(v, 'expert', hop)  42.2 us
    pallas_call x8, Pallas kernels, block_pair(): pl.pallas_call(body, in_specs=[pl.BlockSpec(memory_space=pltpu.SMEM)] + [...  22.2 us
    pallas_call x2, Pallas kernels, wgrad_group(): pl.pallas_call(body, grid=(width // chunk,), in_specs=specs + (acc_specs...  13.1 us
    ppermute x24, starting transfers between devices, other(): return lax.ppermute(v, 'expert', swap)  4.33 us
  transfers between devices with their start and end apart: 45, of which 17 were waited for; matrix products, arithmetic and copies ran while one was open for 3% of the time, Pallas kernels for 25%

profile of v2, /device:TPU:0, one launch (start us, length us, event | category | flops | bytes accessed | tf_op | source)
XLA Modules:
  0.0 140.4 jit_solution(16923458998636370599)
XLA Ops:
  0.6 0.7 select_reduce_fusion
  1.5 1.1 fusion.1.xa.refs_0_
  2.6 0.5 collective-permute-start.1
  3.1 2.6 %collective-permute-start = (bf16[128,2176]{1,0:T(8,128)(2,1)S(1)}, bf16[128,2176]{1,0:T(8,128)(2,1)S(1)}, u32[]{:S(2)}, u32[]{:S(2)}) collective-permute-start(bf16[128,2176]{1,0:T(8,128)(2,1)S(1)} %fusion.1.xa.refs_0_), channel_id=1, source_target_pairs={{0,4},{4,8},{8,12},{12,14},{14,10},{10,6},{6,2},{2,0},{5,1},{9,5},... | collective-permute-start | bytes 1671176 | tf_op jit(solution)/shard_map/ppermute | solution.py:157
  5.9 2.3 %pad_maximum_fusion.wgu = bf16[2048,768]{1,0:T(8,128)(2,1)S(1)} fusion(bf16[2048,384]{1,0:T(8,128)(2,1)} %bitcast.15, bf16[2048,384]{1,0:T(8,128)(2,1)} %bitcast.16), kind=kLoop, calls=%fused_computation | loop fusion | flops 6291456 | bytes 6291456 | tf_op jit(solution)/shard_map/concatenate | solution.py:188
  8.2 1.8 %collective-permute-start.2 = (bf16[128,2048]{1,0:T(8,128)(2,1)S(1)}, bf16[128,2048]{1,0:T(8,128)(2,1)S(1)}, u32[]{:S(2)}, u32[]{:S(2)}) collective-permute-start(bf16[128,2048]{1,0:T(8,128)(2,1)S(1)} %copy-done.1), channel_id=1, source_target_pairs={{0,4},{4,8},{8,12},{12,14},{14,10},{10,6},{6,2},{2,0},{5,1},{9,5},... | collective-permute-start | bytes 1572872 | tf_op jit(solution)/shard_map/ppermute | solution.py:157
  10.0 3.2 %collective-permute-done.xa.refs_2_ = bf16[128,2176]{1,0:T(8,128)(2,1)S(1)} collective-permute-done((bf16[128,2176]{1,0:T(8,128)(2,1)S(1)}, bf16[128,2176]{1,0:T(8,128)(2,1)S(1)}, u32[]{:S(2)}, u32[]{:S(2)}) %collective-permute-start) | collective-permute-done | bytes 557088 | tf_op jit(solution)/shard_map/ppermute | solution.py:157
  13.2 2.1 %collective-permute-start.8 = (bf16[128,2176]{1,0:T(8,128)(2,1)S(1)}, bf16[128,2176]{1,0:T(8,128)(2,1)S(1)}, u32[]{:S(2)}, u32[]{:S(2)}) collective-permute-start(bf16[128,2176]{1,0:T(8,128)(2,1)S(1)} %collective-permute-done.xa.refs_2_), channel_id=1, source_target_pairs={{0,4},{4,8},{8,12},{12,14},{14,10},{10,6},{6,2},{2,0},{5,1},{9,5},... | collective-permute-start | bytes 1671176 | tf_op jit(solution)/shard_map/ppermute | solution.py:157
  15.3 2.8 %block_pair.8 = (bf16[128,2048]{1,0:T(8,128)(2,1)S(1)}, bf16[128,2048]{1,0:T(8,128)(2,1)S(1)}, bf16[256,768]{1,0:T(8,128)(2,1)S(1)}, bf16[256,384]{1,0:T(8,128)(2,1)S(1)}) custom-call(s32[1]{0:T(128)} %bitcast.me, bf16[128,2176]{1,0:T(8,128)(2,1)S(1)} %fusion.1.xa.refs_0_, bf16[128,2176]{1,0:T(8,128)(2,1)S(1)} %collective-permute-done.1.xb.refs_1_, ...), custom_call_target="tpu_custom_call" | custom-call | flops 8053063680 | bytes 7864320 | tf_op jit(solution)/shard_map/block_pair/pallas_call | solution.py:63
  18.1 0.8 collective-permute-done.2.oa.refs_10_
  18.8 2.1 %collective-permute-start.9 = (bf16[128,2048]{1,0:T(8,128)(2,1)S(1)}, bf16[128,2048]{1,0:T(8,128)(2,1)S(1)}, u32[]{:S(2)}, u32[]{:S(2)}) collective-permute-start(bf16[128,2048]{1,0:T(8,128)(2,1)S(1)} %collective-permute-done.2.oa.refs_10_), channel_id=1, source_target_pairs={{0,4},{4,8},{8,12},{12,14},{14,10},{10,6},{6,2},{2,0},{5,1},{9,5},... | collective-permute-start | bytes 1572872 | tf_op jit(solution)/shard_map/ppermute | solution.py:157
  21.1 3.7 %collective-permute-done.8.xa.refs_4_ = bf16[128,2176]{1,0:T(8,128)(2,1)S(1)} collective-permute-done((bf16[128,2176]{1,0:T(8,128)(2,1)S(1)}, bf16[128,2176]{1,0:T(8,128)(2,1)S(1)}, u32[]{:S(2)}, u32[]{:S(2)}) %collective-permute-start.8) | collective-permute-done | bytes 557088 | tf_op jit(solution)/shard_map/ppermute | solution.py:157
  24.8 2.1 %collective-permute-start.14 = (bf16[128,2176]{1,0:T(8,128)(2,1)S(1)}, bf16[128,2176]{1,0:T(8,128)(2,1)S(1)}, u32[]{:S(2)}, u32[]{:S(2)}) collective-permute-start(bf16[128,2176]{1,0:T(8,128)(2,1)S(1)} %collective-permute-done.8.xa.refs_4_), channel_id=1, source_target_pairs={{0,4},{4,8},{8,12},{12,14},{14,10},{10,6},{6,2},{2,0},{5,1},{9,5},... | collective-permute-start | bytes 1671176 | tf_op jit(solution)/shard_map/ppermute | solution.py:157
  26.9 3.5 %collective-permute-done.9.oa.refs_12_ = bf16[128,2048]{1,0:T(8,128)(2,1)S(1)} collective-permute-done((bf16[128,2048]{1,0:T(8,128)(2,1)S(1)}, bf16[128,2048]{1,0:T(8,128)(2,1)S(1)}, u32[]{:S(2)}, u32[]{:S(2)}) %collective-permute-start.9) | collective-permute-done | bytes 524320 | tf_op jit(solution)/shard_map/ppermute | solution.py:157
  30.4 2.1 %collective-permute-start.15 = (bf16[128,2048]{1,0:T(8,128)(2,1)S(1)}, bf16[128,2048]{1,0:T(8,128)(2,1)S(1)}, u32[]{:S(2)}, u32[]{:S(2)}) collective-permute-start(bf16[128,2048]{1,0:T(8,128)(2,1)S(1)} %collective-permute-done.9.oa.refs_12_), channel_id=1, source_target_pairs={{0,4},{4,8},{8,12},{12,14},{14,10},{10,6},{6,2},{2,0},{5,1},{9,5},... | collective-permute-start | bytes 1572872 | tf_op jit(solution)/shard_map/ppermute | solution.py:157
  32.7 2.8 %block_pair.9 = (bf16[128,2048]{1,0:T(8,128)(2,1)S(1)}, bf16[128,2048]{1,0:T(8,128)(2,1)S(1)}, bf16[256,768]{1,0:T(8,128)(2,1)S(1)}, bf16[256,384]{1,0:T(8,128)(2,1)S(1)}) custom-call(s32[1]{0:T(128)} %bitcast.me, bf16[128,2176]{1,0:T(8,128)(2,1)S(1)} %collective-permute-done.xa.refs_2_, bf16[128,2176]{1,0:T(8,128)(2,1)S(1)} %collective-permute-done.4.xb.refs_3_, ...), custom_call_target="tpu_custom_call" | custom-call | flops 8053063680 | bytes 7864320 | tf_op jit(solution)/shard_map/block_pair/pallas_call | solution.py:63
  35.4 0.4 collective-permute-start.6
  35.8 0.5 collective-permute-done.14.xa.refs_6_
  36.4 2.1 %collective-permute-start.20 = (bf16[128,2176]{1,0:T(8,128)(2,1)S(1)}, bf16[128,2176]{1,0:T(8,128)(2,1)S(1)}, u32[]{:S(2)}, u32[]{:S(2)}) collective-permute-start(bf16[128,2176]{1,0:T(8,128)(2,1)S(1)} %collective-permute-done.14.xa.refs_6_), channel_id=1, source_target_pairs={{0,4},{4,8},{8,12},{12,14},{14,10},{10,6},{6,2},{2,0},{5,1},{9,5},... | collective-permute-start | bytes 1671176 | tf_op jit(solution)/shard_map/ppermute | solution.py:157
  38.5 3.5 %collective-permute-done.15.oa.refs_14_ = bf16[128,2048]{1,0:T(8,128)(2,1)S(1)} collective-permute-done((bf16[128,2048]{1,0:T(8,128)(2,1)S(1)}, bf16[128,2048]{1,0:T(8,128)(2,1)S(1)}, u32[]{:S(2)}, u32[]{:S(2)}) %collective-permute-start.15) | collective-permute-done | bytes 524320 | tf_op jit(solution)/shard_map/ppermute | solution.py:157
  42.0 2.1 %collective-permute-start.21 = (bf16[128,2048]{1,0:T(8,128)(2,1)S(1)}, bf16[128,2048]{1,0:T(8,128)(2,1)S(1)}, u32[]{:S(2)}, u32[]{:S(2)}) collective-permute-start(bf16[128,2048]{1,0:T(8,128)(2,1)S(1)} %collective-permute-done.15.oa.refs_14_), channel_id=1, source_target_pairs={{0,4},{4,8},{8,12},{12,14},{14,10},{10,6},{6,2},{2,0},{5,1},{9,5},... | collective-permute-start | bytes 1572872 | tf_op jit(solution)/shard_map/ppermute | solution.py:157
  44.3 2.8 %block_pair.10 = (bf16[128,2048]{1,0:T(8,128)(2,1)S(1)}, bf16[128,2048]{1,0:T(8,128)(2,1)S(1)}, bf16[256,768]{1,0:T(8,128)(2,1)S(1)}, bf16[256,384]{1,0:T(8,128)(2,1)S(1)}) custom-call(s32[1]{0:T(128)} %bitcast.me, bf16[128,2176]{1,0:T(8,128)(2,1)S(1)} %collective-permute-done.8.xa.refs_4_, bf16[128,2176]{1,0:T(8,128)(2,1)S(1)} %collective-permute-done.10.xb.refs_5_, ...), custom_call_target="tpu_custom_call" | custom-call | flops 8053063680 | bytes 7864320 | tf_op jit(solution)/shard_map/block_pair/pallas_call | solution.py:63
  47.0 0.4 collective-permute-start.12
  47.6 0.4 collective-permute-done.20.xa.refs_0_
  48.0 2.1 %collective-permute-start.7 = (bf16[128,2048]{1,0:T(8,128)(2,1)S(1)}, bf16[128,2048]{1,0:T(8,128)(2,1)S(1)}, u32[]{:S(2)}, u32[]{:S(2)}) collective-permute-start(bf16[128,2048]{1,0:T(8,128)(2,1)S(1)} %add_convert_fusion.7), channel_id=1, source_target_pairs={{0,4},{4,8},{8,12},{12,14},{14,10},{10,6},{6,2},{2,0},{5,1},{9,5},... | collective-permute-start | bytes 1572872 | tf_op jit(solution)/shard_map/ppermute | solution.py:157
  50.0 3.5 %collective-permute-done.21.oa.refs_8_ = bf16[128,2048]{1,0:T(8,128)(2,1)S(1)} collective-permute-done((bf16[128,2048]{1,0:T(8,128)(2,1)S(1)}, bf16[128,2048]{1,0:T(8,128)(2,1)S(1)}, u32[]{:S(2)}, u32[]{:S(2)}) %collective-permute-start.21) | collective-permute-done | bytes 524320 | tf_op jit(solution)/shard_map/ppermute | solution.py:157
  53.6 2.1 %collective-permute-start.26 = (bf16[128,2176]{1,0:T(8,128)(2,1)S(1)}, bf16[128,2176]{1,0:T(8,128)(2,1)S(1)}, u32[]{:S(2)}, u32[]{:S(2)}) collective-permute-start(bf16[128,2176]{1,0:T(8,128)(2,1)S(1)} %collective-permute-done.20.xa.refs_0_), channel_id=1, source_target_pairs={{0,4},{4,8},{8,12},{12,14},{14,10},{10,6},{6,2},{2,0},{5,1},{9,5},... | collective-permute-start | bytes 1671176 | tf_op jit(solution)/shard_map/ppermute | solution.py:157
  55.7 1.6 %collective-permute-start.27 = (bf16[128,2048]{1,0:T(8,128)(2,1)S(1)}, bf16[128,2048]{1,0:T(8,128)(2,1)S(1)}, u32[]{:S(2)}, u32[]{:S(2)}) collective-permute-start(bf16[128,2048]{1,0:T(8,128)(2,1)S(1)} %collective-permute-done.21.oa.refs_8_), channel_id=1, source_target_pairs={{0,4},{4,8},{8,12},{12,14},{14,10},{10,6},{6,2},{2,0},{5,1},{9,5},... | collective-permute-start | bytes 1572872 | tf_op jit(solution)/shard_map/ppermute | solution.py:157
  57.3 2.8 %block_pair.11 = (bf16[128,2048]{1,0:T(8,128)(2,1)S(1)}, bf16[128,2048]{1,0:T(8,128)(2,1)S(1)}, bf16[256,768]{1,0:T(8,128)(2,1)S(1)}, bf16[256,384]{1,0:T(8,128)(2,1)S(1)}) custom-call(s32[1]{0:T(128)} %bitcast.me, bf16[128,2176]{1,0:T(8,128)(2,1)S(1)} %collective-permute-done.14.xa.refs_6_, bf16[128,2176]{1,0:T(8,128)(2,1)S(1)} %collective-permute-done.16.xb.refs_7_, ...), custom_call_target="tpu_custom_call" | custom-call | flops 8053063680 | bytes 7864320 | tf_op jit(solution)/shard_map/block_pair/pallas_call | solution.py:63
  60.1 0.6 collective-permute-start.18
  60.7 0.2 add_convert_fusion.6
  60.9 4.3 %collective-permute-done.26.xa.refs_2_ = bf16[128,2176]{1,0:T(8,128)(2,1)S(1)} collective-permute-done((bf16[128,2176]{1,0:T(8,128)(2,1)S(1)}, bf16[128,2176]{1,0:T(8,128)(2,1)S(1)}, u32[]{:S(2)}, u32[]{:S(2)}) %collective-permute-start.26) | collective-permute-done | bytes 557088 | tf_op jit(solution)/shard_map/ppermute | solution.py:157
  65.2 2.1 %collective-permute-start.13 = (bf16[128,2048]{1,0:T(8,128)(2,1)S(1)}, bf16[128,2048]{1,0:T(8,128)(2,1)S(1)}, u32[]{:S(2)}, u32[]{:S(2)}) collective-permute-start(bf16[128,2048]{1,0:T(8,128)(2,1)S(1)} %add_convert_fusion.6), channel_id=1, source_target_pairs={{0,4},{4,8},{8,12},{12,14},{14,10},{10,6},{6,2},{2,0},{5,1},{9,5},... | collective-permute-start | bytes 1572872 | tf_op jit(solution)/shard_map/ppermute | solution.py:157
  67.2 3.5 %collective-permute-done.27.oa.refs_10_ = bf16[128,2048]{1,0:T(8,128)(2,1)S(1)} collective-permute-done((bf16[128,2048]{1,0:T(8,128)(2,1)S(1)}, bf16[128,2048]{1,0:T(8,128)(2,1)S(1)}, u32[]{:S(2)}, u32[]{:S(2)}) %collective-permute-start.27) | collective-permute-done | bytes 524320 | tf_op jit(solution)/shard_map/ppermute | solution.py:157
  70.8 2.1 %collective-permute-start.32 = (bf16[128,2176]{1,0:T(8,128)(2,1)S(1)}, bf16[128,2176]{1,0:T(8,128)(2,1)S(1)}, u32[]{:S(2)}, u32[]{:S(2)}) collective-permute-start(bf16[128,2176]{1,0:T(8,128)(2,1)S(1)} %collective-permute-done.26.xa.refs_2_), channel_id=1, source_target_pairs={{0,4},{4,8},{8,12},{12,14},{14,10},{10,6},{6,2},{2,0},{5,1},{9,5},... | collective-permute-start | bytes 1671176 | tf_op jit(solution)/shard_map/ppermute | solution.py:157
  72.9 1.8 %collective-permute-start.33 = (bf16[128,2048]{1,0:T(8,128)(2,1)S(1)}, bf16[128,2048]{1,0:T(8,128)(2,1)S(1)}, u32[]{:S(2)}, u32[]{:S(2)}) collective-permute-start(bf16[128,2048]{1,0:T(8,128)(2,1)S(1)} %collective-permute-done.27.oa.refs_10_), channel_id=1, source_target_pairs={{0,4},{4,8},{8,12},{12,14},{14,10},{10,6},{6,2},{2,0},{5,1},{9,5},... | collective-permute-start | bytes 1572872 | tf_op jit(solution)/shard_map/ppermute | solution.py:157
  74.7 2.8 %block_pair.12 = (bf16[128,2048]{1,0:T(8,128)(2,1)S(1)}, bf16[128,2048]{1,0:T(8,128)(2,1)S(1)}, bf16[256,768]{1,0:T(8,128)(2,1)S(1)}, bf16[256,384]{1,0:T(8,128)(2,1)S(1)}) custom-call(s32[1]{0:T(128)} %bitcast.me, bf16[128,2176]{1,0:T(8,128)(2,1)S(1)} %collective-permute-done.20.xa.refs_0_, bf16[128,2176]{1,0:T(8,128)(2,1)S(1)} %collective-permute-done.22.xb.refs_1_, ...), custom_call_target="tpu_custom_call" | custom-call | flops 8053063680 | bytes 7864320 | tf_op jit(solution)/shard_map/block_pair/pallas_call | solution.py:63
  77.6 0.5 collective-permute-start.24
  78.1 6.1 %wgrad_group.2 = (f32[2048,384]{1,0:T(8,128)S(1)}, f32[2048,384]{1,0:T(8,128)S(1)}, f32[384,2048]{1,0:T(8,128)S(1)}) custom-call(bf16[128,2176]{1,0:T(8,128)(2,1)S(1)} %fusion.1.xa.refs_0_, bf16[128,2176]{1,0:T(8,128)(2,1)S(1)} %collective-permute-done.1.xb.refs_1_, bf16[128,2176]{1,0:T(8,128)(2,1)S(1)} %collective-permute-done.xa.refs_2_, ...), custom_call_target="tpu_custom_call" | custom-call | flops 4831838208 | bytes 17825792 | tf_op jit(solution)/shard_map/wgrad_group/pallas_call | solution.py:120
  84.2 0.3 add_convert_fusion.5
  84.5 1.6 %collective-permute-start.19 = (bf16[128,2048]{1,0:T(8,128)(2,1)S(1)}, bf16[128,2048]{1,0:T(8,128)(2,1)S(1)}, u32[]{:S(2)}, u32[]{:S(2)}) collective-permute-start(bf16[128,2048]{1,0:T(8,128)(2,1)S(1)} %add_convert_fusion.5), channel_id=1, source_target_pairs={{0,4},{4,8},{8,12},{12,14},{14,10},{10,6},{6,2},{2,0},{5,1},{9,5},... | collective-permute-start | bytes 1572872 | tf_op jit(solution)/shard_map/ppermute | solution.py:157
  86.1 1.9 %collective-permute-done.33.oa.refs_12_ = bf16[128,2048]{1,0:T(8,128)(2,1)S(1)} collective-permute-done((bf16[128,2048]{1,0:T(8,128)(2,1)S(1)}, bf16[128,2048]{1,0:T(8,128)(2,1)S(1)}, u32[]{:S(2)}, u32[]{:S(2)}) %collective-permute-start.33) | collective-permute-done | bytes 524320 | tf_op jit(solution)/shard_map/ppermute | solution.py:157
  88.0 2.1 %collective-permute-start.38 = (bf16[128,2176]{1,0:T(8,128)(2,1)S(1)}, bf16[128,2176]{1,0:T(8,128)(2,1)S(1)}, u32[]{:S(2)}, u32[]{:S(2)}) collective-permute-start(bf16[128,2176]{1,0:T(8,128)(2,1)S(1)} %collective-permute-done.32.xa.refs_4_), channel_id=1, source_target_pairs={{0,4},{4,8},{8,12},{12,14},{14,10},{10,6},{6,2},{2,0},{5,1},{9,5},... | collective-permute-start | bytes 1671176 | tf_op jit(solution)/shard_map/ppermute | solution.py:157
  90.1 1.6 %collective-permute-start.39 = (bf16[128,2048]{1,0:T(8,128)(2,1)S(1)}, bf16[128,2048]{1,0:T(8,128)(2,1)S(1)}, u32[]{:S(2)}, u32[]{:S(2)}) collective-permute-start(bf16[128,2048]{1,0:T(8,128)(2,1)S(1)} %collective-permute-done.33.oa.refs_12_), channel_id=1, source_target_pairs={{0,4},{4,8},{8,12},{12,14},{14,10},{10,6},{6,2},{2,0},{5,1},{9,5},... | collective-permute-start | bytes 1572872 | tf_op jit(solution)/shard_map/ppermute | solution.py:157
  91.7 2.8 %block_pair.13 = (bf16[128,2048]{1,0:T(8,128)(2,1)S(1)}, bf16[128,2048]{1,0:T(8,128)(2,1)S(1)}, bf16[256,768]{1,0:T(8,128)(2,1)S(1)}, bf16[256,384]{1,0:T(8,128)(2,1)S(1)}) custom-call(s32[1]{0:T(128)} %bitcast.me, bf16[128,2176]{1,0:T(8,128)(2,1)S(1)} %collective-permute-done.26.xa.refs_2_, bf16[128,2176]{1,0:T(8,128)(2,1)S(1)} %collective-permute-done.28.xb.refs_3_, ...), custom_call_target="tpu_custom_call" | custom-call | flops 8053063680 | bytes 7864320 | tf_op jit(solution)/shard_map/block_pair/pallas_call | solution.py:63
  94.5 0.6 collective-permute-start.30
  95.1 0.2 add_convert_fusion.4
  95.3 4.3 %collective-permute-done.38.xa.refs_6_ = bf16[128,2176]{1,0:T(8,128)(2,1)S(1)} collective-permute-done((bf16[128,2176]{1,0:T(8,128)(2,1)S(1)}, bf16[128,2176]{1,0:T(8,128)(2,1)S(1)}, u32[]{:S(2)}, u32[]{:S(2)}) %collective-permute-start.38) | collective-permute-done | bytes 557088 | tf_op jit(solution)/shard_map/ppermute | solution.py:157
  99.7 2.0 %collective-permute-start.25 = (bf16[128,2048]{1,0:T(8,128)(2,1)S(1)}, bf16[128,2048]{1,0:T(8,128)(2,1)S(1)}, u32[]{:S(2)}, u32[]{:S(2)}) collective-permute-start(bf16[128,2048]{1,0:T(8,128)(2,1)S(1)} %add_convert_fusion.4), channel_id=1, source_target_pairs={{0,4},{4,8},{8,12},{12,14},{14,10},{10,6},{6,2},{2,0},{5,1},{9,5},... | collective-permute-start | bytes 1572872 | tf_op jit(solution)/shard_map/ppermute | solution.py:157
  101.7 3.6 %collective-permute-done.39.oa.refs_14_ = bf16[128,2048]{1,0:T(8,128)(2,1)S(1)} collective-permute-done((bf16[128,2048]{1,0:T(8,128)(2,1)S(1)}, bf16[128,2048]{1,0:T(8,128)(2,1)S(1)}, u32[]{:S(2)}, u32[]{:S(2)}) %collective-permute-start.39) | collective-permute-done | bytes 524320 | tf_op jit(solution)/shard_map/ppermute | solution.py:157
  105.3 0.5 collective-permute-start.41
  105.8 2.8 %block_pair.14 = (bf16[128,2048]{1,0:T(8,128)(2,1)S(1)}, bf16[128,2048]{1,0:T(8,128)(2,1)S(1)}, bf16[256,768]{1,0:T(8,128)(2,1)S(1)}, bf16[256,384]{1,0:T(8,128)(2,1)S(1)}) custom-call(s32[1]{0:T(128)} %bitcast.me, bf16[128,2176]{1,0:T(8,128)(2,1)S(1)} %collective-permute-done.32.xa.refs_4_, bf16[128,2176]{1,0:T(8,128)(2,1)S(1)} %collective-permute-done.34.xb.refs_5_, ...), custom_call_target="tpu_custom_call" | custom-call | flops 8053063680 | bytes 7864320 | tf_op jit(solution)/shard_map/block_pair/pallas_call | solution.py:63
  108.7 2.2 %collective-permute-done.25 = bf16[128,2048]{1,0:T(8,128)(2,1)S(1)} collective-permute-done((bf16[128,2048]{1,0:T(8,128)(2,1)S(1)}, bf16[128,2048]{1,0:T(8,128)(2,1)S(1)}, u32[]{:S(2)}, u32[]{:S(2)}) %collective-permute-start.25) | collective-permute-done | bytes 524320 | tf_op jit(solution)/shard_map/ppermute | solution.py:157
  110.9 0.2 add_convert_fusion.3
  111.1 2.0 %collective-permute-start.31 = (bf16[128,2048]{1,0:T(8,128)(2,1)S(1)}, bf16[128,2048]{1,0:T(8,128)(2,1)S(1)}, u32[]{:S(2)}, u32[]{:S(2)}) collective-permute-start(bf16[128,2048]{1,0:T(8,128)(2,1)S(1)} %add_convert_fusion.3), channel_id=1, source_target_pairs={{0,4},{4,8},{8,12},{12,14},{14,10},{10,6},{6,2},{2,0},{5,1},{9,5},... | collective-permute-start | bytes 1572872 | tf_op jit(solution)/shard_map/ppermute | solution.py:157
  113.2 2.8 %block_pair.15 = (bf16[128,2048]{1,0:T(8,128)(2,1)S(1)}, bf16[128,2048]{1,0:T(8,128)(2,1)S(1)}, bf16[256,768]{1,0:T(8,128)(2,1)S(1)}, bf16[256,384]{1,0:T(8,128)(2,1)S(1)}) custom-call(s32[1]{0:T(128)} %bitcast.me, bf16[128,2176]{1,0:T(8,128)(2,1)S(1)} %collective-permute-done.38.xa.refs_6_, bf16[128,2176]{1,0:T(8,128)(2,1)S(1)} %collective-permute-done.40.xb.refs_7_, ...), custom_call_target="tpu_custom_call" | custom-call | flops 8053063680 | bytes 7864320 | tf_op jit(solution)/shard_map/block_pair/pallas_call | solution.py:63
  116.1 4.3 %collective-permute-done.31 = bf16[128,2048]{1,0:T(8,128)(2,1)S(1)} collective-permute-done((bf16[128,2048]{1,0:T(8,128)(2,1)S(1)}, bf16[128,2048]{1,0:T(8,128)(2,1)S(1)}, u32[]{:S(2)}, u32[]{:S(2)}) %collective-permute-start.31) | collective-permute-done | bytes 524320 | tf_op jit(solution)/shard_map/ppermute | solution.py:157
  120.4 0.2 add_convert_fusion.2
  120.6 2.0 %collective-permute-start.37 = (bf16[128,2048]{1,0:T(8,128)(2,1)S(1)}, bf16[128,2048]{1,0:T(8,128)(2,1)S(1)}, u32[]{:S(2)}, u32[]{:S(2)}) collective-permute-start(bf16[128,2048]{1,0:T(8,128)(2,1)S(1)} %add_convert_fusion.2), channel_id=1, source_target_pairs={{0,4},{4,8},{8,12},{12,14},{14,10},{10,6},{6,2},{2,0},{5,1},{9,5},... | collective-permute-start | bytes 1572872 | tf_op jit(solution)/shard_map/ppermute | solution.py:157
  122.7 7.2 %collective-permute-done.37 = bf16[128,2048]{1,0:T(8,128)(2,1)S(1)} collective-permute-done((bf16[128,2048]{1,0:T(8,128)(2,1)S(1)}, bf16[128,2048]{1,0:T(8,128)(2,1)S(1)}, u32[]{:S(2)}, u32[]{:S(2)}) %collective-permute-start.37) | collective-permute-done | bytes 524320 | tf_op jit(solution)/shard_map/ppermute | solution.py:157
  129.9 0.2 add_convert_fusion.1
  130.1 2.0 %collective-permute-start.43 = (bf16[128,2048]{1,0:T(8,128)(2,1)S(1)}, bf16[128,2048]{1,0:T(8,128)(2,1)S(1)}, u32[]{:S(2)}, u32[]{:S(2)}) collective-permute-start(bf16[128,2048]{1,0:T(8,128)(2,1)S(1)} %add_convert_fusion.1), channel_id=1, source_target_pairs={{0,4},{4,8},{8,12},{12,14},{14,10},{10,6},{6,2},{2,0},{5,1},{9,5},... | collective-permute-start | bytes 1572872 | tf_op jit(solution)/shard_map/ppermute | solution.py:157
  132.2 7.0 %wgrad_group.3 = (bf16[2048,384]{1,0:T(8,128)(2,1)}, bf16[2048,384]{1,0:T(8,128)(2,1)}, bf16[384,2048]{1,0:T(8,128)(2,1)}) custom-call(bf16[128,2176]{1,0:T(8,128)(2,1)S(1)} %collective-permute-done.20.xa.refs_0_, bf16[128,2176]{1,0:T(8,128)(2,1)S(1)} %collective-permute-done.22.xb.refs_1_, bf16[128,2176]{1,0:T(8,128)(2,1)S(1)} %collective-permute-done.26.xa.refs_2_, ...), custom_call_target="tpu_custom_call" | custom-call | flops 4831838208 | bytes 17825792 | tf_op jit(solution)/shard_map/wgrad_group/pallas_call | solution.py:120
  139.3 1.0 add_convert_fusion
  (54 shorter events, 1.4 us)
Async XLA Ops:
  2.6 3.3 %collective-permute-start.1 = (bf16[128,2176]{1,0:T(8,128)(2,1)S(1)}, bf16[128,2176]{1,0:T(8,128)(2,1)S(1)}, u32[]{:S(2)}, u32[]{:S(2)}) collective-permute-start(bf16[128,2176]{1,0:T(8,128)(2,1)S(1)} %fusion.1.xa.refs_0_), channel_id=1, source_target_pairs={{0,1},{1,0},{2,3},{3,2},{4,5},{5,4},{6,7},{7,6},{8,9},{9,8},{10,11... | collective-permute-start | bytes 1671176 | tf_op jit(solution)/shard_map/ppermute | solution.py:160
  3.1 10.1 %collective-permute-start = (bf16[128,2176]{1,0:T(8,128)(2,1)S(1)}, bf16[128,2176]{1,0:T(8,128)(2,1)S(1)}, u32[]{:S(2)}, u32[]{:S(2)}) collective-permute-start(bf16[128,2176]{1,0:T(8,128)(2,1)S(1)} %fusion.1.xa.refs_0_), channel_id=1, source_target_pairs={{0,4},{4,8},{8,12},{12,14},{14,10},{10,6},{6,2},{2,0},{5,1},{9,5},... | collective-permute-start | bytes 1671176 | tf_op jit(solution)/shard_map/ppermute | solution.py:157
  5.7 9.5 %collective-permute-start.3 = (bf16[128,2048]{1,0:T(8,128)(2,1)}, bf16[128,2048]{1,0:T(8,128)(2,1)S(1)}, u32[]{:S(2)}, u32[]{:S(2)}) collective-permute-start(bf16[128,2048]{1,0:T(8,128)(2,1)} %refs_8_), channel_id=1, source_target_pairs={{0,1},{1,0},{2,3},{3,2},{4,5},{5,4},{6,7},{7,6},{8,9},{9,8},{10,11... | collective-permute-start | bytes 1572872 | tf_op jit(solution)/shard_map/ppermute | solution.py:160
  5.9 2.3 %copy-start.1 = (bf16[128,2048]{1,0:T(8,128)(2,1)S(1)}, bf16[128,2048]{1,0:T(8,128)(2,1)}, u32[]{:S(2)}) copy-start(bf16[128,2048]{1,0:T(8,128)(2,1)} %refs_8_) | copy-start | bytes 1572868
  5.9 9.4 %copy-start = (bf16[1,384,2048]{2,1,0:T(8,128)(2,1)S(1)}, bf16[1,384,2048]{2,1,0:T(8,128)(2,1)}, u32[]{:S(2)}) copy-start(bf16[1,384,2048]{2,1,0:T(8,128)(2,1)} %param.13) | copy-start | bytes 4718596
  8.2 10.7 %collective-permute-start.2 = (bf16[128,2048]{1,0:T(8,128)(2,1)S(1)}, bf16[128,2048]{1,0:T(8,128)(2,1)S(1)}, u32[]{:S(2)}, u32[]{:S(2)}) collective-permute-start(bf16[128,2048]{1,0:T(8,128)(2,1)S(1)} %copy-done.1), channel_id=1, source_target_pairs={{0,4},{4,8},{8,12},{12,14},{14,10},{10,6},{6,2},{2,0},{5,1},{9,5},... | collective-permute-start | bytes 1572872 | tf_op jit(solution)/shard_map/ppermute | solution.py:157
  13.2 11.6 %collective-permute-start.8 = (bf16[128,2176]{1,0:T(8,128)(2,1)S(1)}, bf16[128,2176]{1,0:T(8,128)(2,1)S(1)}, u32[]{:S(2)}, u32[]{:S(2)}) collective-permute-start(bf16[128,2176]{1,0:T(8,128)(2,1)S(1)} %collective-permute-done.xa.refs_2_), channel_id=1, source_target_pairs={{0,4},{4,8},{8,12},{12,14},{14,10},{10,6},{6,2},{2,0},{5,1},{9,5},... | collective-permute-start | bytes 1671176 | tf_op jit(solution)/shard_map/ppermute | solution.py:157
  18.8 13.8 %collective-permute-start.4 = (bf16[128,2176]{1,0:T(8,128)(2,1)S(1)}, bf16[128,2176]{1,0:T(8,128)(2,1)S(1)}, u32[]{:S(2)}, u32[]{:S(2)}) collective-permute-start(bf16[128,2176]{1,0:T(8,128)(2,1)S(1)} %collective-permute-done.xa.refs_2_), channel_id=1, source_target_pairs={{0,1},{1,0},{2,3},{3,2},{4,5},{5,4},{6,7},{7,6},{8,9},{9,8},{10,11... | collective-permute-start | bytes 1671176 | tf_op jit(solution)/shard_map/ppermute | solution.py:160
  18.8 11.6 %collective-permute-start.9 = (bf16[128,2048]{1,0:T(8,128)(2,1)S(1)}, bf16[128,2048]{1,0:T(8,128)(2,1)S(1)}, u32[]{:S(2)}, u32[]{:S(2)}) collective-permute-start(bf16[128,2048]{1,0:T(8,128)(2,1)S(1)} %collective-permute-done.2.oa.refs_10_), channel_id=1, source_target_pairs={{0,4},{4,8},{8,12},{12,14},{14,10},{10,6},{6,2},{2,0},{5,1},{9,5},... | collective-permute-start | bytes 1572872 | tf_op jit(solution)/shard_map/ppermute | solution.py:157
  20.9 11.6 %collective-permute-start.5 = (bf16[128,2048]{1,0:T(8,128)(2,1)S(1)}, bf16[128,2048]{1,0:T(8,128)(2,1)S(1)}, u32[]{:S(2)}, u32[]{:S(2)}) collective-permute-start(bf16[128,2048]{1,0:T(8,128)(2,1)S(1)} %collective-permute-done.2.oa.refs_10_), channel_id=1, source_target_pairs={{0,1},{1,0},{2,3},{3,2},{4,5},{5,4},{6,7},{7,6},{8,9},{9,8},{10,11... | collective-permute-start | bytes 1572872 | tf_op jit(solution)/shard_map/ppermute | solution.py:160
  24.8 11.6 %collective-permute-start.14 = (bf16[128,2176]{1,0:T(8,128)(2,1)S(1)}, bf16[128,2176]{1,0:T(8,128)(2,1)S(1)}, u32[]{:S(2)}, u32[]{:S(2)}) collective-permute-start(bf16[128,2176]{1,0:T(8,128)(2,1)S(1)} %collective-permute-done.8.xa.refs_4_), channel_id=1, source_target_pairs={{0,4},{4,8},{8,12},{12,14},{14,10},{10,6},{6,2},{2,0},{5,1},{9,5},... | collective-permute-start | bytes 1671176 | tf_op jit(solution)/shard_map/ppermute | solution.py:157
  30.4 13.7 %collective-permute-start.10 = (bf16[128,2176]{1,0:T(8,128)(2,1)S(1)}, bf16[128,2176]{1,0:T(8,128)(2,1)S(1)}, u32[]{:S(2)}, u32[]{:S(2)}) collective-permute-start(bf16[128,2176]{1,0:T(8,128)(2,1)S(1)} %collective-permute-done.8.xa.refs_4_), channel_id=1, source_target_pairs={{0,1},{1,0},{2,3},{3,2},{4,5},{5,4},{6,7},{7,6},{8,9},{9,8},{10,11... | collective-permute-start | bytes 1671176 | tf_op jit(solution)/shard_map/ppermute | solution.py:160
  30.4 11.6 %collective-permute-start.15 = (bf16[128,2048]{1,0:T(8,128)(2,1)S(1)}, bf16[128,2048]{1,0:T(8,128)(2,1)S(1)}, u32[]{:S(2)}, u32[]{:S(2)}) collective-permute-start(bf16[128,2048]{1,0:T(8,128)(2,1)S(1)} %collective-permute-done.9.oa.refs_12_), channel_id=1, source_target_pairs={{0,4},{4,8},{8,12},{12,14},{14,10},{10,6},{6,2},{2,0},{5,1},{9,5},... | collective-permute-start | bytes 1572872 | tf_op jit(solution)/shard_map/ppermute | solution.py:157
  32.5 9.5 %collective-permute-start.11 = (bf16[128,2048]{1,0:T(8,128)(2,1)S(1)}, bf16[128,2048]{1,0:T(8,128)(2,1)S(1)}, u32[]{:S(2)}, u32[]{:S(2)}) collective-permute-start(bf16[128,2048]{1,0:T(8,128)(2,1)S(1)} %collective-permute-done.9.oa.refs_12_), channel_id=1, source_target_pairs={{0,1},{1,0},{2,3},{3,2},{4,5},{5,4},{6,7},{7,6},{8,9},{9,8},{10,11... | collective-permute-start | bytes 1572872 | tf_op jit(solution)/shard_map/ppermute | solution.py:160
  35.4 11.6 %collective-permute-start.6 = (bf16[128,2048]{1,0:T(8,128)(2,1)S(1)}, bf16[128,2048]{1,0:T(8,128)(2,1)S(1)}, u32[]{:S(2)}, u32[]{:S(2)}) collective-permute-start(bf16[128,2048]{1,0:T(8,128)(2,1)S(1)} %get-tuple-element.60), channel_id=1, source_target_pairs={{0,1},{1,0},{2,3},{3,2},{4,5},{5,4},{6,7},{7,6},{8,9},{9,8},{10,11... | collective-permute-start | bytes 1572872 | tf_op jit(solution)/shard_map/ppermute | solution.py:160
  36.4 11.6 %collective-permute-start.20 = (bf16[128,2176]{1,0:T(8,128)(2,1)S(1)}, bf16[128,2176]{1,0:T(8,128)(2,1)S(1)}, u32[]{:S(2)}, u32[]{:S(2)}) collective-permute-start(bf16[128,2176]{1,0:T(8,128)(2,1)S(1)} %collective-permute-done.14.xa.refs_6_), channel_id=1, source_target_pairs={{0,4},{4,8},{8,12},{12,14},{14,10},{10,6},{6,2},{2,0},{5,1},{9,5},... | collective-permute-start | bytes 1671176 | tf_op jit(solution)/shard_map/ppermute | solution.py:157
  42.0 13.7 %collective-permute-start.16 = (bf16[128,2176]{1,0:T(8,128)(2,1)S(1)}, bf16[128,2176]{1,0:T(8,128)(2,1)S(1)}, u32[]{:S(2)}, u32[]{:S(2)}) collective-permute-start(bf16[128,2176]{1,0:T(8,128)(2,1)S(1)} %collective-permute-done.14.xa.refs_6_), channel_id=1, source_target_pairs={{0,1},{1,0},{2,3},{3,2},{4,5},{5,4},{6,7},{7,6},{8,9},{9,8},{10,11... | collective-permute-start | bytes 1671176 | tf_op jit(solution)/shard_map/ppermute | solution.py:160
  42.0 11.6 %collective-permute-start.21 = (bf16[128,2048]{1,0:T(8,128)(2,1)S(1)}, bf16[128,2048]{1,0:T(8,128)(2,1)S(1)}, u32[]{:S(2)}, u32[]{:S(2)}) collective-permute-start(bf16[128,2048]{1,0:T(8,128)(2,1)S(1)} %collective-permute-done.15.oa.refs_14_), channel_id=1, source_target_pairs={{0,4},{4,8},{8,12},{12,14},{14,10},{10,6},{6,2},{2,0},{5,1},{9,5},... | collective-permute-start | bytes 1572872 | tf_op jit(solution)/shard_map/ppermute | solution.py:157
  44.1 11.6 %collective-permute-start.17 = (bf16[128,2048]{1,0:T(8,128)(2,1)S(1)}, bf16[128,2048]{1,0:T(8,128)(2,1)S(1)}, u32[]{:S(2)}, u32[]{:S(2)}) collective-permute-start(bf16[128,2048]{1,0:T(8,128)(2,1)S(1)} %collective-permute-done.15.oa.refs_14_), channel_id=1, source_target_pairs={{0,1},{1,0},{2,3},{3,2},{4,5},{5,4},{6,7},{7,6},{8,9},{9,8},{10,11... | collective-permute-start | bytes 1572872 | tf_op jit(solution)/shard_map/ppermute | solution.py:160
  47.0 10.3 %collective-permute-start.12 = (bf16[128,2048]{1,0:T(8,128)(2,1)S(1)}, bf16[128,2048]{1,0:T(8,128)(2,1)S(1)}, u32[]{:S(2)}, u32[]{:S(2)}) collective-permute-start(bf16[128,2048]{1,0:T(8,128)(2,1)S(1)} %get-tuple-element.63), channel_id=1, source_target_pairs={{0,1},{1,0},{2,3},{3,2},{4,5},{5,4},{6,7},{7,6},{8,9},{9,8},{10,11... | collective-permute-start | bytes 1572872 | tf_op jit(solution)/shard_map/ppermute | solution.py:160
  48.0 12.1 %collective-permute-start.7 = (bf16[128,2048]{1,0:T(8,128)(2,1)S(1)}, bf16[128,2048]{1,0:T(8,128)(2,1)S(1)}, u32[]{:S(2)}, u32[]{:S(2)}) collective-permute-start(bf16[128,2048]{1,0:T(8,128)(2,1)S(1)} %add_convert_fusion.7), channel_id=1, source_target_pairs={{0,4},{4,8},{8,12},{12,14},{14,10},{10,6},{6,2},{2,0},{5,1},{9,5},... | collective-permute-start | bytes 1572872 | tf_op jit(solution)/shard_map/ppermute | solution.py:157
  53.6 11.6 %collective-permute-start.26 = (bf16[128,2176]{1,0:T(8,128)(2,1)S(1)}, bf16[128,2176]{1,0:T(8,128)(2,1)S(1)}, u32[]{:S(2)}, u32[]{:S(2)}) collective-permute-start(bf16[128,2176]{1,0:T(8,128)(2,1)S(1)} %collective-permute-done.20.xa.refs_0_), channel_id=1, source_target_pairs={{0,4},{4,8},{8,12},{12,14},{14,10},{10,6},{6,2},{2,0},{5,1},{9,5},... | collective-permute-start | bytes 1671176 | tf_op jit(solution)/shard_map/ppermute | solution.py:157
  55.7 17.2 %collective-permute-start.22 = (bf16[128,2176]{1,0:T(8,128)(2,1)S(1)}, bf16[128,2176]{1,0:T(8,128)(2,1)S(1)}, u32[]{:S(2)}, u32[]{:S(2)}) collective-permute-start(bf16[128,2176]{1,0:T(8,128)(2,1)S(1)} %collective-permute-done.20.xa.refs_0_), channel_id=1, source_target_pairs={{0,1},{1,0},{2,3},{3,2},{4,5},{5,4},{6,7},{7,6},{8,9},{9,8},{10,11... | collective-permute-start | bytes 1671176 | tf_op jit(solution)/shard_map/ppermute | solution.py:160
  55.7 15.1 %collective-permute-start.27 = (bf16[128,2048]{1,0:T(8,128)(2,1)S(1)}, bf16[128,2048]{1,0:T(8,128)(2,1)S(1)}, u32[]{:S(2)}, u32[]{:S(2)}) collective-permute-start(bf16[128,2048]{1,0:T(8,128)(2,1)S(1)} %collective-permute-done.21.oa.refs_8_), channel_id=1, source_target_pairs={{0,4},{4,8},{8,12},{12,14},{14,10},{10,6},{6,2},{2,0},{5,1},{9,5},... | collective-permute-start | bytes 1572872 | tf_op jit(solution)/shard_map/ppermute | solution.py:157
  57.3 15.6 %collective-permute-start.23 = (bf16[128,2048]{1,0:T(8,128)(2,1)S(1)}, bf16[128,2048]{1,0:T(8,128)(2,1)S(1)}, u32[]{:S(2)}, u32[]{:S(2)}) collective-permute-start(bf16[128,2048]{1,0:T(8,128)(2,1)S(1)} %collective-permute-done.21.oa.refs_8_), channel_id=1, source_target_pairs={{0,1},{1,0},{2,3},{3,2},{4,5},{5,4},{6,7},{7,6},{8,9},{9,8},{10,11... | collective-permute-start | bytes 1572872 | tf_op jit(solution)/shard_map/ppermute | solution.py:160
  60.1 17.4 %collective-permute-start.18 = (bf16[128,2048]{1,0:T(8,128)(2,1)S(1)}, bf16[128,2048]{1,0:T(8,128)(2,1)S(1)}, u32[]{:S(2)}, u32[]{:S(2)}) collective-permute-start(bf16[128,2048]{1,0:T(8,128)(2,1)S(1)} %get-tuple-element.66), channel_id=1, source_target_pairs={{0,1},{1,0},{2,3},{3,2},{4,5},{5,4},{6,7},{7,6},{8,9},{9,8},{10,11... | collective-permute-start | bytes 1572872 | tf_op jit(solution)/shard_map/ppermute | solution.py:160
  65.2 12.4 %collective-permute-start.13 = (bf16[128,2048]{1,0:T(8,128)(2,1)S(1)}, bf16[128,2048]{1,0:T(8,128)(2,1)S(1)}, u32[]{:S(2)}, u32[]{:S(2)}) collective-permute-start(bf16[128,2048]{1,0:T(8,128)(2,1)S(1)} %add_convert_fusion.6), channel_id=1, source_target_pairs={{0,4},{4,8},{8,12},{12,14},{14,10},{10,6},{6,2},{2,0},{5,1},{9,5},... | collective-permute-start | bytes 1572872 | tf_op jit(solution)/shard_map/ppermute | solution.py:157
  70.8 13.7 %collective-permute-start.32 = (bf16[128,2176]{1,0:T(8,128)(2,1)S(1)}, bf16[128,2176]{1,0:T(8,128)(2,1)S(1)}, u32[]{:S(2)}, u32[]{:S(2)}) collective-permute-start(bf16[128,2176]{1,0:T(8,128)(2,1)S(1)} %collective-permute-done.26.xa.refs_2_), channel_id=1, source_target_pairs={{0,4},{4,8},{8,12},{12,14},{14,10},{10,6},{6,2},{2,0},{5,1},{9,5},... | collective-permute-start | bytes 1671176 | tf_op jit(solution)/shard_map/ppermute | solution.py:157
  72.9 17.2 %collective-permute-start.28 = (bf16[128,2176]{1,0:T(8,128)(2,1)S(1)}, bf16[128,2176]{1,0:T(8,128)(2,1)S(1)}, u32[]{:S(2)}, u32[]{:S(2)}) collective-permute-start(bf16[128,2176]{1,0:T(8,128)(2,1)S(1)} %collective-permute-done.26.xa.refs_2_), channel_id=1, source_target_pairs={{0,1},{1,0},{2,3},{3,2},{4,5},{5,4},{6,7},{7,6},{8,9},{9,8},{10,11... | collective-permute-start | bytes 1671176 | tf_op jit(solution)/shard_map/ppermute | solution.py:160
  72.9 15.1 %collective-permute-start.33 = (bf16[128,2048]{1,0:T(8,128)(2,1)S(1)}, bf16[128,2048]{1,0:T(8,128)(2,1)S(1)}, u32[]{:S(2)}, u32[]{:S(2)}) collective-permute-start(bf16[128,2048]{1,0:T(8,128)(2,1)S(1)} %collective-permute-done.27.oa.refs_10_), channel_id=1, source_target_pairs={{0,4},{4,8},{8,12},{12,14},{14,10},{10,6},{6,2},{2,0},{5,1},{9,5},... | collective-permute-start | bytes 1572872 | tf_op jit(solution)/shard_map/ppermute | solution.py:157
  77.5 12.6 %collective-permute-start.29 = (bf16[128,2048]{1,0:T(8,128)(2,1)S(1)}, bf16[128,2048]{1,0:T(8,128)(2,1)S(1)}, u32[]{:S(2)}, u32[]{:S(2)}) collective-permute-start(bf16[128,2048]{1,0:T(8,128)(2,1)S(1)} %collective-permute-done.27.oa.refs_10_), channel_id=1, source_target_pairs={{0,1},{1,0},{2,3},{3,2},{4,5},{5,4},{6,7},{7,6},{8,9},{9,8},{10,11... | collective-permute-start | bytes 1572872 | tf_op jit(solution)/shard_map/ppermute | solution.py:160
  77.6 14.1 %collective-permute-start.24 = (bf16[128,2048]{1,0:T(8,128)(2,1)S(1)}, bf16[128,2048]{1,0:T(8,128)(2,1)S(1)}, u32[]{:S(2)}, u32[]{:S(2)}) collective-permute-start(bf16[128,2048]{1,0:T(8,128)(2,1)S(1)} %get-tuple-element.69), channel_id=1, source_target_pairs={{0,1},{1,0},{2,3},{3,2},{4,5},{5,4},{6,7},{7,6},{8,9},{9,8},{10,11... | collective-permute-start | bytes 1572872 | tf_op jit(solution)/shard_map/ppermute | solution.py:160
  84.5 10.0 %collective-permute-start.19 = (bf16[128,2048]{1,0:T(8,128)(2,1)S(1)}, bf16[128,2048]{1,0:T(8,128)(2,1)S(1)}, u32[]{:S(2)}, u32[]{:S(2)}) collective-permute-start(bf16[128,2048]{1,0:T(8,128)(2,1)S(1)} %add_convert_fusion.5), channel_id=1, source_target_pairs={{0,4},{4,8},{8,12},{12,14},{14,10},{10,6},{6,2},{2,0},{5,1},{9,5},... | collective-permute-start | bytes 1572872 | tf_op jit(solution)/shard_map/ppermute | solution.py:157
  88.0 11.7 %collective-permute-start.38 = (bf16[128,2176]{1,0:T(8,128)(2,1)S(1)}, bf16[128,2176]{1,0:T(8,128)(2,1)S(1)}, u32[]{:S(2)}, u32[]{:S(2)}) collective-permute-start(bf16[128,2176]{1,0:T(8,128)(2,1)S(1)} %collective-permute-done.32.xa.refs_4_), channel_id=1, source_target_pairs={{0,4},{4,8},{8,12},{12,14},{14,10},{10,6},{6,2},{2,0},{5,1},{9,5},... | collective-permute-start | bytes 1671176 | tf_op jit(solution)/shard_map/ppermute | solution.py:157
  90.1 15.7 %collective-permute-start.34 = (bf16[128,2176]{1,0:T(8,128)(2,1)S(1)}, bf16[128,2176]{1,0:T(8,128)(2,1)S(1)}, u32[]{:S(2)}, u32[]{:S(2)}) collective-permute-start(bf16[128,2176]{1,0:T(8,128)(2,1)S(1)} %collective-permute-done.32.xa.refs_4_), channel_id=1, source_target_pairs={{0,1},{1,0},{2,3},{3,2},{4,5},{5,4},{6,7},{7,6},{8,9},{9,8},{10,11... | collective-permute-start | bytes 1671176 | tf_op jit(solution)/shard_map/ppermute | solution.py:160
  90.1 15.2 %collective-permute-start.39 = (bf16[128,2048]{1,0:T(8,128)(2,1)S(1)}, bf16[128,2048]{1,0:T(8,128)(2,1)S(1)}, u32[]{:S(2)}, u32[]{:S(2)}) collective-permute-start(bf16[128,2048]{1,0:T(8,128)(2,1)S(1)} %collective-permute-done.33.oa.refs_12_), channel_id=1, source_target_pairs={{0,4},{4,8},{8,12},{12,14},{14,10},{10,6},{6,2},{2,0},{5,1},{9,5},... | collective-permute-start | bytes 1572872 | tf_op jit(solution)/shard_map/ppermute | solution.py:157
  91.7 13.6 %collective-permute-start.35 = (bf16[128,2048]{1,0:T(8,128)(2,1)S(1)}, bf16[128,2048]{1,0:T(8,128)(2,1)S(1)}, u32[]{:S(2)}, u32[]{:S(2)}) collective-permute-start(bf16[128,2048]{1,0:T(8,128)(2,1)S(1)} %collective-permute-done.33.oa.refs_12_), channel_id=1, source_target_pairs={{0,1},{1,0},{2,3},{3,2},{4,5},{5,4},{6,7},{7,6},{8,9},{9,8},{10,11... | collective-permute-start | bytes 1572872 | tf_op jit(solution)/shard_map/ppermute | solution.py:160
  94.5 14.2 %collective-permute-start.30 = (bf16[128,2048]{1,0:T(8,128)(2,1)S(1)}, bf16[128,2048]{1,0:T(8,128)(2,1)S(1)}, u32[]{:S(2)}, u32[]{:S(2)}) collective-permute-start(bf16[128,2048]{1,0:T(8,128)(2,1)S(1)} %get-tuple-element.72), channel_id=1, source_target_pairs={{0,1},{1,0},{2,3},{3,2},{4,5},{5,4},{6,7},{7,6},{8,9},{9,8},{10,11... | collective-permute-start | bytes 1572872 | tf_op jit(solution)/shard_map/ppermute | solution.py:160
  99.7 11.2 %collective-permute-start.25 = (bf16[128,2048]{1,0:T(8,128)(2,1)S(1)}, bf16[128,2048]{1,0:T(8,128)(2,1)S(1)}, u32[]{:S(2)}, u32[]{:S(2)}) collective-permute-start(bf16[128,2048]{1,0:T(8,128)(2,1)S(1)} %add_convert_fusion.4), channel_id=1, source_target_pairs={{0,4},{4,8},{8,12},{12,14},{14,10},{10,6},{6,2},{2,0},{5,1},{9,5},... | collective-permute-start | bytes 1572872 | tf_op jit(solution)/shard_map/ppermute | solution.py:157
  105.3 7.9 %collective-permute-start.40 = (bf16[128,2176]{1,0:T(8,128)(2,1)S(1)}, bf16[128,2176]{1,0:T(8,128)(2,1)S(1)}, u32[]{:S(2)}, u32[]{:S(2)}) collective-permute-start(bf16[128,2176]{1,0:T(8,128)(2,1)S(1)} %collective-permute-done.38.xa.refs_6_), channel_id=1, source_target_pairs={{0,1},{1,0},{2,3},{3,2},{4,5},{5,4},{6,7},{7,6},{8,9},{9,8},{10,11... | collective-permute-start | bytes 1671176 | tf_op jit(solution)/shard_map/ppermute | solution.py:160
  105.3 7.9 %collective-permute-start.41 = (bf16[128,2048]{1,0:T(8,128)(2,1)S(1)}, bf16[128,2048]{1,0:T(8,128)(2,1)S(1)}, u32[]{:S(2)}, u32[]{:S(2)}) collective-permute-start(bf16[128,2048]{1,0:T(8,128)(2,1)S(1)} %collective-permute-done.39.oa.refs_14_), channel_id=1, source_target_pairs={{0,1},{1,0},{2,3},{3,2},{4,5},{5,4},{6,7},{7,6},{8,9},{9,8},{10,11... | collective-permute-start | bytes 1572872 | tf_op jit(solution)/shard_map/ppermute | solution.py:160
  108.6 7.5 %collective-permute-start.36 = (bf16[128,2048]{1,0:T(8,128)(2,1)S(1)}, bf16[128,2048]{1,0:T(8,128)(2,1)S(1)}, u32[]{:S(2)}, u32[]{:S(2)}) collective-permute-start(bf16[128,2048]{1,0:T(8,128)(2,1)S(1)} %get-tuple-element.75), channel_id=1, source_target_pairs={{0,1},{1,0},{2,3},{3,2},{4,5},{5,4},{6,7},{7,6},{8,9},{9,8},{10,11... | collective-permute-start | bytes 1572872 | tf_op jit(solution)/shard_map/ppermute | solution.py:160
  111.1 9.2 %collective-permute-start.31 = (bf16[128,2048]{1,0:T(8,128)(2,1)S(1)}, bf16[128,2048]{1,0:T(8,128)(2,1)S(1)}, u32[]{:S(2)}, u32[]{:S(2)}) collective-permute-start(bf16[128,2048]{1,0:T(8,128)(2,1)S(1)} %add_convert_fusion.3), channel_id=1, source_target_pairs={{0,4},{4,8},{8,12},{12,14},{14,10},{10,6},{6,2},{2,0},{5,1},{9,5},... | collective-permute-start | bytes 1572872 | tf_op jit(solution)/shard_map/ppermute | solution.py:157
  116.0 6.7 %collective-permute-start.42 = (bf16[128,2048]{1,0:T(8,128)(2,1)S(1)}, bf16[128,2048]{1,0:T(8,128)(2,1)S(1)}, u32[]{:S(2)}, u32[]{:S(2)}) collective-permute-start(bf16[128,2048]{1,0:T(8,128)(2,1)S(1)} %get-tuple-element.89), channel_id=1, source_target_pairs={{0,1},{1,0},{2,3},{3,2},{4,5},{5,4},{6,7},{7,6},{8,9},{9,8},{10,11... | collective-permute-start | bytes 1572872 | tf_op jit(solution)/shard_map/ppermute | solution.py:160
  120.6 9.2 %collective-permute-start.37 = (bf16[128,2048]{1,0:T(8,128)(2,1)S(1)}, bf16[128,2048]{1,0:T(8,128)(2,1)S(1)}, u32[]{:S(2)}, u32[]{:S(2)}) collective-permute-start(bf16[128,2048]{1,0:T(8,128)(2,1)S(1)} %add_convert_fusion.2), channel_id=1, source_target_pairs={{0,4},{4,8},{8,12},{12,14},{14,10},{10,6},{6,2},{2,0},{5,1},{9,5},... | collective-permute-start | bytes 1572872 | tf_op jit(solution)/shard_map/ppermute | solution.py:157
  122.7 16.5 %collective-permute-start.44 = (bf16[128,2048]{1,0:T(8,128)(2,1)S(1)}, bf16[128,2048]{1,0:T(8,128)(2,1)S(1)}, u32[]{:S(2)}, u32[]{:S(2)}) collective-permute-start(bf16[128,2048]{1,0:T(8,128)(2,1)S(1)} %get-tuple-element.57), channel_id=1, source_target_pairs={{0,1},{1,0},{2,3},{3,2},{4,5},{5,4},{6,7},{7,6},{8,9},{9,8},{10,11... | collective-permute-start | bytes 1572872 | tf_op jit(solution)/shard_map/ppermute | solution.py:160
  130.1 9.2 %collective-permute-start.43 = (bf16[128,2048]{1,0:T(8,128)(2,1)S(1)}, bf16[128,2048]{1,0:T(8,128)(2,1)S(1)}, u32[]{:S(2)}, u32[]{:S(2)}) collective-permute-start(bf16[128,2048]{1,0:T(8,128)(2,1)S(1)} %add_convert_fusion.1), channel_id=1, source_target_pairs={{0,4},{4,8},{8,12},{12,14},{14,10},{10,6},{6,2},{2,0},{5,1},{9,5},... | collective-permute-start | bytes 1572872 | tf_op jit(solution)/shard_map/ppermute | solution.py:157

commit v3 on v1

--- a/solution.py
+++ b/solution.py
@@ -14,6 +14,16 @@
 TN = (((0,), (0,)), ((), ()))
 GROUP = 4
 PARTS = 3
+TIES = {'xo': (('o', 0), ('sum', 3)), 'ohop': (('back', 2),)}
+LATE = 6
+LATE_TIES = {'xo': (('o', 0), ('sum', 3)), 'ohop': (('back', 2),)}
+OWN_AT = 'xo'
+WGRAD_AT = 'ohop'
+WGRAD_STEP = 7
+GROUPS = (5, 8)
+LAST_PIECES = 1
+BLOCK_COST = 4
+WGRAD_COST = 1
 BLOCK_VMEM = 16 << 20
 WGRAD_VMEM = 24 << 20
 
@@ -50,7 +60,7 @@
         p = jnp.sum(jnp.where(mine, coded, 0.0), axis=1, keepdims=True)
         pre = mm(x, wgu[...], NN)
         gate, up = pre[:, :ff], pre[:, ff:]
-        hid = p * mm(o, wd[...], NT)
+        hid = mm((p * o.astype(F32)).astype(BF16), wd[...], NT)
         sig = jax.nn.sigmoid(gate)
         act = gate * sig
         hidden[...] = (p * (act * up)).astype(BF16)
@@ -72,7 +82,7 @@
         ],
         compiler_params=pltpu.CompilerParams(vmem_limit_bytes=BLOCK_VMEM),
         cost_estimate=pl.CostEstimate(
-            flops=2 * (2 * rows) * width * ff * 5,
+            flops=BLOCK_COST * 2 * (2 * rows) * width * ff * 5,
             bytes_accessed=2 * (6 * rows * width + 3 * width * ff),
             transcendentals=2 * rows * ff,
         ),
@@ -114,7 +124,9 @@
         specs = [pl.BlockSpec(memory_space=pltpu.VMEM)] * len(inputs)
     else:
         inputs = [*xs, *os, *grads, *hiddens]
-        specs = [pl.BlockSpec((rows, chunk), lambda j: (0, j))] * (2 * count)
+        specs = [
+            pl.BlockSpec((v.shape[0], chunk), lambda j: (0, j)) for v in (*xs, *os)
+        ]
         specs += [pl.BlockSpec(v.shape, lambda j: (0, 0)) for v in (*grads, *hiddens)]
     alias = {len(inputs) + i: i for i in range(3)} if has and not last else {}
     return pl.pallas_call(
@@ -130,7 +142,7 @@
         input_output_aliases=alias,
         compiler_params=pltpu.CompilerParams(vmem_limit_bytes=WGRAD_VMEM),
         cost_estimate=pl.CostEstimate(
-            flops=2 * count * rows * width * ff * 3,
+            flops=WGRAD_COST * 2 * count * rows * width * ff * 3,
             bytes_accessed=2 * 2 * count * rows * width + 4 * 3 * width * ff,
             transcendentals=0,
         ),
@@ -165,25 +177,64 @@
     probs = jnp.sum(jnp.where(named, gate_probs[:, :, None], 0.0), axis=1)
     x = jnp.concatenate([tokens, encode(probs)], axis=1)
     o = out_grad
-    wgu = jnp.concatenate([w_gate[0], w_up[0]], axis=1)
     wd = w_down[0]
 
+    def after(v, *others):
+        return lax.optimization_barrier((v, *others))[0] if others else v
+
     acc, total, own = None, None, None
-    held = []
+    sums, backs, xs_seen, os_seen, held = [], [], [], [], []
+
+    def ties_for(name, s):
+        found = []
+        for kind, lag in TIES.get(name, ()) if s < LATE else LATE_TIES.get(name, ()):
+            seen = {"sum": sums, "back": backs, "x": xs_seen, "o": os_seen}[kind]
+            index = s - lag
+            if 0 <= index < len(seen):
+                found.append(seen[index])
+        if name == OWN_AT and s == 1:
+            found.append(backs[0])
+        if resident and acc is not None and name == WGRAD_AT and s == WGRAD_STEP:
+            found.extend(acc)
+        return found
+
     for s in range(chips):
+        pieces = [(x, o)]
         if s:
-            x, o = forward(x), forward(o)
-        xo, oo = other(x), other(o)
-        row_a, row_b, grads, hidden = block_pair(me, devices, x, xo, o, oo, wgu, wd)
-        partial = row_a.astype(F32) + other(row_b).astype(F32)
+            x = after(x, *ties_for("xhop", s))
+            o = after(o, *ties_for("ohop", s))
+            count = LAST_PIECES if s == chips - 1 else 1
+            pieces = [
+                (forward(a), forward(b))
+                for a, b in zip(jnp.split(x, count), jnp.split(o, count))
+            ]
+        x, o = pieces[0]
+        partial = []
+        for k, (x, o) in enumerate(pieces):
+            xs_seen.append(x)
+            os_seen.append(o)
+            xo = other(after(x, *ties_for("xo", s + k)) if s else x)
+            oo = other(after(o, *ties_for("oo", s + k)) if s else o)
+            if s == 0:
+                pair = lax.optimization_barrier((w_gate[0], w_up[0], xo))[:2]
+                wgu = jnp.concatenate(pair, axis=1)
+                o, wgu = lax.optimization_barrier((o, wgu))
+            row_a, row_b, grads, hidden = block_pair(
+                me, devices, x, xo, o, after(oo, *ties_for("block", s + k)), wgu, wd
+            )
+            backs.append(row_b)
+            partial.append(row_a.astype(F32) + other(row_b).astype(F32))
+            held.append((x, xo, o, oo, grads, hidden))
         if s == 0:
-            own = partial
+            own = partial[0]
         else:
             if total is not None:
-                partial = forward(total).astype(F32) + partial
-            total = partial.astype(BF16)
-        held.append((x, xo, o, oo, grads, hidden))
-        if len(held) == GROUP or s == chips - 1:
+                came = forward(after(total, *ties_for("rs", s))).astype(F32)
+                parts = jnp.split(came, len(partial))
+                partial = [a + b for a, b in zip(parts, partial)]
+            total = partial[0].astype(BF16)
+            sums.append(total)
+        if (s + 1 in GROUPS) if resident else (len(held) >= GROUP or s == chips - 1):
             acc = wgrad_group(
                 [v for h in held for v in h[:2]],
                 [v for h in held for v in h[2:4]],
@@ -196,7 +247,8 @@
             held = []
             if not resident:
                 x, o, acc = lax.optimization_barrier((x, o, acc))
-    total = forward(total).astype(F32) + own if chips > 1 else own
+    total = [forward(p.astype(BF16)) for p in partial]
+    total = jnp.concatenate(total, axis=0).astype(F32) + own
     gate_wgrad, up_wgrad, down_wgrad = acc
     return (
         total.astype(BF16),

time: 153 us -> 137 us (0.90)
  waiting for transfers between devices: 63.8 us -> 46.1 us
  starting transfers between devices: 45.4 us -> 47.6 us
    ppermute x21, waiting for transfers between devices: 63.7 us -> 46.1 us  [forward(): return lax.ppermute(v, 'expert', hop)]
  transfers between devices with their start and end apart: 45 -> 45, of which waited for: 14 -> 16; matrix products, arithmetic and copies ran while one was open for 3% -> 3% of each run, Pallas kernels for 23% -> 26%
where the time goes in v3:
time: 137 us
  starting transfers between devices  47.6 us (35%)
  waiting for transfers between devices  46.1 us (34%)
  Pallas kernels  35.2 us (26%)
  other arithmetic  6.72 us (5%)
    ppermute x21, waiting for transfers between devices, forward(): return lax.ppermute(v, 'expert', hop)  46.1 us
    ppermute x21, starting transfers between devices, forward(): return lax.ppermute(v, 'expert', hop)  42.2 us
    pallas_call x8, Pallas kernels, block_pair(): pl.pallas_call(body, in_specs=[pl.BlockSpec(memory_space=pltpu.SMEM)] + [...  22.2 us
    pallas_call x2, Pallas kernels, wgrad_group(): pl.pallas_call(body, grid=(width // chunk,), in_specs=specs + (acc_specs...  13 us
    ppermute x24, starting transfers between devices, other(): return lax.ppermute(v, 'expert', swap)  5.39 us
  transfers between devices with their start and end apart: 45, of which 16 were waited for; matrix products, arithmetic and copies ran while one was open for 3% of the time, Pallas kernels for 26%

profile of v3, /device:TPU:0, one launch (start us, length us, event | category | flops | bytes accessed | tf_op | source)
XLA Modules:
  0.0 136.7 jit_solution(16658716418348528990)
XLA Ops:
  0.6 0.7 select_reduce_fusion
  1.5 1.1 fusion.1.xa.refs_0_
  2.6 0.5 collective-permute-start.1
  3.1 2.6 %collective-permute-start = (bf16[128,2176]{1,0:T(8,128)(2,1)S(1)}, bf16[128,2176]{1,0:T(8,128)(2,1)S(1)}, u32[]{:S(2)}, u32[]{:S(2)}) collective-permute-start(bf16[128,2176]{1,0:T(8,128)(2,1)S(1)} %fusion.1.xa.refs_0_), channel_id=1, source_target_pairs={{0,4},{4,8},{8,12},{12,14},{14,10},{10,6},{6,2},{2,0},{5,1},{9,5},... | collective-permute-start | bytes 1671176 | tf_op jit(solution)/shard_map/ppermute | solution.py:169
  5.9 2.3 %pad_maximum_fusion.wgu = bf16[2048,768]{1,0:T(8,128)(2,1)S(1)} fusion(bf16[2048,384]{1,0:T(8,128)(2,1)} %bitcast.15, bf16[2048,384]{1,0:T(8,128)(2,1)} %bitcast.16), kind=kLoop, calls=%fused_computation | loop fusion | flops 6291456 | bytes 6291456 | tf_op jit(solution)/shard_map/concatenate | solution.py:220
  8.2 1.8 %collective-permute-start.2 = (bf16[128,2048]{1,0:T(8,128)(2,1)S(1)}, bf16[128,2048]{1,0:T(8,128)(2,1)S(1)}, u32[]{:S(2)}, u32[]{:S(2)}) collective-permute-start(bf16[128,2048]{1,0:T(8,128)(2,1)S(1)} %copy-done.1), channel_id=1, source_target_pairs={{0,4},{4,8},{8,12},{12,14},{14,10},{10,6},{6,2},{2,0},{5,1},{9,5},... | collective-permute-start | bytes 1572872 | tf_op jit(solution)/shard_map/ppermute | solution.py:169
  10.0 3.2 %collective-permute-done.xa.refs_2_ = bf16[128,2176]{1,0:T(8,128)(2,1)S(1)} collective-permute-done((bf16[128,2176]{1,0:T(8,128)(2,1)S(1)}, bf16[128,2176]{1,0:T(8,128)(2,1)S(1)}, u32[]{:S(2)}, u32[]{:S(2)}) %collective-permute-start) | collective-permute-done | bytes 557088 | tf_op jit(solution)/shard_map/ppermute | solution.py:169
  13.2 2.1 %collective-permute-start.8 = (bf16[128,2176]{1,0:T(8,128)(2,1)S(1)}, bf16[128,2176]{1,0:T(8,128)(2,1)S(1)}, u32[]{:S(2)}, u32[]{:S(2)}) collective-permute-start(bf16[128,2176]{1,0:T(8,128)(2,1)S(1)} %collective-permute-done.xa.refs_2_), channel_id=1, source_target_pairs={{0,4},{4,8},{8,12},{12,14},{14,10},{10,6},{6,2},{2,0},{5,1},{9,5},... | collective-permute-start | bytes 1671176 | tf_op jit(solution)/shard_map/ppermute | solution.py:169
  15.3 2.8 %block_pair.8 = (bf16[128,2048]{1,0:T(8,128)(2,1)S(1)}, bf16[128,2048]{1,0:T(8,128)(2,1)S(1)}, bf16[256,768]{1,0:T(8,128)(2,1)S(1)}, bf16[256,384]{1,0:T(8,128)(2,1)S(1)}) custom-call(s32[1]{0:T(128)} %bitcast.me, bf16[128,2176]{1,0:T(8,128)(2,1)S(1)} %fusion.1.xa.refs_0_, bf16[128,2176]{1,0:T(8,128)(2,1)S(1)} %collective-permute-done.1.xb.refs_1_, ...), custom_call_target="tpu_custom_call" | custom-call | flops 8053063680 | bytes 7864320 | tf_op jit(solution)/shard_map/block_pair/pallas_call | solution.py:73
  18.1 0.8 collective-permute-done.2.oa.refs_12_
  18.8 0.5 collective-permute-start.5
  19.3 2.1 %collective-permute-start.9 = (bf16[128,2048]{1,0:T(8,128)(2,1)S(1)}, bf16[128,2048]{1,0:T(8,128)(2,1)S(1)}, u32[]{:S(2)}, u32[]{:S(2)}) collective-permute-start(bf16[128,2048]{1,0:T(8,128)(2,1)S(1)} %collective-permute-done.2.oa.refs_12_), channel_id=1, source_target_pairs={{0,4},{4,8},{8,12},{12,14},{14,10},{10,6},{6,2},{2,0},{5,1},{9,5},... | collective-permute-start | bytes 1572872 | tf_op jit(solution)/shard_map/ppermute | solution.py:169
  21.4 3.4 %collective-permute-done.8.xa.refs_4_ = bf16[128,2176]{1,0:T(8,128)(2,1)S(1)} collective-permute-done((bf16[128,2176]{1,0:T(8,128)(2,1)S(1)}, bf16[128,2176]{1,0:T(8,128)(2,1)S(1)}, u32[]{:S(2)}, u32[]{:S(2)}) %collective-permute-start.8) | collective-permute-done | bytes 557088 | tf_op jit(solution)/shard_map/ppermute | solution.py:169
  24.8 2.1 %collective-permute-start.14 = (bf16[128,2176]{1,0:T(8,128)(2,1)S(1)}, bf16[128,2176]{1,0:T(8,128)(2,1)S(1)}, u32[]{:S(2)}, u32[]{:S(2)}) collective-permute-start(bf16[128,2176]{1,0:T(8,128)(2,1)S(1)} %collective-permute-done.8.xa.refs_4_), channel_id=1, source_target_pairs={{0,4},{4,8},{8,12},{12,14},{14,10},{10,6},{6,2},{2,0},{5,1},{9,5},... | collective-permute-start | bytes 1671176 | tf_op jit(solution)/shard_map/ppermute | solution.py:169
  26.9 2.8 %block_pair.9 = (bf16[128,2048]{1,0:T(8,128)(2,1)S(1)}, bf16[128,2048]{1,0:T(8,128)(2,1)S(1)}, bf16[256,768]{1,0:T(8,128)(2,1)S(1)}, bf16[256,384]{1,0:T(8,128)(2,1)S(1)}) custom-call(s32[1]{0:T(128)} %bitcast.me, bf16[128,2176]{1,0:T(8,128)(2,1)S(1)} %collective-permute-done.xa.refs_2_, bf16[128,2176]{1,0:T(8,128)(2,1)S(1)} %collective-permute-done.4.xb.refs_3_, ...), custom_call_target="tpu_custom_call" | custom-call | flops 8053063680 | bytes 7864320 | tf_op jit(solution)/shard_map/block_pair/pallas_call | solution.py:73
  29.7 0.7 collective-permute-done.9.oa.refs_14_
  30.4 0.5 collective-permute-start.11
  30.9 2.1 %collective-permute-start.15 = (bf16[128,2048]{1,0:T(8,128)(2,1)S(1)}, bf16[128,2048]{1,0:T(8,128)(2,1)S(1)}, u32[]{:S(2)}, u32[]{:S(2)}) collective-permute-start(bf16[128,2048]{1,0:T(8,128)(2,1)S(1)} %collective-permute-done.9.oa.refs_14_), channel_id=1, source_target_pairs={{0,4},{4,8},{8,12},{12,14},{14,10},{10,6},{6,2},{2,0},{5,1},{9,5},... | collective-permute-start | bytes 1572872 | tf_op jit(solution)/shard_map/ppermute | solution.py:169
  33.0 3.4 %collective-permute-done.14.xa.refs_6_ = bf16[128,2176]{1,0:T(8,128)(2,1)S(1)} collective-permute-done((bf16[128,2176]{1,0:T(8,128)(2,1)S(1)}, bf16[128,2176]{1,0:T(8,128)(2,1)S(1)}, u32[]{:S(2)}, u32[]{:S(2)}) %collective-permute-start.14) | collective-permute-done | bytes 557088 | tf_op jit(solution)/shard_map/ppermute | solution.py:169
  36.4 2.1 %collective-permute-start.20 = (bf16[128,2176]{1,0:T(8,128)(2,1)S(1)}, bf16[128,2176]{1,0:T(8,128)(2,1)S(1)}, u32[]{:S(2)}, u32[]{:S(2)}) collective-permute-start(bf16[128,2176]{1,0:T(8,128)(2,1)S(1)} %collective-permute-done.14.xa.refs_6_), channel_id=1, source_target_pairs={{0,4},{4,8},{8,12},{12,14},{14,10},{10,6},{6,2},{2,0},{5,1},{9,5},... | collective-permute-start | bytes 1671176 | tf_op jit(solution)/shard_map/ppermute | solution.py:169
  38.6 1.6 %collective-permute-start.7 = (bf16[128,2048]{1,0:T(8,128)(2,1)S(1)}, bf16[128,2048]{1,0:T(8,128)(2,1)S(1)}, u32[]{:S(2)}, u32[]{:S(2)}) collective-permute-start(bf16[128,2048]{1,0:T(8,128)(2,1)S(1)} %add_convert_fusion.7), channel_id=1, source_target_pairs={{0,4},{4,8},{8,12},{12,14},{14,10},{10,6},{6,2},{2,0},{5,1},{9,5},... | collective-permute-start | bytes 1572872 | tf_op jit(solution)/shard_map/ppermute | solution.py:169
  40.2 2.8 %block_pair.10 = (bf16[128,2048]{1,0:T(8,128)(2,1)S(1)}, bf16[128,2048]{1,0:T(8,128)(2,1)S(1)}, bf16[256,768]{1,0:T(8,128)(2,1)S(1)}, bf16[256,384]{1,0:T(8,128)(2,1)S(1)}) custom-call(s32[1]{0:T(128)} %bitcast.me, bf16[128,2176]{1,0:T(8,128)(2,1)S(1)} %collective-permute-done.8.xa.refs_4_, bf16[128,2176]{1,0:T(8,128)(2,1)S(1)} %collective-permute-done.10.xb.refs_5_, ...), custom_call_target="tpu_custom_call" | custom-call | flops 8053063680 | bytes 7864320 | tf_op jit(solution)/shard_map/block_pair/pallas_call | solution.py:73
  43.1 0.5 collective-permute-start.16
  43.7 4.3 %collective-permute-done.20.xa.refs_8_ = bf16[128,2176]{1,0:T(8,128)(2,1)S(1)} collective-permute-done((bf16[128,2176]{1,0:T(8,128)(2,1)S(1)}, bf16[128,2176]{1,0:T(8,128)(2,1)S(1)}, u32[]{:S(2)}, u32[]{:S(2)}) %collective-permute-start.20) | collective-permute-done | bytes 557088 | tf_op jit(solution)/shard_map/ppermute | solution.py:169
  48.0 2.1 %collective-permute-start.21 = (bf16[128,2048]{1,0:T(8,128)(2,1)S(1)}, bf16[128,2048]{1,0:T(8,128)(2,1)S(1)}, u32[]{:S(2)}, u32[]{:S(2)}) collective-permute-start(bf16[128,2048]{1,0:T(8,128)(2,1)S(1)} %collective-permute-done.15.oa.refs_16_), channel_id=1, source_target_pairs={{0,4},{4,8},{8,12},{12,14},{14,10},{10,6},{6,2},{2,0},{5,1},{9,5},... | collective-permute-start | bytes 1572872 | tf_op jit(solution)/shard_map/ppermute | solution.py:169
  50.0 3.5 %collective-permute-done.7 = bf16[128,2048]{1,0:T(8,128)(2,1)S(1)} collective-permute-done((bf16[128,2048]{1,0:T(8,128)(2,1)S(1)}, bf16[128,2048]{1,0:T(8,128)(2,1)S(1)}, u32[]{:S(2)}, u32[]{:S(2)}) %collective-permute-start.7) | collective-permute-done | bytes 524320 | tf_op jit(solution)/shard_map/ppermute | solution.py:169
  53.6 2.1 %collective-permute-start.26 = (bf16[128,2176]{1,0:T(8,128)(2,1)S(1)}, bf16[128,2176]{1,0:T(8,128)(2,1)S(1)}, u32[]{:S(2)}, u32[]{:S(2)}) collective-permute-start(bf16[128,2176]{1,0:T(8,128)(2,1)S(1)} %collective-permute-done.20.xa.refs_8_), channel_id=1, source_target_pairs={{0,4},{4,8},{8,12},{12,14},{14,10},{10,6},{6,2},{2,0},{5,1},{9,5},... | collective-permute-start | bytes 1671176 | tf_op jit(solution)/shard_map/ppermute | solution.py:169
  55.7 0.2 add_convert_fusion.6
  55.9 1.6 %collective-permute-start.13 = (bf16[128,2048]{1,0:T(8,128)(2,1)S(1)}, bf16[128,2048]{1,0:T(8,128)(2,1)S(1)}, u32[]{:S(2)}, u32[]{:S(2)}) collective-permute-start(bf16[128,2048]{1,0:T(8,128)(2,1)S(1)} %add_convert_fusion.6), channel_id=1, source_target_pairs={{0,4},{4,8},{8,12},{12,14},{14,10},{10,6},{6,2},{2,0},{5,1},{9,5},... | collective-permute-start | bytes 1572872 | tf_op jit(solution)/shard_map/ppermute | solution.py:169
  57.5 2.8 %block_pair.11 = (bf16[128,2048]{1,0:T(8,128)(2,1)S(1)}, bf16[128,2048]{1,0:T(8,128)(2,1)S(1)}, bf16[256,768]{1,0:T(8,128)(2,1)S(1)}, bf16[256,384]{1,0:T(8,128)(2,1)S(1)}) custom-call(s32[1]{0:T(128)} %bitcast.me, bf16[128,2176]{1,0:T(8,128)(2,1)S(1)} %collective-permute-done.14.xa.refs_6_, bf16[128,2176]{1,0:T(8,128)(2,1)S(1)} %collective-permute-done.16.xb.refs_7_, ...), custom_call_target="tpu_custom_call" | custom-call | flops 8053063680 | bytes 7864320 | tf_op jit(solution)/shard_map/block_pair/pallas_call | solution.py:73
  60.4 0.5 collective-permute-start.22
  60.9 1.6 %collective-permute-start.27 = (bf16[128,2048]{1,0:T(8,128)(2,1)S(1)}, bf16[128,2048]{1,0:T(8,128)(2,1)S(1)}, u32[]{:S(2)}, u32[]{:S(2)}) collective-permute-start(bf16[128,2048]{1,0:T(8,128)(2,1)S(1)} %collective-permute-done.21.oa.refs_18_), channel_id=1, source_target_pairs={{0,4},{4,8},{8,12},{12,14},{14,10},{10,6},{6,2},{2,0},{5,1},{9,5},... | collective-permute-start | bytes 1572872 | tf_op jit(solution)/shard_map/ppermute | solution.py:169
  62.5 2.7 %collective-permute-done.26.xa.refs_0_ = bf16[128,2176]{1,0:T(8,128)(2,1)S(1)} collective-permute-done((bf16[128,2176]{1,0:T(8,128)(2,1)S(1)}, bf16[128,2176]{1,0:T(8,128)(2,1)S(1)}, u32[]{:S(2)}, u32[]{:S(2)}) %collective-permute-start.26) | collective-permute-done | bytes 557088 | tf_op jit(solution)/shard_map/ppermute | solution.py:169
  65.2 5.6 %collective-permute-done.13 = bf16[128,2048]{1,0:T(8,128)(2,1)S(1)} collective-permute-done((bf16[128,2048]{1,0:T(8,128)(2,1)S(1)}, bf16[128,2048]{1,0:T(8,128)(2,1)S(1)}, u32[]{:S(2)}, u32[]{:S(2)}) %collective-permute-start.13) | collective-permute-done | bytes 524320 | tf_op jit(solution)/shard_map/ppermute | solution.py:169
  70.8 2.1 %collective-permute-start.32 = (bf16[128,2176]{1,0:T(8,128)(2,1)S(1)}, bf16[128,2176]{1,0:T(8,128)(2,1)S(1)}, u32[]{:S(2)}, u32[]{:S(2)}) collective-permute-start(bf16[128,2176]{1,0:T(8,128)(2,1)S(1)} %collective-permute-done.26.xa.refs_0_), channel_id=1, source_target_pairs={{0,4},{4,8},{8,12},{12,14},{14,10},{10,6},{6,2},{2,0},{5,1},{9,5},... | collective-permute-start | bytes 1671176 | tf_op jit(solution)/shard_map/ppermute | solution.py:169
  72.9 0.2 add_convert_fusion.5
  73.1 1.8 %collective-permute-start.19 = (bf16[128,2048]{1,0:T(8,128)(2,1)S(1)}, bf16[128,2048]{1,0:T(8,128)(2,1)S(1)}, u32[]{:S(2)}, u32[]{:S(2)}) collective-permute-start(bf16[128,2048]{1,0:T(8,128)(2,1)S(1)} %add_convert_fusion.5), channel_id=1, source_target_pairs={{0,4},{4,8},{8,12},{12,14},{14,10},{10,6},{6,2},{2,0},{5,1},{9,5},... | collective-permute-start | bytes 1572872 | tf_op jit(solution)/shard_map/ppermute | solution.py:169
  74.9 1.5 %collective-permute-done.27.oa.refs_6_ = bf16[128,2048]{1,0:T(8,128)(2,1)S(1)} collective-permute-done((bf16[128,2048]{1,0:T(8,128)(2,1)S(1)}, bf16[128,2048]{1,0:T(8,128)(2,1)S(1)}, u32[]{:S(2)}, u32[]{:S(2)}) %collective-permute-start.27) | collective-permute-done | bytes 524320 | tf_op jit(solution)/shard_map/ppermute | solution.py:169
  76.4 2.8 %block_pair.12 = (bf16[128,2048]{1,0:T(8,128)(2,1)S(1)}, bf16[128,2048]{1,0:T(8,128)(2,1)S(1)}, bf16[256,768]{1,0:T(8,128)(2,1)S(1)}, bf16[256,384]{1,0:T(8,128)(2,1)S(1)}) custom-call(s32[1]{0:T(128)} %bitcast.me, bf16[128,2176]{1,0:T(8,128)(2,1)S(1)} %collective-permute-done.20.xa.refs_8_, bf16[128,2176]{1,0:T(8,128)(2,1)S(1)} %collective-permute-done.22.xb.refs_9_, ...), custom_call_target="tpu_custom_call" | custom-call | flops 8053063680 | bytes 7864320 | tf_op jit(solution)/shard_map/block_pair/pallas_call | solution.py:73
  79.2 0.6 collective-permute-start.24
  79.8 2.1 %collective-permute-start.33 = (bf16[128,2048]{1,0:T(8,128)(2,1)S(1)}, bf16[128,2048]{1,0:T(8,128)(2,1)S(1)}, u32[]{:S(2)}, u32[]{:S(2)}) collective-permute-start(bf16[128,2048]{1,0:T(8,128)(2,1)S(1)} %collective-permute-done.27.oa.refs_6_), channel_id=1, source_target_pairs={{0,4},{4,8},{8,12},{12,14},{14,10},{10,6},{6,2},{2,0},{5,1},{9,5},... | collective-permute-start | bytes 1572872 | tf_op jit(solution)/shard_map/ppermute | solution.py:169
  81.8 0.5 collective-permute-done.32.xa.refs_2_
  82.4 7.2 %wgrad_group.2 = (f32[2048,384]{1,0:T(8,128)S(1)}, f32[2048,384]{1,0:T(8,128)S(1)}, f32[384,2048]{1,0:T(8,128)S(1)}) custom-call(bf16[128,2176]{1,0:T(8,128)(2,1)S(1)} %fusion.1.xa.refs_0_, bf16[128,2176]{1,0:T(8,128)(2,1)S(1)} %collective-permute-done.1.xb.refs_1_, bf16[128,2176]{1,0:T(8,128)(2,1)S(1)} %collective-permute-done.xa.refs_2_, ...), custom_call_target="tpu_custom_call" | custom-call | flops 6039797760 | bytes 19922944 | tf_op jit(solution)/shard_map/wgrad_group/pallas_call | solution.py:132
  89.6 2.1 %collective-permute-start.38 = (bf16[128,2176]{1,0:T(8,128)(2,1)S(1)}, bf16[128,2176]{1,0:T(8,128)(2,1)S(1)}, u32[]{:S(2)}, u32[]{:S(2)}) collective-permute-start(bf16[128,2176]{1,0:T(8,128)(2,1)S(1)} %collective-permute-done.32.xa.refs_2_), channel_id=1, source_target_pairs={{0,4},{4,8},{8,12},{12,14},{14,10},{10,6},{6,2},{2,0},{5,1},{9,5},... | collective-permute-start | bytes 1671176 | tf_op jit(solution)/shard_map/ppermute | solution.py:169
  91.7 0.2 add_convert_fusion.4
  92.0 1.6 %collective-permute-start.25 = (bf16[128,2048]{1,0:T(8,128)(2,1)S(1)}, bf16[128,2048]{1,0:T(8,128)(2,1)S(1)}, u32[]{:S(2)}, u32[]{:S(2)}) collective-permute-start(bf16[128,2048]{1,0:T(8,128)(2,1)S(1)} %add_convert_fusion.4), channel_id=1, source_target_pairs={{0,4},{4,8},{8,12},{12,14},{14,10},{10,6},{6,2},{2,0},{5,1},{9,5},... | collective-permute-start | bytes 1572872 | tf_op jit(solution)/shard_map/ppermute | solution.py:169
  93.6 0.5 collective-permute-start.35
  94.1 2.8 %block_pair.13 = (bf16[128,2048]{1,0:T(8,128)(2,1)S(1)}, bf16[128,2048]{1,0:T(8,128)(2,1)S(1)}, bf16[256,768]{1,0:T(8,128)(2,1)S(1)}, bf16[256,384]{1,0:T(8,128)(2,1)S(1)}) custom-call(s32[1]{0:T(128)} %bitcast.me, bf16[128,2176]{1,0:T(8,128)(2,1)S(1)} %collective-permute-done.26.xa.refs_0_, bf16[128,2176]{1,0:T(8,128)(2,1)S(1)} %collective-permute-done.28.xb.refs_1_, ...), custom_call_target="tpu_custom_call" | custom-call | flops 8053063680 | bytes 7864320 | tf_op jit(solution)/shard_map/block_pair/pallas_call | solution.py:73
  97.1 2.1 %collective-permute-start.39 = (bf16[128,2048]{1,0:T(8,128)(2,1)S(1)}, bf16[128,2048]{1,0:T(8,128)(2,1)S(1)}, u32[]{:S(2)}, u32[]{:S(2)}) collective-permute-start(bf16[128,2048]{1,0:T(8,128)(2,1)S(1)} %collective-permute-done.33.oa.refs_8_), channel_id=1, source_target_pairs={{0,4},{4,8},{8,12},{12,14},{14,10},{10,6},{6,2},{2,0},{5,1},{9,5},... | collective-permute-start | bytes 1572872 | tf_op jit(solution)/shard_map/ppermute | solution.py:169
  99.1 2.8 %block_pair.14 = (bf16[128,2048]{1,0:T(8,128)(2,1)S(1)}, bf16[128,2048]{1,0:T(8,128)(2,1)S(1)}, bf16[256,768]{1,0:T(8,128)(2,1)S(1)}, bf16[256,384]{1,0:T(8,128)(2,1)S(1)}) custom-call(s32[1]{0:T(128)} %bitcast.me, bf16[128,2176]{1,0:T(8,128)(2,1)S(1)} %collective-permute-done.32.xa.refs_2_, bf16[128,2176]{1,0:T(8,128)(2,1)S(1)} %collective-permute-done.34.xb.refs_3_, ...), custom_call_target="tpu_custom_call" | custom-call | flops 8053063680 | bytes 7864320 | tf_op jit(solution)/shard_map/block_pair/pallas_call | solution.py:73
  102.1 3.1 %collective-permute-done.25 = bf16[128,2048]{1,0:T(8,128)(2,1)S(1)} collective-permute-done((bf16[128,2048]{1,0:T(8,128)(2,1)S(1)}, bf16[128,2048]{1,0:T(8,128)(2,1)S(1)}, u32[]{:S(2)}, u32[]{:S(2)}) %collective-permute-start.25) | collective-permute-done | bytes 524320 | tf_op jit(solution)/shard_map/ppermute | solution.py:169
  105.4 2.1 %collective-permute-start.31 = (bf16[128,2048]{1,0:T(8,128)(2,1)S(1)}, bf16[128,2048]{1,0:T(8,128)(2,1)S(1)}, u32[]{:S(2)}, u32[]{:S(2)}) collective-permute-start(bf16[128,2048]{1,0:T(8,128)(2,1)S(1)} %add_convert_fusion.3), channel_id=1, source_target_pairs={{0,4},{4,8},{8,12},{12,14},{14,10},{10,6},{6,2},{2,0},{5,1},{9,5},... | collective-permute-start | bytes 1572872 | tf_op jit(solution)/shard_map/ppermute | solution.py:169
  107.6 3.2 %collective-permute-done.39.oa.refs_10_ = bf16[128,2048]{1,0:T(8,128)(2,1)S(1)} collective-permute-done((bf16[128,2048]{1,0:T(8,128)(2,1)S(1)}, bf16[128,2048]{1,0:T(8,128)(2,1)S(1)}, u32[]{:S(2)}, u32[]{:S(2)}) %collective-permute-start.39) | collective-permute-done | bytes 524320 | tf_op jit(solution)/shard_map/ppermute | solution.py:169
  110.8 0.5 collective-permute-start.41
  111.3 5.1 %collective-permute-done.31 = bf16[128,2048]{1,0:T(8,128)(2,1)S(1)} collective-permute-done((bf16[128,2048]{1,0:T(8,128)(2,1)S(1)}, bf16[128,2048]{1,0:T(8,128)(2,1)S(1)}, u32[]{:S(2)}, u32[]{:S(2)}) %collective-permute-start.31) | collective-permute-done | bytes 524320 | tf_op jit(solution)/shard_map/ppermute | solution.py:169
  116.7 2.3 %collective-permute-start.37 = (bf16[128,2048]{1,0:T(8,128)(2,1)S(1)}, bf16[128,2048]{1,0:T(8,128)(2,1)S(1)}, u32[]{:S(2)}, u32[]{:S(2)}) collective-permute-start(bf16[128,2048]{1,0:T(8,128)(2,1)S(1)} %add_convert_fusion.2), channel_id=1, source_target_pairs={{0,4},{4,8},{8,12},{12,14},{14,10},{10,6},{6,2},{2,0},{5,1},{9,5},... | collective-permute-start | bytes 1572872 | tf_op jit(solution)/shard_map/ppermute | solution.py:169
  119.0 2.8 %block_pair.15 = (bf16[128,2048]{1,0:T(8,128)(2,1)S(1)}, bf16[128,2048]{1,0:T(8,128)(2,1)S(1)}, bf16[256,768]{1,0:T(8,128)(2,1)S(1)}, bf16[256,384]{1,0:T(8,128)(2,1)S(1)}) custom-call(s32[1]{0:T(128)} %bitcast.me, bf16[128,2176]{1,0:T(8,128)(2,1)S(1)} %collective-permute-done.38.xa.refs_4_, bf16[128,2176]{1,0:T(8,128)(2,1)S(1)} %collective-permute-done.40.xb.refs_5_, ...), custom_call_target="tpu_custom_call" | custom-call | flops 8053063680 | bytes 7864320 | tf_op jit(solution)/shard_map/block_pair/pallas_call | solution.py:73
  121.9 0.5 collective-permute-start.44
  122.4 3.7 %collective-permute-done.37 = bf16[128,2048]{1,0:T(8,128)(2,1)S(1)} collective-permute-done((bf16[128,2048]{1,0:T(8,128)(2,1)S(1)}, bf16[128,2048]{1,0:T(8,128)(2,1)S(1)}, u32[]{:S(2)}, u32[]{:S(2)}) %collective-permute-start.37) | collective-permute-done | bytes 524320 | tf_op jit(solution)/shard_map/ppermute | solution.py:169
  126.1 0.2 add_convert_fusion.1
  126.4 2.1 %collective-permute-start.43 = (bf16[128,2048]{1,0:T(8,128)(2,1)S(1)}, bf16[128,2048]{1,0:T(8,128)(2,1)S(1)}, u32[]{:S(2)}, u32[]{:S(2)}) collective-permute-start(bf16[128,2048]{1,0:T(8,128)(2,1)S(1)} %add_convert_fusion.1), channel_id=1, source_target_pairs={{0,4},{4,8},{8,12},{12,14},{14,10},{10,6},{6,2},{2,0},{5,1},{9,5},... | collective-permute-start | bytes 1572872 | tf_op jit(solution)/shard_map/ppermute | solution.py:169
  128.5 5.8 %wgrad_group.3 = (bf16[2048,384]{1,0:T(8,128)(2,1)}, bf16[2048,384]{1,0:T(8,128)(2,1)}, bf16[384,2048]{1,0:T(8,128)(2,1)}) custom-call(bf16[128,2176]{1,0:T(8,128)(2,1)S(1)} %collective-permute-done.26.xa.refs_0_, bf16[128,2176]{1,0:T(8,128)(2,1)S(1)} %collective-permute-done.28.xb.refs_1_, bf16[128,2176]{1,0:T(8,128)(2,1)S(1)} %collective-permute-done.32.xa.refs_2_, ...), custom_call_target="tpu_custom_call" | custom-call | flops 3623878656 | bytes 15728640 | tf_op jit(solution)/shard_map/wgrad_group/pallas_call | solution.py:132
  134.3 1.3 collective-permute-done.43
  135.6 1.0 add_convert_fusion
  (54 shorter events, 1.6 us)
Async XLA Ops:
  2.6 3.3 %collective-permute-start.1 = (bf16[128,2176]{1,0:T(8,128)(2,1)S(1)}, bf16[128,2176]{1,0:T(8,128)(2,1)S(1)}, u32[]{:S(2)}, u32[]{:S(2)}) collective-permute-start(bf16[128,2176]{1,0:T(8,128)(2,1)S(1)} %fusion.1.xa.refs_0_), channel_id=1, source_target_pairs={{0,1},{1,0},{2,3},{3,2},{4,5},{5,4},{6,7},{7,6},{8,9},{9,8},{10,11... | collective-permute-start | bytes 1671176 | tf_op jit(solution)/shard_map/ppermute | solution.py:172
  3.1 10.1 %collective-permute-start = (bf16[128,2176]{1,0:T(8,128)(2,1)S(1)}, bf16[128,2176]{1,0:T(8,128)(2,1)S(1)}, u32[]{:S(2)}, u32[]{:S(2)}) collective-permute-start(bf16[128,2176]{1,0:T(8,128)(2,1)S(1)} %fusion.1.xa.refs_0_), channel_id=1, source_target_pairs={{0,4},{4,8},{8,12},{12,14},{14,10},{10,6},{6,2},{2,0},{5,1},{9,5},... | collective-permute-start | bytes 1671176 | tf_op jit(solution)/shard_map/ppermute | solution.py:169
  5.7 9.5 %collective-permute-start.3 = (bf16[128,2048]{1,0:T(8,128)(2,1)}, bf16[128,2048]{1,0:T(8,128)(2,1)S(1)}, u32[]{:S(2)}, u32[]{:S(2)}) collective-permute-start(bf16[128,2048]{1,0:T(8,128)(2,1)} %refs_10_), channel_id=1, source_target_pairs={{0,1},{1,0},{2,3},{3,2},{4,5},{5,4},{6,7},{7,6},{8,9},{9,8},{10,11... | collective-permute-start | bytes 1572872 | tf_op jit(solution)/shard_map/ppermute | solution.py:172
  5.9 2.3 %copy-start.1 = (bf16[128,2048]{1,0:T(8,128)(2,1)S(1)}, bf16[128,2048]{1,0:T(8,128)(2,1)}, u32[]{:S(2)}) copy-start(bf16[128,2048]{1,0:T(8,128)(2,1)} %refs_10_) | copy-start | bytes 1572868
  5.9 9.4 %copy-start = (bf16[1,384,2048]{2,1,0:T(8,128)(2,1)S(1)}, bf16[1,384,2048]{2,1,0:T(8,128)(2,1)}, u32[]{:S(2)}) copy-start(bf16[1,384,2048]{2,1,0:T(8,128)(2,1)} %param.13) | copy-start | bytes 4718596
  8.2 10.7 %collective-permute-start.2 = (bf16[128,2048]{1,0:T(8,128)(2,1)S(1)}, bf16[128,2048]{1,0:T(8,128)(2,1)S(1)}, u32[]{:S(2)}, u32[]{:S(2)}) collective-permute-start(bf16[128,2048]{1,0:T(8,128)(2,1)S(1)} %copy-done.1), channel_id=1, source_target_pairs={{0,4},{4,8},{8,12},{12,14},{14,10},{10,6},{6,2},{2,0},{5,1},{9,5},... | collective-permute-start | bytes 1572872 | tf_op jit(solution)/shard_map/ppermute | solution.py:169
  13.2 11.6 %collective-permute-start.8 = (bf16[128,2176]{1,0:T(8,128)(2,1)S(1)}, bf16[128,2176]{1,0:T(8,128)(2,1)S(1)}, u32[]{:S(2)}, u32[]{:S(2)}) collective-permute-start(bf16[128,2176]{1,0:T(8,128)(2,1)S(1)} %collective-permute-done.xa.refs_2_), channel_id=1, source_target_pairs={{0,4},{4,8},{8,12},{12,14},{14,10},{10,6},{6,2},{2,0},{5,1},{9,5},... | collective-permute-start | bytes 1671176 | tf_op jit(solution)/shard_map/ppermute | solution.py:169
  18.8 8.1 %collective-permute-start.4 = (bf16[128,2176]{1,0:T(8,128)(2,1)S(1)}, bf16[128,2176]{1,0:T(8,128)(2,1)S(1)}, u32[]{:S(2)}, u32[]{:S(2)}) collective-permute-start(bf16[128,2176]{1,0:T(8,128)(2,1)S(1)} %collective-permute-done.xa.refs_2_), channel_id=1, source_target_pairs={{0,1},{1,0},{2,3},{3,2},{4,5},{5,4},{6,7},{7,6},{8,9},{9,8},{10,11... | collective-permute-start | bytes 1671176 | tf_op jit(solution)/shard_map/ppermute | solution.py:172
  18.8 8.0 %collective-permute-start.5 = (bf16[128,2048]{1,0:T(8,128)(2,1)S(1)}, bf16[128,2048]{1,0:T(8,128)(2,1)S(1)}, u32[]{:S(2)}, u32[]{:S(2)}) collective-permute-start(bf16[128,2048]{1,0:T(8,128)(2,1)S(1)} %collective-permute-done.2.oa.refs_12_), channel_id=1, source_target_pairs={{0,1},{1,0},{2,3},{3,2},{4,5},{5,4},{6,7},{7,6},{8,9},{9,8},{10,11... | collective-permute-start | bytes 1572872 | tf_op jit(solution)/shard_map/ppermute | solution.py:172
  19.3 11.1 %collective-permute-start.9 = (bf16[128,2048]{1,0:T(8,128)(2,1)S(1)}, bf16[128,2048]{1,0:T(8,128)(2,1)S(1)}, u32[]{:S(2)}, u32[]{:S(2)}) collective-permute-start(bf16[128,2048]{1,0:T(8,128)(2,1)S(1)} %collective-permute-done.2.oa.refs_12_), channel_id=1, source_target_pairs={{0,4},{4,8},{8,12},{12,14},{14,10},{10,6},{6,2},{2,0},{5,1},{9,5},... | collective-permute-start | bytes 1572872 | tf_op jit(solution)/shard_map/ppermute | solution.py:169
  24.8 11.6 %collective-permute-start.14 = (bf16[128,2176]{1,0:T(8,128)(2,1)S(1)}, bf16[128,2176]{1,0:T(8,128)(2,1)S(1)}, u32[]{:S(2)}, u32[]{:S(2)}) collective-permute-start(bf16[128,2176]{1,0:T(8,128)(2,1)S(1)} %collective-permute-done.8.xa.refs_4_), channel_id=1, source_target_pairs={{0,4},{4,8},{8,12},{12,14},{14,10},{10,6},{6,2},{2,0},{5,1},{9,5},... | collective-permute-start | bytes 1671176 | tf_op jit(solution)/shard_map/ppermute | solution.py:169
  29.7 8.8 %collective-permute-start.6 = (bf16[128,2048]{1,0:T(8,128)(2,1)S(1)}, bf16[128,2048]{1,0:T(8,128)(2,1)S(1)}, u32[]{:S(2)}, u32[]{:S(2)}) collective-permute-start(bf16[128,2048]{1,0:T(8,128)(2,1)S(1)} %get-tuple-element.66), channel_id=1, source_target_pairs={{0,1},{1,0},{2,3},{3,2},{4,5},{5,4},{6,7},{7,6},{8,9},{9,8},{10,11... | collective-permute-start | bytes 1572872 | tf_op jit(solution)/shard_map/ppermute | solution.py:172
  30.4 9.8 %collective-permute-start.10 = (bf16[128,2176]{1,0:T(8,128)(2,1)S(1)}, bf16[128,2176]{1,0:T(8,128)(2,1)S(1)}, u32[]{:S(2)}, u32[]{:S(2)}) collective-permute-start(bf16[128,2176]{1,0:T(8,128)(2,1)S(1)} %collective-permute-done.8.xa.refs_4_), channel_id=1, source_target_pairs={{0,1},{1,0},{2,3},{3,2},{4,5},{5,4},{6,7},{7,6},{8,9},{9,8},{10,11... | collective-permute-start | bytes 1671176 | tf_op jit(solution)/shard_map/ppermute | solution.py:172
  30.4 9.8 %collective-permute-start.11 = (bf16[128,2048]{1,0:T(8,128)(2,1)S(1)}, bf16[128,2048]{1,0:T(8,128)(2,1)S(1)}, u32[]{:S(2)}, u32[]{:S(2)}) collective-permute-start(bf16[128,2048]{1,0:T(8,128)(2,1)S(1)} %collective-permute-done.9.oa.refs_14_), channel_id=1, source_target_pairs={{0,1},{1,0},{2,3},{3,2},{4,5},{5,4},{6,7},{7,6},{8,9},{9,8},{10,11... | collective-permute-start | bytes 1572872 | tf_op jit(solution)/shard_map/ppermute | solution.py:172
  30.9 12.2 %collective-permute-start.15 = (bf16[128,2048]{1,0:T(8,128)(2,1)S(1)}, bf16[128,2048]{1,0:T(8,128)(2,1)S(1)}, u32[]{:S(2)}, u32[]{:S(2)}) collective-permute-start(bf16[128,2048]{1,0:T(8,128)(2,1)S(1)} %collective-permute-done.9.oa.refs_14_), channel_id=1, source_target_pairs={{0,4},{4,8},{8,12},{12,14},{14,10},{10,6},{6,2},{2,0},{5,1},{9,5},... | collective-permute-start | bytes 1572872 | tf_op jit(solution)/shard_map/ppermute | solution.py:169
  36.4 11.6 %collective-permute-start.20 = (bf16[128,2176]{1,0:T(8,128)(2,1)S(1)}, bf16[128,2176]{1,0:T(8,128)(2,1)S(1)}, u32[]{:S(2)}, u32[]{:S(2)}) collective-permute-start(bf16[128,2176]{1,0:T(8,128)(2,1)S(1)} %collective-permute-done.14.xa.refs_6_), channel_id=1, source_target_pairs={{0,4},{4,8},{8,12},{12,14},{14,10},{10,6},{6,2},{2,0},{5,1},{9,5},... | collective-permute-start | bytes 1671176 | tf_op jit(solution)/shard_map/ppermute | solution.py:169
  38.6 15.0 %collective-permute-start.7 = (bf16[128,2048]{1,0:T(8,128)(2,1)S(1)}, bf16[128,2048]{1,0:T(8,128)(2,1)S(1)}, u32[]{:S(2)}, u32[]{:S(2)}) collective-permute-start(bf16[128,2048]{1,0:T(8,128)(2,1)S(1)} %add_convert_fusion.7), channel_id=1, source_target_pairs={{0,4},{4,8},{8,12},{12,14},{14,10},{10,6},{6,2},{2,0},{5,1},{9,5},... | collective-permute-start | bytes 1572872 | tf_op jit(solution)/shard_map/ppermute | solution.py:169
  43.0 12.7 %collective-permute-start.12 = (bf16[128,2048]{1,0:T(8,128)(2,1)S(1)}, bf16[128,2048]{1,0:T(8,128)(2,1)S(1)}, u32[]{:S(2)}, u32[]{:S(2)}) collective-permute-start(bf16[128,2048]{1,0:T(8,128)(2,1)S(1)} %get-tuple-element.70), channel_id=1, source_target_pairs={{0,1},{1,0},{2,3},{3,2},{4,5},{5,4},{6,7},{7,6},{8,9},{9,8},{10,11... | collective-permute-start | bytes 1572872 | tf_op jit(solution)/shard_map/ppermute | solution.py:172
  43.1 14.5 %collective-permute-start.16 = (bf16[128,2176]{1,0:T(8,128)(2,1)S(1)}, bf16[128,2176]{1,0:T(8,128)(2,1)S(1)}, u32[]{:S(2)}, u32[]{:S(2)}) collective-permute-start(bf16[128,2176]{1,0:T(8,128)(2,1)S(1)} %collective-permute-done.14.xa.refs_6_), channel_id=1, source_target_pairs={{0,1},{1,0},{2,3},{3,2},{4,5},{5,4},{6,7},{7,6},{8,9},{9,8},{10,11... | collective-permute-start | bytes 1671176 | tf_op jit(solution)/shard_map/ppermute | solution.py:172
  43.6 14.0 %collective-permute-start.17 = (bf16[128,2048]{1,0:T(8,128)(2,1)S(1)}, bf16[128,2048]{1,0:T(8,128)(2,1)S(1)}, u32[]{:S(2)}, u32[]{:S(2)}) collective-permute-start(bf16[128,2048]{1,0:T(8,128)(2,1)S(1)} %collective-permute-done.15.oa.refs_16_), channel_id=1, source_target_pairs={{0,1},{1,0},{2,3},{3,2},{4,5},{5,4},{6,7},{7,6},{8,9},{9,8},{10,11... | collective-permute-start | bytes 1572872 | tf_op jit(solution)/shard_map/ppermute | solution.py:172
  48.0 12.4 %collective-permute-start.21 = (bf16[128,2048]{1,0:T(8,128)(2,1)S(1)}, bf16[128,2048]{1,0:T(8,128)(2,1)S(1)}, u32[]{:S(2)}, u32[]{:S(2)}) collective-permute-start(bf16[128,2048]{1,0:T(8,128)(2,1)S(1)} %collective-permute-done.15.oa.refs_16_), channel_id=1, source_target_pairs={{0,4},{4,8},{8,12},{12,14},{14,10},{10,6},{6,2},{2,0},{5,1},{9,5},... | collective-permute-start | bytes 1572872 | tf_op jit(solution)/shard_map/ppermute | solution.py:169
  53.6 11.6 %collective-permute-start.26 = (bf16[128,2176]{1,0:T(8,128)(2,1)S(1)}, bf16[128,2176]{1,0:T(8,128)(2,1)S(1)}, u32[]{:S(2)}, u32[]{:S(2)}) collective-permute-start(bf16[128,2176]{1,0:T(8,128)(2,1)S(1)} %collective-permute-done.20.xa.refs_8_), channel_id=1, source_target_pairs={{0,4},{4,8},{8,12},{12,14},{14,10},{10,6},{6,2},{2,0},{5,1},{9,5},... | collective-permute-start | bytes 1671176 | tf_op jit(solution)/shard_map/ppermute | solution.py:169
  55.9 14.9 %collective-permute-start.13 = (bf16[128,2048]{1,0:T(8,128)(2,1)S(1)}, bf16[128,2048]{1,0:T(8,128)(2,1)S(1)}, u32[]{:S(2)}, u32[]{:S(2)}) collective-permute-start(bf16[128,2048]{1,0:T(8,128)(2,1)S(1)} %add_convert_fusion.6), channel_id=1, source_target_pairs={{0,4},{4,8},{8,12},{12,14},{14,10},{10,6},{6,2},{2,0},{5,1},{9,5},... | collective-permute-start | bytes 1572872 | tf_op jit(solution)/shard_map/ppermute | solution.py:169
  60.3 12.5 %collective-permute-start.18 = (bf16[128,2048]{1,0:T(8,128)(2,1)S(1)}, bf16[128,2048]{1,0:T(8,128)(2,1)S(1)}, u32[]{:S(2)}, u32[]{:S(2)}) collective-permute-start(bf16[128,2048]{1,0:T(8,128)(2,1)S(1)} %get-tuple-element.74), channel_id=1, source_target_pairs={{0,1},{1,0},{2,3},{3,2},{4,5},{5,4},{6,7},{7,6},{8,9},{9,8},{10,11... | collective-permute-start | bytes 1572872 | tf_op jit(solution)/shard_map/ppermute | solution.py:172
  60.4 16.0 %collective-permute-start.22 = (bf16[128,2176]{1,0:T(8,128)(2,1)S(1)}, bf16[128,2176]{1,0:T(8,128)(2,1)S(1)}, u32[]{:S(2)}, u32[]{:S(2)}) collective-permute-start(bf16[128,2176]{1,0:T(8,128)(2,1)S(1)} %collective-permute-done.20.xa.refs_8_), channel_id=1, source_target_pairs={{0,1},{1,0},{2,3},{3,2},{4,5},{5,4},{6,7},{7,6},{8,9},{9,8},{10,11... | collective-permute-start | bytes 1671176 | tf_op jit(solution)/shard_map/ppermute | solution.py:172
  60.9 15.5 %collective-permute-start.27 = (bf16[128,2048]{1,0:T(8,128)(2,1)S(1)}, bf16[128,2048]{1,0:T(8,128)(2,1)S(1)}, u32[]{:S(2)}, u32[]{:S(2)}) collective-permute-start(bf16[128,2048]{1,0:T(8,128)(2,1)S(1)} %collective-permute-done.21.oa.refs_18_), channel_id=1, source_target_pairs={{0,4},{4,8},{8,12},{12,14},{14,10},{10,6},{6,2},{2,0},{5,1},{9,5},... | collective-permute-start | bytes 1572872 | tf_op jit(solution)/shard_map/ppermute | solution.py:169
  65.2 11.2 %collective-permute-start.23 = (bf16[128,2048]{1,0:T(8,128)(2,1)S(1)}, bf16[128,2048]{1,0:T(8,128)(2,1)S(1)}, u32[]{:S(2)}, u32[]{:S(2)}) collective-permute-start(bf16[128,2048]{1,0:T(8,128)(2,1)S(1)} %collective-permute-done.21.oa.refs_18_), channel_id=1, source_target_pairs={{0,1},{1,0},{2,3},{3,2},{4,5},{5,4},{6,7},{7,6},{8,9},{9,8},{10,11... | collective-permute-start | bytes 1572872 | tf_op jit(solution)/shard_map/ppermute | solution.py:172
  70.8 11.6 %collective-permute-start.32 = (bf16[128,2176]{1,0:T(8,128)(2,1)S(1)}, bf16[128,2176]{1,0:T(8,128)(2,1)S(1)}, u32[]{:S(2)}, u32[]{:S(2)}) collective-permute-start(bf16[128,2176]{1,0:T(8,128)(2,1)S(1)} %collective-permute-done.26.xa.refs_0_), channel_id=1, source_target_pairs={{0,4},{4,8},{8,12},{12,14},{14,10},{10,6},{6,2},{2,0},{5,1},{9,5},... | collective-permute-start | bytes 1671176 | tf_op jit(solution)/shard_map/ppermute | solution.py:169
  73.1 16.5 %collective-permute-start.19 = (bf16[128,2048]{1,0:T(8,128)(2,1)S(1)}, bf16[128,2048]{1,0:T(8,128)(2,1)S(1)}, u32[]{:S(2)}, u32[]{:S(2)}) collective-permute-start(bf16[128,2048]{1,0:T(8,128)(2,1)S(1)} %add_convert_fusion.5), channel_id=1, source_target_pairs={{0,4},{4,8},{8,12},{12,14},{14,10},{10,6},{6,2},{2,0},{5,1},{9,5},... | collective-permute-start | bytes 1572872 | tf_op jit(solution)/shard_map/ppermute | solution.py:169
  76.4 17.7 %collective-permute-start.28 = (bf16[128,2176]{1,0:T(8,128)(2,1)S(1)}, bf16[128,2176]{1,0:T(8,128)(2,1)S(1)}, u32[]{:S(2)}, u32[]{:S(2)}) collective-permute-start(bf16[128,2176]{1,0:T(8,128)(2,1)S(1)} %collective-permute-done.26.xa.refs_0_), channel_id=1, source_target_pairs={{0,1},{1,0},{2,3},{3,2},{4,5},{5,4},{6,7},{7,6},{8,9},{9,8},{10,11... | collective-permute-start | bytes 1671176 | tf_op jit(solution)/shard_map/ppermute | solution.py:172
  79.2 12.5 %collective-permute-start.24 = (bf16[128,2048]{1,0:T(8,128)(2,1)S(1)}, bf16[128,2048]{1,0:T(8,128)(2,1)S(1)}, u32[]{:S(2)}, u32[]{:S(2)}) collective-permute-start(bf16[128,2048]{1,0:T(8,128)(2,1)S(1)} %get-tuple-element.78), channel_id=1, source_target_pairs={{0,1},{1,0},{2,3},{3,2},{4,5},{5,4},{6,7},{7,6},{8,9},{9,8},{10,11... | collective-permute-start | bytes 1572872 | tf_op jit(solution)/shard_map/ppermute | solution.py:172
  79.8 13.9 %collective-permute-start.33 = (bf16[128,2048]{1,0:T(8,128)(2,1)S(1)}, bf16[128,2048]{1,0:T(8,128)(2,1)S(1)}, u32[]{:S(2)}, u32[]{:S(2)}) collective-permute-start(bf16[128,2048]{1,0:T(8,128)(2,1)S(1)} %collective-permute-done.27.oa.refs_6_), channel_id=1, source_target_pairs={{0,4},{4,8},{8,12},{12,14},{14,10},{10,6},{6,2},{2,0},{5,1},{9,5},... | collective-permute-start | bytes 1572872 | tf_op jit(solution)/shard_map/ppermute | solution.py:169
  82.4 11.3 %collective-permute-start.29 = (bf16[128,2048]{1,0:T(8,128)(2,1)S(1)}, bf16[128,2048]{1,0:T(8,128)(2,1)S(1)}, u32[]{:S(2)}, u32[]{:S(2)}) collective-permute-start(bf16[128,2048]{1,0:T(8,128)(2,1)S(1)} %collective-permute-done.27.oa.refs_6_), channel_id=1, source_target_pairs={{0,1},{1,0},{2,3},{3,2},{4,5},{5,4},{6,7},{7,6},{8,9},{9,8},{10,11... | collective-permute-start | bytes 1572872 | tf_op jit(solution)/shard_map/ppermute | solution.py:172
  89.6 18.0 %collective-permute-start.38 = (bf16[128,2176]{1,0:T(8,128)(2,1)S(1)}, bf16[128,2176]{1,0:T(8,128)(2,1)S(1)}, u32[]{:S(2)}, u32[]{:S(2)}) collective-permute-start(bf16[128,2176]{1,0:T(8,128)(2,1)S(1)} %collective-permute-done.32.xa.refs_2_), channel_id=1, source_target_pairs={{0,4},{4,8},{8,12},{12,14},{14,10},{10,6},{6,2},{2,0},{5,1},{9,5},... | collective-permute-start | bytes 1671176 | tf_op jit(solution)/shard_map/ppermute | solution.py:169
  92.0 13.2 %collective-permute-start.25 = (bf16[128,2048]{1,0:T(8,128)(2,1)S(1)}, bf16[128,2048]{1,0:T(8,128)(2,1)S(1)}, u32[]{:S(2)}, u32[]{:S(2)}) collective-permute-start(bf16[128,2048]{1,0:T(8,128)(2,1)S(1)} %add_convert_fusion.4), channel_id=1, source_target_pairs={{0,4},{4,8},{8,12},{12,14},{14,10},{10,6},{6,2},{2,0},{5,1},{9,5},... | collective-permute-start | bytes 1572872 | tf_op jit(solution)/shard_map/ppermute | solution.py:169
  93.6 5.5 %collective-permute-start.34 = (bf16[128,2176]{1,0:T(8,128)(2,1)S(1)}, bf16[128,2176]{1,0:T(8,128)(2,1)S(1)}, u32[]{:S(2)}, u32[]{:S(2)}) collective-permute-start(bf16[128,2176]{1,0:T(8,128)(2,1)S(1)} %collective-permute-done.32.xa.refs_2_), channel_id=1, source_target_pairs={{0,1},{1,0},{2,3},{3,2},{4,5},{5,4},{6,7},{7,6},{8,9},{9,8},{10,11... | collective-permute-start | bytes 1671176 | tf_op jit(solution)/shard_map/ppermute | solution.py:172
  93.6 3.4 %collective-permute-start.35 = (bf16[128,2048]{1,0:T(8,128)(2,1)S(1)}, bf16[128,2048]{1,0:T(8,128)(2,1)S(1)}, u32[]{:S(2)}, u32[]{:S(2)}) collective-permute-start(bf16[128,2048]{1,0:T(8,128)(2,1)S(1)} %collective-permute-done.33.oa.refs_8_), channel_id=1, source_target_pairs={{0,1},{1,0},{2,3},{3,2},{4,5},{5,4},{6,7},{7,6},{8,9},{9,8},{10,11... | collective-permute-start | bytes 1572872 | tf_op jit(solution)/shard_map/ppermute | solution.py:172
  96.9 8.3 %collective-permute-start.30 = (bf16[128,2048]{1,0:T(8,128)(2,1)S(1)}, bf16[128,2048]{1,0:T(8,128)(2,1)S(1)}, u32[]{:S(2)}, u32[]{:S(2)}) collective-permute-start(bf16[128,2048]{1,0:T(8,128)(2,1)S(1)} %get-tuple-element.82), channel_id=1, source_target_pairs={{0,1},{1,0},{2,3},{3,2},{4,5},{5,4},{6,7},{7,6},{8,9},{9,8},{10,11... | collective-permute-start | bytes 1572872 | tf_op jit(solution)/shard_map/ppermute | solution.py:172
  97.1 13.7 %collective-permute-start.39 = (bf16[128,2048]{1,0:T(8,128)(2,1)S(1)}, bf16[128,2048]{1,0:T(8,128)(2,1)S(1)}, u32[]{:S(2)}, u32[]{:S(2)}) collective-permute-start(bf16[128,2048]{1,0:T(8,128)(2,1)S(1)} %collective-permute-done.33.oa.refs_8_), channel_id=1, source_target_pairs={{0,4},{4,8},{8,12},{12,14},{14,10},{10,6},{6,2},{2,0},{5,1},{9,5},... | collective-permute-start | bytes 1572872 | tf_op jit(solution)/shard_map/ppermute | solution.py:169
  101.9 9.4 %collective-permute-start.36 = (bf16[128,2048]{1,0:T(8,128)(2,1)S(1)}, bf16[128,2048]{1,0:T(8,128)(2,1)S(1)}, u32[]{:S(2)}, u32[]{:S(2)}) collective-permute-start(bf16[128,2048]{1,0:T(8,128)(2,1)S(1)} %get-tuple-element.86), channel_id=1, source_target_pairs={{0,1},{1,0},{2,3},{3,2},{4,5},{5,4},{6,7},{7,6},{8,9},{9,8},{10,11... | collective-permute-start | bytes 1572872 | tf_op jit(solution)/shard_map/ppermute | solution.py:172
  105.4 11.0 %collective-permute-start.31 = (bf16[128,2048]{1,0:T(8,128)(2,1)S(1)}, bf16[128,2048]{1,0:T(8,128)(2,1)S(1)}, u32[]{:S(2)}, u32[]{:S(2)}) collective-permute-start(bf16[128,2048]{1,0:T(8,128)(2,1)S(1)} %add_convert_fusion.3), channel_id=1, source_target_pairs={{0,4},{4,8},{8,12},{12,14},{14,10},{10,6},{6,2},{2,0},{5,1},{9,5},... | collective-permute-start | bytes 1572872 | tf_op jit(solution)/shard_map/ppermute | solution.py:169
  110.8 8.2 %collective-permute-start.40 = (bf16[128,2176]{1,0:T(8,128)(2,1)S(1)}, bf16[128,2176]{1,0:T(8,128)(2,1)S(1)}, u32[]{:S(2)}, u32[]{:S(2)}) collective-permute-start(bf16[128,2176]{1,0:T(8,128)(2,1)S(1)} %collective-permute-done.38.xa.refs_4_), channel_id=1, source_target_pairs={{0,1},{1,0},{2,3},{3,2},{4,5},{5,4},{6,7},{7,6},{8,9},{9,8},{10,11... | collective-permute-start | bytes 1671176 | tf_op jit(solution)/shard_map/ppermute | solution.py:172
  110.8 8.2 %collective-permute-start.41 = (bf16[128,2048]{1,0:T(8,128)(2,1)S(1)}, bf16[128,2048]{1,0:T(8,128)(2,1)S(1)}, u32[]{:S(2)}, u32[]{:S(2)}) collective-permute-start(bf16[128,2048]{1,0:T(8,128)(2,1)S(1)} %collective-permute-done.39.oa.refs_10_), channel_id=1, source_target_pairs={{0,1},{1,0},{2,3},{3,2},{4,5},{5,4},{6,7},{7,6},{8,9},{9,8},{10,11... | collective-permute-start | bytes 1572872 | tf_op jit(solution)/shard_map/ppermute | solution.py:172
  116.7 9.5 %collective-permute-start.37 = (bf16[128,2048]{1,0:T(8,128)(2,1)S(1)}, bf16[128,2048]{1,0:T(8,128)(2,1)S(1)}, u32[]{:S(2)}, u32[]{:S(2)}) collective-permute-start(bf16[128,2048]{1,0:T(8,128)(2,1)S(1)} %add_convert_fusion.2), channel_id=1, source_target_pairs={{0,4},{4,8},{8,12},{12,14},{14,10},{10,6},{6,2},{2,0},{5,1},{9,5},... | collective-permute-start | bytes 1572872 | tf_op jit(solution)/shard_map/ppermute | solution.py:169
  121.8 4.3 %collective-permute-start.42 = (bf16[128,2048]{1,0:T(8,128)(2,1)S(1)}, bf16[128,2048]{1,0:T(8,128)(2,1)S(1)}, u32[]{:S(2)}, u32[]{:S(2)}) collective-permute-start(bf16[128,2048]{1,0:T(8,128)(2,1)S(1)} %get-tuple-element.103), channel_id=1, source_target_pairs={{0,1},{1,0},{2,3},{3,2},{4,5},{5,4},{6,7},{7,6},{8,9},{9,8},{10,11... | collective-permute-start | bytes 1572872 | tf_op jit(solution)/shard_map/ppermute | solution.py:172
  121.9 12.4 %collective-permute-start.44 = (bf16[128,2048]{1,0:T(8,128)(2,1)S(1)}, bf16[128,2048]{1,0:T(8,128)(2,1)S(1)}, u32[]{:S(2)}, u32[]{:S(2)}) collective-permute-start(bf16[128,2048]{1,0:T(8,128)(2,1)S(1)} %get-tuple-element.63), channel_id=1, source_target_pairs={{0,1},{1,0},{2,3},{3,2},{4,5},{5,4},{6,7},{7,6},{8,9},{9,8},{10,11... | collective-permute-start | bytes 1572872 | tf_op jit(solution)/shard_map/ppermute | solution.py:172
  126.4 9.2 %collective-permute-start.43 = (bf16[128,2048]{1,0:T(8,128)(2,1)S(1)}, bf16[128,2048]{1,0:T(8,128)(2,1)S(1)}, u32[]{:S(2)}, u32[]{:S(2)}) collective-permute-start(bf16[128,2048]{1,0:T(8,128)(2,1)S(1)} %add_convert_fusion.1), channel_id=1, source_target_pairs={{0,4},{4,8},{8,12},{12,14},{14,10},{10,6},{6,2},{2,0},{5,1},{9,5},... | collective-permute-start | bytes 1572872 | tf_op jit(solution)/shard_map/ppermute | solution.py:169

commit v4 on v1

--- a/solution.py
+++ b/solution.py
@@ -14,6 +14,12 @@
 TN = (((0,), (0,)), ((), ()))
 GROUP = 4
 PARTS = 3
+TIES = {'xo': (('o', 0), ('sum', 3)), 'ohop': (('back', 2),)}
+OWN_AT = 'xo'
+WGRAD_TIES = ((0, 'block', 6),)
+GROUPS = (5, 8)
+BLOCK_COST = 16
+WGRAD_COST = 1
 BLOCK_VMEM = 16 << 20
 WGRAD_VMEM = 24 << 20
 
@@ -50,7 +56,7 @@
         p = jnp.sum(jnp.where(mine, coded, 0.0), axis=1, keepdims=True)
         pre = mm(x, wgu[...], NN)
         gate, up = pre[:, :ff], pre[:, ff:]
-        hid = p * mm(o, wd[...], NT)
+        hid = mm((p * o.astype(F32)).astype(BF16), wd[...], NT)
         sig = jax.nn.sigmoid(gate)
         act = gate * sig
         hidden[...] = (p * (act * up)).astype(BF16)
@@ -72,7 +78,7 @@
         ],
         compiler_params=pltpu.CompilerParams(vmem_limit_bytes=BLOCK_VMEM),
         cost_estimate=pl.CostEstimate(
-            flops=2 * (2 * rows) * width * ff * 5,
+            flops=BLOCK_COST * 2 * (2 * rows) * width * ff * 5,
             bytes_accessed=2 * (6 * rows * width + 3 * width * ff),
             transcendentals=2 * rows * ff,
         ),
@@ -114,7 +120,9 @@
         specs = [pl.BlockSpec(memory_space=pltpu.VMEM)] * len(inputs)
     else:
         inputs = [*xs, *os, *grads, *hiddens]
-        specs = [pl.BlockSpec((rows, chunk), lambda j: (0, j))] * (2 * count)
+        specs = [
+            pl.BlockSpec((v.shape[0], chunk), lambda j: (0, j)) for v in (*xs, *os)
+        ]
         specs += [pl.BlockSpec(v.shape, lambda j: (0, 0)) for v in (*grads, *hiddens)]
     alias = {len(inputs) + i: i for i in range(3)} if has and not last else {}
     return pl.pallas_call(
@@ -130,7 +138,7 @@
         input_output_aliases=alias,
         compiler_params=pltpu.CompilerParams(vmem_limit_bytes=WGRAD_VMEM),
         cost_estimate=pl.CostEstimate(
-            flops=2 * count * rows * width * ff * 3,
+            flops=WGRAD_COST * 2 * count * rows * width * ff * 3,
             bytes_accessed=2 * 2 * count * rows * width + 4 * 3 * width * ff,
             transcendentals=0,
         ),
@@ -165,25 +173,68 @@
     probs = jnp.sum(jnp.where(named, gate_probs[:, :, None], 0.0), axis=1)
     x = jnp.concatenate([tokens, encode(probs)], axis=1)
     o = out_grad
-    wgu = jnp.concatenate([w_gate[0], w_up[0]], axis=1)
     wd = w_down[0]
 
+    def after(v, *others):
+        return lax.optimization_barrier((v, *others))[0] if others else v
+
     acc, total, own = None, None, None
-    held = []
+    sums, backs, xs_seen, os_seen, held, accs = [], [], [], [], [], []
+
+    def ties_for(name, s):
+        found = []
+        for kind, lag in TIES.get(name, ()):
+            seen = {"sum": sums, "back": backs, "x": xs_seen, "o": os_seen}[kind]
+            index = s - lag
+            if 0 <= index < len(seen):
+                found.append(seen[index])
+        if name == OWN_AT and s == 1:
+            found.append(backs[0])
+        for group, place, step in WGRAD_TIES if resident else ():
+            if (place, step) == (name, s) and group < len(accs):
+                found.extend(accs[group])
+        return found
+
     for s in range(chips):
         if s:
+            x = after(x, *ties_for("xhop", s))
+            o = after(o, *ties_for("ohop", s))
             x, o = forward(x), forward(o)
-        xo, oo = other(x), other(o)
-        row_a, row_b, grads, hidden = block_pair(me, devices, x, xo, o, oo, wgu, wd)
+        xs_seen.append(x)
+        os_seen.append(o)
+        xo = other(after(x, *ties_for("xo", s)) if s else x)
+        oo = other(after(o, *ties_for("oo", s)) if s else o)
+        if s == 0:
+            pair = lax.optimization_barrier((w_gate[0], w_up[0], xo))[:2]
+            wgu = jnp.concatenate(pair, axis=1)
+            o, wgu = lax.optimization_barrier((o, wgu))
+        row_a, row_b, grads, hidden = block_pair(
+            me, devices, x, xo, o, after(oo, *ties_for("block", s)), wgu, wd
+        )
+        backs.append(row_b)
+        held.append((x, xo, o, oo, grads, hidden))
+        if s == chips - 1 and chips > 2:
+            row_a, row_b, late = lax.optimization_barrier((row_a, row_b, late))
+            halves = zip(jnp.split(late, 2), jnp.split(owed, 2))
+            total = [(a.astype(F32) + b).astype(BF16) for a, b in halves]
         partial = row_a.astype(F32) + other(row_b).astype(F32)
         if s == 0:
             own = partial
+        elif s == chips - 2 and s > 1:
+            late, owed = forward(after(total, *ties_for("rs", s))), partial
+        elif s == chips - 1 and chips > 2:
+            top, low = [forward(t) for t in total]
+            top_part, low_part = jnp.split(partial, 2)
+            top = (top.astype(F32) + top_part).astype(BF16)
+            low = (after(low, top).astype(F32) + low_part).astype(BF16)
+            total = jnp.concatenate([forward(top), forward(low)], axis=0)
         else:
             if total is not None:
-                partial = forward(total).astype(F32) + partial
+                came = forward(after(total, *ties_for("rs", s)))
+                partial = came.astype(F32) + partial
             total = partial.astype(BF16)
-        held.append((x, xo, o, oo, grads, hidden))
-        if len(held) == GROUP or s == chips - 1:
+            sums.append(total)
+        if (s + 1 in GROUPS) if resident else (len(held) >= GROUP or s == chips - 1):
             acc = wgrad_group(
                 [v for h in held for v in h[:2]],
                 [v for h in held for v in h[2:4]],
@@ -194,9 +245,12 @@
                 resident,
             )
             held = []
+            accs.append(acc)
             if not resident:
                 x, o, acc = lax.optimization_barrier((x, o, acc))
-    total = forward(total).astype(F32) + own if chips > 1 else own
+    if chips <= 2:
+        total = forward(total)
+    total = total.astype(F32) + own
     gate_wgrad, up_wgrad, down_wgrad = acc
     return (
         total.astype(BF16),

time: 153 us -> 136 us (0.89)
  waiting for transfers between devices: 63.8 us -> 42.5 us
  starting transfers between devices: 45.4 us -> 50.6 us
    ppermute x21 -> x23, waiting for transfers between devices: 63.7 us -> 42.4 us  [forward(): return lax.ppermute(v, 'expert', hop)]
    ppermute x21 -> x23, starting transfers between devices: 41.3 us -> 45.1 us  [forward(): return lax.ppermute(v, 'expert', hop)]
  transfers between devices with their start and end apart: 45 -> 47, of which waited for: 14 -> 15; matrix products, arithmetic and copies ran while one was open for 3% -> 3% of each run, Pallas kernels for 23% -> 26%
where the time goes in v4:
time: 136 us
  starting transfers between devices  50.6 us (37%)
  waiting for transfers between devices  42.5 us (31%)
  Pallas kernels  35.2 us (26%)
  other arithmetic  6.74 us (5%)
    ppermute x23, starting transfers between devices, forward(): return lax.ppermute(v, 'expert', hop)  45.1 us
    ppermute x23, waiting for transfers between devices, forward(): return lax.ppermute(v, 'expert', hop)  42.4 us
    pallas_call x8, Pallas kernels, block_pair(): pl.pallas_call(body, in_specs=[pl.BlockSpec(memory_space=pltpu.SMEM)] + [...  22.2 us
    pallas_call x2, Pallas kernels, wgrad_group(): pl.pallas_call(body, grid=(width // chunk,), in_specs=specs + (acc_specs...  13 us
    ppermute x24, starting transfers between devices, other(): return lax.ppermute(v, 'expert', swap)  5.45 us
  transfers between devices with their start and end apart: 47, of which 15 were waited for; matrix products, arithmetic and copies ran while one was open for 3% of the time, Pallas kernels for 26%

profile of v4, /device:TPU:0, one launch (start us, length us, event | category | flops | bytes accessed | tf_op | source)
XLA Modules:
  0.0 136.1 jit_solution(2444773852404691509)
XLA Ops:
  0.6 0.7 select_reduce_fusion
  1.5 1.1 fusion.1.xa.refs_0_
  2.6 0.5 collective-permute-start.7
  3.1 2.6 %collective-permute-start = (bf16[128,2176]{1,0:T(8,128)(2,1)S(1)}, bf16[128,2176]{1,0:T(8,128)(2,1)S(1)}, u32[]{:S(2)}, u32[]{:S(2)}) collective-permute-start(bf16[128,2176]{1,0:T(8,128)(2,1)S(1)} %fusion.1.xa.refs_0_), channel_id=1, source_target_pairs={{0,4},{4,8},{8,12},{12,14},{14,10},{10,6},{6,2},{2,0},{5,1},{9,5},... | collective-permute-start | bytes 1671176 | tf_op jit(solution)/shard_map/ppermute | solution.py:165
  5.9 2.3 %pad_maximum_fusion.wgu = bf16[2048,768]{1,0:T(8,128)(2,1)S(1)} fusion(bf16[2048,384]{1,0:T(8,128)(2,1)} %bitcast.15, bf16[2048,384]{1,0:T(8,128)(2,1)} %bitcast.16), kind=kLoop, calls=%fused_computation | loop fusion | flops 6291456 | bytes 6291456 | tf_op jit(solution)/shard_map/concatenate | solution.py:209
  8.2 1.8 %collective-permute-start.8 = (bf16[128,2048]{1,0:T(8,128)(2,1)S(1)}, bf16[128,2048]{1,0:T(8,128)(2,1)S(1)}, u32[]{:S(2)}, u32[]{:S(2)}) collective-permute-start(bf16[128,2048]{1,0:T(8,128)(2,1)S(1)} %copy-done.1), channel_id=1, source_target_pairs={{0,4},{4,8},{8,12},{12,14},{14,10},{10,6},{6,2},{2,0},{5,1},{9,5},... | collective-permute-start | bytes 1572872 | tf_op jit(solution)/shard_map/ppermute | solution.py:165
  10.0 3.2 %collective-permute-done.xa.refs_2_ = bf16[128,2176]{1,0:T(8,128)(2,1)S(1)} collective-permute-done((bf16[128,2176]{1,0:T(8,128)(2,1)S(1)}, bf16[128,2176]{1,0:T(8,128)(2,1)S(1)}, u32[]{:S(2)}, u32[]{:S(2)}) %collective-permute-start) | collective-permute-done | bytes 557088 | tf_op jit(solution)/shard_map/ppermute | solution.py:165
  13.2 2.1 %collective-permute-start.1 = (bf16[128,2176]{1,0:T(8,128)(2,1)S(1)}, bf16[128,2176]{1,0:T(8,128)(2,1)S(1)}, u32[]{:S(2)}, u32[]{:S(2)}) collective-permute-start(bf16[128,2176]{1,0:T(8,128)(2,1)S(1)} %collective-permute-done.xa.refs_2_), channel_id=1, source_target_pairs={{0,4},{4,8},{8,12},{12,14},{14,10},{10,6},{6,2},{2,0},{5,1},{9,5},... | collective-permute-start | bytes 1671176 | tf_op jit(solution)/shard_map/ppermute | solution.py:165
  15.3 2.8 %block_pair.8 = (bf16[128,2048]{1,0:T(8,128)(2,1)S(1)}, bf16[128,2048]{1,0:T(8,128)(2,1)S(1)}, bf16[256,768]{1,0:T(8,128)(2,1)S(1)}, bf16[256,384]{1,0:T(8,128)(2,1)S(1)}) custom-call(s32[1]{0:T(128)} %bitcast.me, bf16[128,2176]{1,0:T(8,128)(2,1)S(1)} %fusion.1.xa.refs_0_, bf16[128,2176]{1,0:T(8,128)(2,1)S(1)} %collective-permute-done.7.xb.refs_1_, ...), custom_call_target="tpu_custom_call" | custom-call | flops 32212254720 | bytes 7864320 | tf_op jit(solution)/shard_map/block_pair/pallas_call | solution.py:69
  18.1 0.8 collective-permute-done.8.oa.refs_12_
  18.8 0.5 collective-permute-start.12
  19.3 2.1 %collective-permute-start.10 = (bf16[128,2048]{1,0:T(8,128)(2,1)S(1)}, bf16[128,2048]{1,0:T(8,128)(2,1)S(1)}, u32[]{:S(2)}, u32[]{:S(2)}) collective-permute-start(bf16[128,2048]{1,0:T(8,128)(2,1)S(1)} %collective-permute-done.8.oa.refs_12_), channel_id=1, source_target_pairs={{0,4},{4,8},{8,12},{12,14},{14,10},{10,6},{6,2},{2,0},{5,1},{9,5},... | collective-permute-start | bytes 1572872 | tf_op jit(solution)/shard_map/ppermute | solution.py:165
  21.4 3.4 %collective-permute-done.1.xa.refs_4_ = bf16[128,2176]{1,0:T(8,128)(2,1)S(1)} collective-permute-done((bf16[128,2176]{1,0:T(8,128)(2,1)S(1)}, bf16[128,2176]{1,0:T(8,128)(2,1)S(1)}, u32[]{:S(2)}, u32[]{:S(2)}) %collective-permute-start.1) | collective-permute-done | bytes 557088 | tf_op jit(solution)/shard_map/ppermute | solution.py:165
  24.8 2.1 %collective-permute-start.2 = (bf16[128,2176]{1,0:T(8,128)(2,1)S(1)}, bf16[128,2176]{1,0:T(8,128)(2,1)S(1)}, u32[]{:S(2)}, u32[]{:S(2)}) collective-permute-start(bf16[128,2176]{1,0:T(8,128)(2,1)S(1)} %collective-permute-done.1.xa.refs_4_), channel_id=1, source_target_pairs={{0,4},{4,8},{8,12},{12,14},{14,10},{10,6},{6,2},{2,0},{5,1},{9,5},... | collective-permute-start | bytes 1671176 | tf_op jit(solution)/shard_map/ppermute | solution.py:165
  26.9 2.8 %block_pair.9 = (bf16[128,2048]{1,0:T(8,128)(2,1)S(1)}, bf16[128,2048]{1,0:T(8,128)(2,1)S(1)}, bf16[256,768]{1,0:T(8,128)(2,1)S(1)}, bf16[256,384]{1,0:T(8,128)(2,1)S(1)}) custom-call(s32[1]{0:T(128)} %bitcast.me, bf16[128,2176]{1,0:T(8,128)(2,1)S(1)} %collective-permute-done.xa.refs_2_, bf16[128,2176]{1,0:T(8,128)(2,1)S(1)} %collective-permute-done.11.xb.refs_3_, ...), custom_call_target="tpu_custom_call" | custom-call | flops 32212254720 | bytes 7864320 | tf_op jit(solution)/shard_map/block_pair/pallas_call | solution.py:69
  29.7 0.7 collective-permute-done.10.oa.refs_14_
  30.4 0.5 collective-permute-start.15
  30.9 2.1 %collective-permute-start.13 = (bf16[128,2048]{1,0:T(8,128)(2,1)S(1)}, bf16[128,2048]{1,0:T(8,128)(2,1)S(1)}, u32[]{:S(2)}, u32[]{:S(2)}) collective-permute-start(bf16[128,2048]{1,0:T(8,128)(2,1)S(1)} %collective-permute-done.10.oa.refs_14_), channel_id=1, source_target_pairs={{0,4},{4,8},{8,12},{12,14},{14,10},{10,6},{6,2},{2,0},{5,1},{9,5},... | collective-permute-start | bytes 1572872 | tf_op jit(solution)/shard_map/ppermute | solution.py:165
  33.0 3.4 %collective-permute-done.2.xa.refs_6_ = bf16[128,2176]{1,0:T(8,128)(2,1)S(1)} collective-permute-done((bf16[128,2176]{1,0:T(8,128)(2,1)S(1)}, bf16[128,2176]{1,0:T(8,128)(2,1)S(1)}, u32[]{:S(2)}, u32[]{:S(2)}) %collective-permute-start.2) | collective-permute-done | bytes 557088 | tf_op jit(solution)/shard_map/ppermute | solution.py:165
  36.4 2.1 %collective-permute-start.3 = (bf16[128,2176]{1,0:T(8,128)(2,1)S(1)}, bf16[128,2176]{1,0:T(8,128)(2,1)S(1)}, u32[]{:S(2)}, u32[]{:S(2)}) collective-permute-start(bf16[128,2176]{1,0:T(8,128)(2,1)S(1)} %collective-permute-done.2.xa.refs_6_), channel_id=1, source_target_pairs={{0,4},{4,8},{8,12},{12,14},{14,10},{10,6},{6,2},{2,0},{5,1},{9,5},... | collective-permute-start | bytes 1671176 | tf_op jit(solution)/shard_map/ppermute | solution.py:165
  38.6 1.6 %collective-permute-start.21 = (bf16[128,2048]{1,0:T(8,128)(2,1)S(1)}, bf16[128,2048]{1,0:T(8,128)(2,1)S(1)}, u32[]{:S(2)}, u32[]{:S(2)}) collective-permute-start(bf16[128,2048]{1,0:T(8,128)(2,1)S(1)} %add_convert_fusion.5), channel_id=1, source_target_pairs={{0,4},{4,8},{8,12},{12,14},{14,10},{10,6},{6,2},{2,0},{5,1},{9,5},... | collective-permute-start | bytes 1572872 | tf_op jit(solution)/shard_map/ppermute | solution.py:165
  40.2 2.8 %block_pair.10 = (bf16[128,2048]{1,0:T(8,128)(2,1)S(1)}, bf16[128,2048]{1,0:T(8,128)(2,1)S(1)}, bf16[256,768]{1,0:T(8,128)(2,1)S(1)}, bf16[256,384]{1,0:T(8,128)(2,1)S(1)}) custom-call(s32[1]{0:T(128)} %bitcast.me, bf16[128,2176]{1,0:T(8,128)(2,1)S(1)} %collective-permute-done.1.xa.refs_4_, bf16[128,2176]{1,0:T(8,128)(2,1)S(1)} %collective-permute-done.14.xb.refs_5_, ...), custom_call_target="tpu_custom_call" | custom-call | flops 32212254720 | bytes 7864320 | tf_op jit(solution)/shard_map/block_pair/pallas_call | solution.py:69
  43.1 0.5 collective-permute-start.18
  43.7 4.3 %collective-permute-done.3.xa.refs_8_ = bf16[128,2176]{1,0:T(8,128)(2,1)S(1)} collective-permute-done((bf16[128,2176]{1,0:T(8,128)(2,1)S(1)}, bf16[128,2176]{1,0:T(8,128)(2,1)S(1)}, u32[]{:S(2)}, u32[]{:S(2)}) %collective-permute-start.3) | collective-permute-done | bytes 557088 | tf_op jit(solution)/shard_map/ppermute | solution.py:165
  48.0 2.1 %collective-permute-start.16 = (bf16[128,2048]{1,0:T(8,128)(2,1)S(1)}, bf16[128,2048]{1,0:T(8,128)(2,1)S(1)}, u32[]{:S(2)}, u32[]{:S(2)}) collective-permute-start(bf16[128,2048]{1,0:T(8,128)(2,1)S(1)} %collective-permute-done.13.oa.refs_16_), channel_id=1, source_target_pairs={{0,4},{4,8},{8,12},{12,14},{14,10},{10,6},{6,2},{2,0},{5,1},{9,5},... | collective-permute-start | bytes 1572872 | tf_op jit(solution)/shard_map/ppermute | solution.py:165
  50.0 3.5 %collective-permute-done.21 = bf16[128,2048]{1,0:T(8,128)(2,1)S(1)} collective-permute-done((bf16[128,2048]{1,0:T(8,128)(2,1)S(1)}, bf16[128,2048]{1,0:T(8,128)(2,1)S(1)}, u32[]{:S(2)}, u32[]{:S(2)}) %collective-permute-start.21) | collective-permute-done | bytes 524320 | tf_op jit(solution)/shard_map/ppermute | solution.py:165
  53.6 2.1 %collective-permute-start.4 = (bf16[128,2176]{1,0:T(8,128)(2,1)S(1)}, bf16[128,2176]{1,0:T(8,128)(2,1)S(1)}, u32[]{:S(2)}, u32[]{:S(2)}) collective-permute-start(bf16[128,2176]{1,0:T(8,128)(2,1)S(1)} %collective-permute-done.3.xa.refs_8_), channel_id=1, source_target_pairs={{0,4},{4,8},{8,12},{12,14},{14,10},{10,6},{6,2},{2,0},{5,1},{9,5},... | collective-permute-start | bytes 1671176 | tf_op jit(solution)/shard_map/ppermute | solution.py:165
  55.7 0.2 add_convert_fusion.4
  55.9 1.6 %collective-permute-start.26 = (bf16[128,2048]{1,0:T(8,128)(2,1)S(1)}, bf16[128,2048]{1,0:T(8,128)(2,1)S(1)}, u32[]{:S(2)}, u32[]{:S(2)}) collective-permute-start(bf16[128,2048]{1,0:T(8,128)(2,1)S(1)} %add_convert_fusion.4), channel_id=1, source_target_pairs={{0,4},{4,8},{8,12},{12,14},{14,10},{10,6},{6,2},{2,0},{5,1},{9,5},... | collective-permute-start | bytes 1572872 | tf_op jit(solution)/shard_map/ppermute | solution.py:165
  57.5 2.8 %block_pair.11 = (bf16[128,2048]{1,0:T(8,128)(2,1)S(1)}, bf16[128,2048]{1,0:T(8,128)(2,1)S(1)}, bf16[256,768]{1,0:T(8,128)(2,1)S(1)}, bf16[256,384]{1,0:T(8,128)(2,1)S(1)}) custom-call(s32[1]{0:T(128)} %bitcast.me, bf16[128,2176]{1,0:T(8,128)(2,1)S(1)} %collective-permute-done.2.xa.refs_6_, bf16[128,2176]{1,0:T(8,128)(2,1)S(1)} %collective-permute-done.18.xb.refs_7_, ...), custom_call_target="tpu_custom_call" | custom-call | flops 32212254720 | bytes 7864320 | tf_op jit(solution)/shard_map/block_pair/pallas_call | solution.py:69
  60.4 0.5 collective-permute-start.23
  61.0 4.2 %collective-permute-done.4.xa.refs_0_ = bf16[128,2176]{1,0:T(8,128)(2,1)S(1)} collective-permute-done((bf16[128,2176]{1,0:T(8,128)(2,1)S(1)}, bf16[128,2176]{1,0:T(8,128)(2,1)S(1)}, u32[]{:S(2)}, u32[]{:S(2)}) %collective-permute-start.4) | collective-permute-done | bytes 557088 | tf_op jit(solution)/shard_map/ppermute | solution.py:165
  65.2 2.1 %collective-permute-start.20 = (bf16[128,2048]{1,0:T(8,128)(2,1)S(1)}, bf16[128,2048]{1,0:T(8,128)(2,1)S(1)}, u32[]{:S(2)}, u32[]{:S(2)}) collective-permute-start(bf16[128,2048]{1,0:T(8,128)(2,1)S(1)} %collective-permute-done.16.oa.refs_18_), channel_id=1, source_target_pairs={{0,4},{4,8},{8,12},{12,14},{14,10},{10,6},{6,2},{2,0},{5,1},{9,5},... | collective-permute-start | bytes 1572872 | tf_op jit(solution)/shard_map/ppermute | solution.py:165
  67.2 3.5 %collective-permute-done.26 = bf16[128,2048]{1,0:T(8,128)(2,1)S(1)} collective-permute-done((bf16[128,2048]{1,0:T(8,128)(2,1)S(1)}, bf16[128,2048]{1,0:T(8,128)(2,1)S(1)}, u32[]{:S(2)}, u32[]{:S(2)}) %collective-permute-start.26) | collective-permute-done | bytes 524320 | tf_op jit(solution)/shard_map/ppermute | solution.py:165
  70.8 2.1 %collective-permute-start.5 = (bf16[128,2176]{1,0:T(8,128)(2,1)S(1)}, bf16[128,2176]{1,0:T(8,128)(2,1)S(1)}, u32[]{:S(2)}, u32[]{:S(2)}) collective-permute-start(bf16[128,2176]{1,0:T(8,128)(2,1)S(1)} %collective-permute-done.4.xa.refs_0_), channel_id=1, source_target_pairs={{0,4},{4,8},{8,12},{12,14},{14,10},{10,6},{6,2},{2,0},{5,1},{9,5},... | collective-permute-start | bytes 1671176 | tf_op jit(solution)/shard_map/ppermute | solution.py:165
  72.9 0.2 add_convert_fusion.3
  73.1 1.8 %collective-permute-start.31 = (bf16[128,2048]{1,0:T(8,128)(2,1)S(1)}, bf16[128,2048]{1,0:T(8,128)(2,1)S(1)}, u32[]{:S(2)}, u32[]{:S(2)}) collective-permute-start(bf16[128,2048]{1,0:T(8,128)(2,1)S(1)} %add_convert_fusion.3), channel_id=1, source_target_pairs={{0,4},{4,8},{8,12},{12,14},{14,10},{10,6},{6,2},{2,0},{5,1},{9,5},... | collective-permute-start | bytes 1572872 | tf_op jit(solution)/shard_map/ppermute | solution.py:165
  74.9 2.8 %block_pair.12 = (bf16[128,2048]{1,0:T(8,128)(2,1)S(1)}, bf16[128,2048]{1,0:T(8,128)(2,1)S(1)}, bf16[256,768]{1,0:T(8,128)(2,1)S(1)}, bf16[256,384]{1,0:T(8,128)(2,1)S(1)}) custom-call(s32[1]{0:T(128)} %bitcast.me, bf16[128,2176]{1,0:T(8,128)(2,1)S(1)} %collective-permute-done.3.xa.refs_8_, bf16[128,2176]{1,0:T(8,128)(2,1)S(1)} %collective-permute-done.23.xb.refs_9_, ...), custom_call_target="tpu_custom_call" | custom-call | flops 32212254720 | bytes 7864320 | tf_op jit(solution)/shard_map/block_pair/pallas_call | solution.py:69
  77.8 0.5 collective-permute-start.28
  78.3 1.6 %collective-permute-start.25 = (bf16[128,2048]{1,0:T(8,128)(2,1)S(1)}, bf16[128,2048]{1,0:T(8,128)(2,1)S(1)}, u32[]{:S(2)}, u32[]{:S(2)}) collective-permute-start(bf16[128,2048]{1,0:T(8,128)(2,1)S(1)} %collective-permute-done.20.oa.refs_6_), channel_id=1, source_target_pairs={{0,4},{4,8},{8,12},{12,14},{14,10},{10,6},{6,2},{2,0},{5,1},{9,5},... | collective-permute-start | bytes 1572872 | tf_op jit(solution)/shard_map/ppermute | solution.py:165
  79.9 2.5 %collective-permute-done.5.xa.refs_2_ = bf16[128,2176]{1,0:T(8,128)(2,1)S(1)} collective-permute-done((bf16[128,2176]{1,0:T(8,128)(2,1)S(1)}, bf16[128,2176]{1,0:T(8,128)(2,1)S(1)}, u32[]{:S(2)}, u32[]{:S(2)}) %collective-permute-start.5) | collective-permute-done | bytes 557088 | tf_op jit(solution)/shard_map/ppermute | solution.py:165
  82.4 5.6 %collective-permute-done.31 = bf16[128,2048]{1,0:T(8,128)(2,1)S(1)} collective-permute-done((bf16[128,2048]{1,0:T(8,128)(2,1)S(1)}, bf16[128,2048]{1,0:T(8,128)(2,1)S(1)}, u32[]{:S(2)}, u32[]{:S(2)}) %collective-permute-start.31) | collective-permute-done | bytes 524320 | tf_op jit(solution)/shard_map/ppermute | solution.py:165
  88.0 2.1 %collective-permute-start.6 = (bf16[128,2176]{1,0:T(8,128)(2,1)S(1)}, bf16[128,2176]{1,0:T(8,128)(2,1)S(1)}, u32[]{:S(2)}, u32[]{:S(2)}) collective-permute-start(bf16[128,2176]{1,0:T(8,128)(2,1)S(1)} %collective-permute-done.5.xa.refs_2_), channel_id=1, source_target_pairs={{0,4},{4,8},{8,12},{12,14},{14,10},{10,6},{6,2},{2,0},{5,1},{9,5},... | collective-permute-start | bytes 1671176 | tf_op jit(solution)/shard_map/ppermute | solution.py:165
  90.3 1.6 %collective-permute-start.33 = (bf16[128,2048]{1,0:T(8,128)(2,1)S(1)}, bf16[128,2048]{1,0:T(8,128)(2,1)S(1)}, u32[]{:S(2)}, u32[]{:S(2)}) collective-permute-start(bf16[128,2048]{1,0:T(8,128)(2,1)S(1)} %add_convert_fusion.2), channel_id=1, source_target_pairs={{0,4},{4,8},{8,12},{12,14},{14,10},{10,6},{6,2},{2,0},{5,1},{9,5},... | collective-permute-start | bytes 1572872 | tf_op jit(solution)/shard_map/ppermute | solution.py:165
  91.9 1.7 %collective-permute-done.25.oa.refs_8_ = bf16[128,2048]{1,0:T(8,128)(2,1)S(1)} collective-permute-done((bf16[128,2048]{1,0:T(8,128)(2,1)S(1)}, bf16[128,2048]{1,0:T(8,128)(2,1)S(1)}, u32[]{:S(2)}, u32[]{:S(2)}) %collective-permute-start.25) | collective-permute-done | bytes 524320 | tf_op jit(solution)/shard_map/ppermute | solution.py:165
  93.6 0.5 collective-permute-start.39
  94.1 2.8 %block_pair.13 = (bf16[128,2048]{1,0:T(8,128)(2,1)S(1)}, bf16[128,2048]{1,0:T(8,128)(2,1)S(1)}, bf16[256,768]{1,0:T(8,128)(2,1)S(1)}, bf16[256,384]{1,0:T(8,128)(2,1)S(1)}) custom-call(s32[1]{0:T(128)} %bitcast.me, bf16[128,2176]{1,0:T(8,128)(2,1)S(1)} %collective-permute-done.4.xa.refs_0_, bf16[128,2176]{1,0:T(8,128)(2,1)S(1)} %collective-permute-done.28.xb.refs_1_, ...), custom_call_target="tpu_custom_call" | custom-call | flops 32212254720 | bytes 7864320 | tf_op jit(solution)/shard_map/block_pair/pallas_call | solution.py:69
  97.0 2.1 %collective-permute-start.30 = (bf16[128,2048]{1,0:T(8,128)(2,1)S(1)}, bf16[128,2048]{1,0:T(8,128)(2,1)S(1)}, u32[]{:S(2)}, u32[]{:S(2)}) collective-permute-start(bf16[128,2048]{1,0:T(8,128)(2,1)S(1)} %collective-permute-done.25.oa.refs_8_), channel_id=1, source_target_pairs={{0,4},{4,8},{8,12},{12,14},{14,10},{10,6},{6,2},{2,0},{5,1},{9,5},... | collective-permute-start | bytes 1572872 | tf_op jit(solution)/shard_map/ppermute | solution.py:165
  99.1 7.2 %wgrad_group.2 = (f32[2048,384]{1,0:T(8,128)S(1)}, f32[2048,384]{1,0:T(8,128)S(1)}, f32[384,2048]{1,0:T(8,128)S(1)}) custom-call(bf16[128,2176]{1,0:T(8,128)(2,1)S(1)} %fusion.1.xa.refs_0_, bf16[128,2176]{1,0:T(8,128)(2,1)S(1)} %collective-permute-done.7.xb.refs_1_, bf16[128,2176]{1,0:T(8,128)(2,1)S(1)} %collective-permute-done.xa.refs_2_, ...), custom_call_target="tpu_custom_call" | custom-call | flops 6039797760 | bytes 19922944 | tf_op jit(solution)/shard_map/wgrad_group/pallas_call | solution.py:128
  106.5 0.2 add_convert_fusion.1
  106.8 1.5 %collective-permute-start.37 = (bf16[128,2048]{1,0:T(8,128)(2,1)S(1)}, bf16[128,2048]{1,0:T(8,128)(2,1)S(1)}, u32[]{:S(2)}, u32[]{:S(2)}) collective-permute-start(bf16[128,2048]{1,0:T(8,128)(2,1)S(1)} %add_convert_fusion.1), channel_id=1, source_target_pairs={{0,4},{4,8},{8,12},{12,14},{14,10},{10,6},{6,2},{2,0},{5,1},{9,5},... | collective-permute-start | bytes 1572872 | tf_op jit(solution)/shard_map/ppermute | solution.py:165
  108.3 2.5 %collective-permute-done.30.oa.refs_10_ = bf16[128,2048]{1,0:T(8,128)(2,1)S(1)} collective-permute-done((bf16[128,2048]{1,0:T(8,128)(2,1)S(1)}, bf16[128,2048]{1,0:T(8,128)(2,1)S(1)}, u32[]{:S(2)}, u32[]{:S(2)}) %collective-permute-start.30) | collective-permute-done | bytes 524320 | tf_op jit(solution)/shard_map/ppermute | solution.py:165
  110.8 0.5 collective-permute-start.36
  111.3 2.8 %block_pair.15 = (bf16[128,2048]{1,0:T(8,128)(2,1)S(1)}, bf16[128,2048]{1,0:T(8,128)(2,1)S(1)}, bf16[256,768]{1,0:T(8,128)(2,1)S(1)}, bf16[256,384]{1,0:T(8,128)(2,1)S(1)}) custom-call(s32[1]{0:T(128)} %bitcast.me, bf16[128,2176]{1,0:T(8,128)(2,1)S(1)} %collective-permute-done.5.xa.refs_2_, bf16[128,2176]{1,0:T(8,128)(2,1)S(1)} %collective-permute-done.38.xb.refs_3_, ...), custom_call_target="tpu_custom_call" | custom-call | flops 32212254720 | bytes 7864320 | tf_op jit(solution)/shard_map/block_pair/pallas_call | solution.py:69
  114.2 2.8 %block_pair.14 = (bf16[128,2048]{1,0:T(8,128)(2,1)S(1)}, bf16[128,2048]{1,0:T(8,128)(2,1)S(1)}, bf16[256,768]{1,0:T(8,128)(2,1)S(1)}, bf16[256,384]{1,0:T(8,128)(2,1)S(1)}) custom-call(s32[1]{0:T(128)} %bitcast.me, bf16[128,2176]{1,0:T(8,128)(2,1)S(1)} %collective-permute-done.6.xa.refs_4_, bf16[128,2176]{1,0:T(8,128)(2,1)S(1)} %collective-permute-done.35.xb.refs_5_, ...), custom_call_target="tpu_custom_call" | custom-call | flops 32212254720 | bytes 7864320 | tf_op jit(solution)/shard_map/block_pair/pallas_call | solution.py:69
  117.0 0.5 collective-permute-start.42
  117.8 2.1 %collective-permute-start.41 = (bf16[64,2048]{1,0:T(8,128)(2,1)S(1)}, bf16[64,2048]{1,0:T(8,128)(2,1)S(1)}, u32[]{:S(2)}, u32[]{:S(2)}) collective-permute-start(bf16[64,2048]{1,0:T(8,128)(2,1)S(1)} %get-tuple-element.124), channel_id=1, source_target_pairs={{0,4},{4,8},{8,12},{12,14},{14,10},{10,6},{6,2},{2,0},{5,1},{9,5},... | collective-permute-start | bytes 786440 | tf_op jit(solution)/shard_map/ppermute | solution.py:165
  120.0 1.6 %collective-permute-start.44 = (bf16[64,2048]{1,0:T(8,128)(2,1)S(1)}, bf16[64,2048]{1,0:T(8,128)(2,1)S(1)}, u32[]{:S(2)}, u32[]{:S(2)}) collective-permute-start(bf16[64,2048]{1,0:T(8,128)(2,1)S(1)} %get-tuple-element.125), channel_id=1, source_target_pairs={{0,4},{4,8},{8,12},{12,14},{14,10},{10,6},{6,2},{2,0},{5,1},{9,5},... | collective-permute-start | bytes 786440 | tf_op jit(solution)/shard_map/ppermute | solution.py:165
  121.7 2.6 %collective-permute-done.41 = bf16[64,2048]{1,0:T(8,128)(2,1)S(1)} collective-permute-done((bf16[64,2048]{1,0:T(8,128)(2,1)S(1)}, bf16[64,2048]{1,0:T(8,128)(2,1)S(1)}, u32[]{:S(2)}, u32[]{:S(2)}) %collective-permute-start.41) | collective-permute-done | bytes 262176 | tf_op jit(solution)/shard_map/ppermute | solution.py:165
  124.3 2.1 %collective-permute-start.43 = (bf16[64,2048]{1,0:T(8,128)(2,1)S(1)}, bf16[64,2048]{1,0:T(8,128)(2,1)S(1)}, u32[]{:S(2)}, u32[]{:S(2)}) collective-permute-start(bf16[64,2048]{1,0:T(8,128)(2,1)S(1)} %fusion.4), channel_id=1, source_target_pairs={{0,4},{4,8},{8,12},{12,14},{14,10},{10,6},{6,2},{2,0},{5,1},{9,5},... | collective-permute-start | bytes 786440 | tf_op jit(solution)/shard_map/ppermute | solution.py:165
  126.4 0.6 collective-permute-done.44
  127.1 2.1 %collective-permute-start.45 = (bf16[64,2048]{1,0:T(8,128)(2,1)S(1)}, bf16[64,2048]{1,0:T(8,128)(2,1)S(1)}, u32[]{:S(2)}, u32[]{:S(2)}) collective-permute-start(bf16[64,2048]{1,0:T(8,128)(2,1)S(1)} %fusion.2), channel_id=1, source_target_pairs={{0,4},{4,8},{8,12},{12,14},{14,10},{10,6},{6,2},{2,0},{5,1},{9,5},... | collective-permute-start | bytes 786440 | tf_op jit(solution)/shard_map/ppermute | solution.py:165
  129.3 5.8 %wgrad_group.3 = (bf16[2048,384]{1,0:T(8,128)(2,1)}, bf16[2048,384]{1,0:T(8,128)(2,1)}, bf16[384,2048]{1,0:T(8,128)(2,1)}) custom-call(bf16[128,2176]{1,0:T(8,128)(2,1)S(1)} %collective-permute-done.4.xa.refs_0_, bf16[128,2176]{1,0:T(8,128)(2,1)S(1)} %collective-permute-done.28.xb.refs_1_, bf16[128,2176]{1,0:T(8,128)(2,1)S(1)} %collective-permute-done.5.xa.refs_2_, ...), custom_call_target="tpu_custom_call" | custom-call | flops 3623878656 | bytes 15728640 | tf_op jit(solution)/shard_map/wgrad_group/pallas_call | solution.py:128
  135.0 1.0 add_convert_fusion
  (61 shorter events, 2.0 us)
Async XLA Ops:
  2.6 3.3 %collective-permute-start.7 = (bf16[128,2176]{1,0:T(8,128)(2,1)S(1)}, bf16[128,2176]{1,0:T(8,128)(2,1)S(1)}, u32[]{:S(2)}, u32[]{:S(2)}) collective-permute-start(bf16[128,2176]{1,0:T(8,128)(2,1)S(1)} %fusion.1.xa.refs_0_), channel_id=1, source_target_pairs={{0,1},{1,0},{2,3},{3,2},{4,5},{5,4},{6,7},{7,6},{8,9},{9,8},{10,11... | collective-permute-start | bytes 1671176 | tf_op jit(solution)/shard_map/ppermute | solution.py:168
  3.1 10.1 %collective-permute-start = (bf16[128,2176]{1,0:T(8,128)(2,1)S(1)}, bf16[128,2176]{1,0:T(8,128)(2,1)S(1)}, u32[]{:S(2)}, u32[]{:S(2)}) collective-permute-start(bf16[128,2176]{1,0:T(8,128)(2,1)S(1)} %fusion.1.xa.refs_0_), channel_id=1, source_target_pairs={{0,4},{4,8},{8,12},{12,14},{14,10},{10,6},{6,2},{2,0},{5,1},{9,5},... | collective-permute-start | bytes 1671176 | tf_op jit(solution)/shard_map/ppermute | solution.py:165
  5.7 9.5 %collective-permute-start.9 = (bf16[128,2048]{1,0:T(8,128)(2,1)}, bf16[128,2048]{1,0:T(8,128)(2,1)S(1)}, u32[]{:S(2)}, u32[]{:S(2)}) collective-permute-start(bf16[128,2048]{1,0:T(8,128)(2,1)} %refs_10_), channel_id=1, source_target_pairs={{0,1},{1,0},{2,3},{3,2},{4,5},{5,4},{6,7},{7,6},{8,9},{9,8},{10,11... | collective-permute-start | bytes 1572872 | tf_op jit(solution)/shard_map/ppermute | solution.py:168
  5.9 2.3 %copy-start.1 = (bf16[128,2048]{1,0:T(8,128)(2,1)S(1)}, bf16[128,2048]{1,0:T(8,128)(2,1)}, u32[]{:S(2)}) copy-start(bf16[128,2048]{1,0:T(8,128)(2,1)} %refs_10_) | copy-start | bytes 1572868
  5.9 9.4 %copy-start = (bf16[1,384,2048]{2,1,0:T(8,128)(2,1)S(1)}, bf16[1,384,2048]{2,1,0:T(8,128)(2,1)}, u32[]{:S(2)}) copy-start(bf16[1,384,2048]{2,1,0:T(8,128)(2,1)} %param.13) | copy-start | bytes 4718596
  8.2 10.7 %collective-permute-start.8 = (bf16[128,2048]{1,0:T(8,128)(2,1)S(1)}, bf16[128,2048]{1,0:T(8,128)(2,1)S(1)}, u32[]{:S(2)}, u32[]{:S(2)}) collective-permute-start(bf16[128,2048]{1,0:T(8,128)(2,1)S(1)} %copy-done.1), channel_id=1, source_target_pairs={{0,4},{4,8},{8,12},{12,14},{14,10},{10,6},{6,2},{2,0},{5,1},{9,5},... | collective-permute-start | bytes 1572872 | tf_op jit(solution)/shard_map/ppermute | solution.py:165
  13.2 11.6 %collective-permute-start.1 = (bf16[128,2176]{1,0:T(8,128)(2,1)S(1)}, bf16[128,2176]{1,0:T(8,128)(2,1)S(1)}, u32[]{:S(2)}, u32[]{:S(2)}) collective-permute-start(bf16[128,2176]{1,0:T(8,128)(2,1)S(1)} %collective-permute-done.xa.refs_2_), channel_id=1, source_target_pairs={{0,4},{4,8},{8,12},{12,14},{14,10},{10,6},{6,2},{2,0},{5,1},{9,5},... | collective-permute-start | bytes 1671176 | tf_op jit(solution)/shard_map/ppermute | solution.py:165
  18.8 8.1 %collective-permute-start.11 = (bf16[128,2176]{1,0:T(8,128)(2,1)S(1)}, bf16[128,2176]{1,0:T(8,128)(2,1)S(1)}, u32[]{:S(2)}, u32[]{:S(2)}) collective-permute-start(bf16[128,2176]{1,0:T(8,128)(2,1)S(1)} %collective-permute-done.xa.refs_2_), channel_id=1, source_target_pairs={{0,1},{1,0},{2,3},{3,2},{4,5},{5,4},{6,7},{7,6},{8,9},{9,8},{10,11... | collective-permute-start | bytes 1671176 | tf_op jit(solution)/shard_map/ppermute | solution.py:168
  18.8 8.0 %collective-permute-start.12 = (bf16[128,2048]{1,0:T(8,128)(2,1)S(1)}, bf16[128,2048]{1,0:T(8,128)(2,1)S(1)}, u32[]{:S(2)}, u32[]{:S(2)}) collective-permute-start(bf16[128,2048]{1,0:T(8,128)(2,1)S(1)} %collective-permute-done.8.oa.refs_12_), channel_id=1, source_target_pairs={{0,1},{1,0},{2,3},{3,2},{4,5},{5,4},{6,7},{7,6},{8,9},{9,8},{10,11... | collective-permute-start | bytes 1572872 | tf_op jit(solution)/shard_map/ppermute | solution.py:168
  19.3 11.1 %collective-permute-start.10 = (bf16[128,2048]{1,0:T(8,128)(2,1)S(1)}, bf16[128,2048]{1,0:T(8,128)(2,1)S(1)}, u32[]{:S(2)}, u32[]{:S(2)}) collective-permute-start(bf16[128,2048]{1,0:T(8,128)(2,1)S(1)} %collective-permute-done.8.oa.refs_12_), channel_id=1, source_target_pairs={{0,4},{4,8},{8,12},{12,14},{14,10},{10,6},{6,2},{2,0},{5,1},{9,5},... | collective-permute-start | bytes 1572872 | tf_op jit(solution)/shard_map/ppermute | solution.py:165
  24.8 11.6 %collective-permute-start.2 = (bf16[128,2176]{1,0:T(8,128)(2,1)S(1)}, bf16[128,2176]{1,0:T(8,128)(2,1)S(1)}, u32[]{:S(2)}, u32[]{:S(2)}) collective-permute-start(bf16[128,2176]{1,0:T(8,128)(2,1)S(1)} %collective-permute-done.1.xa.refs_4_), channel_id=1, source_target_pairs={{0,4},{4,8},{8,12},{12,14},{14,10},{10,6},{6,2},{2,0},{5,1},{9,5},... | collective-permute-start | bytes 1671176 | tf_op jit(solution)/shard_map/ppermute | solution.py:165
  29.7 8.8 %collective-permute-start.17 = (bf16[128,2048]{1,0:T(8,128)(2,1)S(1)}, bf16[128,2048]{1,0:T(8,128)(2,1)S(1)}, u32[]{:S(2)}, u32[]{:S(2)}) collective-permute-start(bf16[128,2048]{1,0:T(8,128)(2,1)S(1)} %get-tuple-element.71), channel_id=1, source_target_pairs={{0,1},{1,0},{2,3},{3,2},{4,5},{5,4},{6,7},{7,6},{8,9},{9,8},{10,11... | collective-permute-start | bytes 1572872 | tf_op jit(solution)/shard_map/ppermute | solution.py:168
  30.4 9.8 %collective-permute-start.14 = (bf16[128,2176]{1,0:T(8,128)(2,1)S(1)}, bf16[128,2176]{1,0:T(8,128)(2,1)S(1)}, u32[]{:S(2)}, u32[]{:S(2)}) collective-permute-start(bf16[128,2176]{1,0:T(8,128)(2,1)S(1)} %collective-permute-done.1.xa.refs_4_), channel_id=1, source_target_pairs={{0,1},{1,0},{2,3},{3,2},{4,5},{5,4},{6,7},{7,6},{8,9},{9,8},{10,11... | collective-permute-start | bytes 1671176 | tf_op jit(solution)/shard_map/ppermute | solution.py:168
  30.4 9.8 %collective-permute-start.15 = (bf16[128,2048]{1,0:T(8,128)(2,1)S(1)}, bf16[128,2048]{1,0:T(8,128)(2,1)S(1)}, u32[]{:S(2)}, u32[]{:S(2)}) collective-permute-start(bf16[128,2048]{1,0:T(8,128)(2,1)S(1)} %collective-permute-done.10.oa.refs_14_), channel_id=1, source_target_pairs={{0,1},{1,0},{2,3},{3,2},{4,5},{5,4},{6,7},{7,6},{8,9},{9,8},{10,11... | collective-permute-start | bytes 1572872 | tf_op jit(solution)/shard_map/ppermute | solution.py:168
  30.9 12.2 %collective-permute-start.13 = (bf16[128,2048]{1,0:T(8,128)(2,1)S(1)}, bf16[128,2048]{1,0:T(8,128)(2,1)S(1)}, u32[]{:S(2)}, u32[]{:S(2)}) collective-permute-start(bf16[128,2048]{1,0:T(8,128)(2,1)S(1)} %collective-permute-done.10.oa.refs_14_), channel_id=1, source_target_pairs={{0,4},{4,8},{8,12},{12,14},{14,10},{10,6},{6,2},{2,0},{5,1},{9,5},... | collective-permute-start | bytes 1572872 | tf_op jit(solution)/shard_map/ppermute | solution.py:165
  36.4 11.6 %collective-permute-start.3 = (bf16[128,2176]{1,0:T(8,128)(2,1)S(1)}, bf16[128,2176]{1,0:T(8,128)(2,1)S(1)}, u32[]{:S(2)}, u32[]{:S(2)}) collective-permute-start(bf16[128,2176]{1,0:T(8,128)(2,1)S(1)} %collective-permute-done.2.xa.refs_6_), channel_id=1, source_target_pairs={{0,4},{4,8},{8,12},{12,14},{14,10},{10,6},{6,2},{2,0},{5,1},{9,5},... | collective-permute-start | bytes 1671176 | tf_op jit(solution)/shard_map/ppermute | solution.py:165
  38.6 15.0 %collective-permute-start.21 = (bf16[128,2048]{1,0:T(8,128)(2,1)S(1)}, bf16[128,2048]{1,0:T(8,128)(2,1)S(1)}, u32[]{:S(2)}, u32[]{:S(2)}) collective-permute-start(bf16[128,2048]{1,0:T(8,128)(2,1)S(1)} %add_convert_fusion.5), channel_id=1, source_target_pairs={{0,4},{4,8},{8,12},{12,14},{14,10},{10,6},{6,2},{2,0},{5,1},{9,5},... | collective-permute-start | bytes 1572872 | tf_op jit(solution)/shard_map/ppermute | solution.py:165
  43.0 12.7 %collective-permute-start.22 = (bf16[128,2048]{1,0:T(8,128)(2,1)S(1)}, bf16[128,2048]{1,0:T(8,128)(2,1)S(1)}, u32[]{:S(2)}, u32[]{:S(2)}) collective-permute-start(bf16[128,2048]{1,0:T(8,128)(2,1)S(1)} %get-tuple-element.74), channel_id=1, source_target_pairs={{0,1},{1,0},{2,3},{3,2},{4,5},{5,4},{6,7},{7,6},{8,9},{9,8},{10,11... | collective-permute-start | bytes 1572872 | tf_op jit(solution)/shard_map/ppermute | solution.py:168
  43.1 14.5 %collective-permute-start.18 = (bf16[128,2176]{1,0:T(8,128)(2,1)S(1)}, bf16[128,2176]{1,0:T(8,128)(2,1)S(1)}, u32[]{:S(2)}, u32[]{:S(2)}) collective-permute-start(bf16[128,2176]{1,0:T(8,128)(2,1)S(1)} %collective-permute-done.2.xa.refs_6_), channel_id=1, source_target_pairs={{0,1},{1,0},{2,3},{3,2},{4,5},{5,4},{6,7},{7,6},{8,9},{9,8},{10,11... | collective-permute-start | bytes 1671176 | tf_op jit(solution)/shard_map/ppermute | solution.py:168
  43.6 14.0 %collective-permute-start.19 = (bf16[128,2048]{1,0:T(8,128)(2,1)S(1)}, bf16[128,2048]{1,0:T(8,128)(2,1)S(1)}, u32[]{:S(2)}, u32[]{:S(2)}) collective-permute-start(bf16[128,2048]{1,0:T(8,128)(2,1)S(1)} %collective-permute-done.13.oa.refs_16_), channel_id=1, source_target_pairs={{0,1},{1,0},{2,3},{3,2},{4,5},{5,4},{6,7},{7,6},{8,9},{9,8},{10,11... | collective-permute-start | bytes 1572872 | tf_op jit(solution)/shard_map/ppermute | solution.py:168
  48.0 12.4 %collective-permute-start.16 = (bf16[128,2048]{1,0:T(8,128)(2,1)S(1)}, bf16[128,2048]{1,0:T(8,128)(2,1)S(1)}, u32[]{:S(2)}, u32[]{:S(2)}) collective-permute-start(bf16[128,2048]{1,0:T(8,128)(2,1)S(1)} %collective-permute-done.13.oa.refs_16_), channel_id=1, source_target_pairs={{0,4},{4,8},{8,12},{12,14},{14,10},{10,6},{6,2},{2,0},{5,1},{9,5},... | collective-permute-start | bytes 1572872 | tf_op jit(solution)/shard_map/ppermute | solution.py:165
  53.6 11.6 %collective-permute-start.4 = (bf16[128,2176]{1,0:T(8,128)(2,1)S(1)}, bf16[128,2176]{1,0:T(8,128)(2,1)S(1)}, u32[]{:S(2)}, u32[]{:S(2)}) collective-permute-start(bf16[128,2176]{1,0:T(8,128)(2,1)S(1)} %collective-permute-done.3.xa.refs_8_), channel_id=1, source_target_pairs={{0,4},{4,8},{8,12},{12,14},{14,10},{10,6},{6,2},{2,0},{5,1},{9,5},... | collective-permute-start | bytes 1671176 | tf_op jit(solution)/shard_map/ppermute | solution.py:165
  55.9 14.9 %collective-permute-start.26 = (bf16[128,2048]{1,0:T(8,128)(2,1)S(1)}, bf16[128,2048]{1,0:T(8,128)(2,1)S(1)}, u32[]{:S(2)}, u32[]{:S(2)}) collective-permute-start(bf16[128,2048]{1,0:T(8,128)(2,1)S(1)} %add_convert_fusion.4), channel_id=1, source_target_pairs={{0,4},{4,8},{8,12},{12,14},{14,10},{10,6},{6,2},{2,0},{5,1},{9,5},... | collective-permute-start | bytes 1572872 | tf_op jit(solution)/shard_map/ppermute | solution.py:165
  60.3 12.5 %collective-permute-start.27 = (bf16[128,2048]{1,0:T(8,128)(2,1)S(1)}, bf16[128,2048]{1,0:T(8,128)(2,1)S(1)}, u32[]{:S(2)}, u32[]{:S(2)}) collective-permute-start(bf16[128,2048]{1,0:T(8,128)(2,1)S(1)} %get-tuple-element.78), channel_id=1, source_target_pairs={{0,1},{1,0},{2,3},{3,2},{4,5},{5,4},{6,7},{7,6},{8,9},{9,8},{10,11... | collective-permute-start | bytes 1572872 | tf_op jit(solution)/shard_map/ppermute | solution.py:168
  60.4 14.5 %collective-permute-start.23 = (bf16[128,2176]{1,0:T(8,128)(2,1)S(1)}, bf16[128,2176]{1,0:T(8,128)(2,1)S(1)}, u32[]{:S(2)}, u32[]{:S(2)}) collective-permute-start(bf16[128,2176]{1,0:T(8,128)(2,1)S(1)} %collective-permute-done.3.xa.refs_8_), channel_id=1, source_target_pairs={{0,1},{1,0},{2,3},{3,2},{4,5},{5,4},{6,7},{7,6},{8,9},{9,8},{10,11... | collective-permute-start | bytes 1671176 | tf_op jit(solution)/shard_map/ppermute | solution.py:168
  60.9 14.0 %collective-permute-start.24 = (bf16[128,2048]{1,0:T(8,128)(2,1)S(1)}, bf16[128,2048]{1,0:T(8,128)(2,1)S(1)}, u32[]{:S(2)}, u32[]{:S(2)}) collective-permute-start(bf16[128,2048]{1,0:T(8,128)(2,1)S(1)} %collective-permute-done.16.oa.refs_18_), channel_id=1, source_target_pairs={{0,1},{1,0},{2,3},{3,2},{4,5},{5,4},{6,7},{7,6},{8,9},{9,8},{10,11... | collective-permute-start | bytes 1572872 | tf_op jit(solution)/shard_map/ppermute | solution.py:168
  65.2 12.6 %collective-permute-start.20 = (bf16[128,2048]{1,0:T(8,128)(2,1)S(1)}, bf16[128,2048]{1,0:T(8,128)(2,1)S(1)}, u32[]{:S(2)}, u32[]{:S(2)}) collective-permute-start(bf16[128,2048]{1,0:T(8,128)(2,1)S(1)} %collective-permute-done.16.oa.refs_18_), channel_id=1, source_target_pairs={{0,4},{4,8},{8,12},{12,14},{14,10},{10,6},{6,2},{2,0},{5,1},{9,5},... | collective-permute-start | bytes 1572872 | tf_op jit(solution)/shard_map/ppermute | solution.py:165
  70.8 11.6 %collective-permute-start.5 = (bf16[128,2176]{1,0:T(8,128)(2,1)S(1)}, bf16[128,2176]{1,0:T(8,128)(2,1)S(1)}, u32[]{:S(2)}, u32[]{:S(2)}) collective-permute-start(bf16[128,2176]{1,0:T(8,128)(2,1)S(1)} %collective-permute-done.4.xa.refs_0_), channel_id=1, source_target_pairs={{0,4},{4,8},{8,12},{12,14},{14,10},{10,6},{6,2},{2,0},{5,1},{9,5},... | collective-permute-start | bytes 1671176 | tf_op jit(solution)/shard_map/ppermute | solution.py:165
  73.1 14.9 %collective-permute-start.31 = (bf16[128,2048]{1,0:T(8,128)(2,1)S(1)}, bf16[128,2048]{1,0:T(8,128)(2,1)S(1)}, u32[]{:S(2)}, u32[]{:S(2)}) collective-permute-start(bf16[128,2048]{1,0:T(8,128)(2,1)S(1)} %add_convert_fusion.3), channel_id=1, source_target_pairs={{0,4},{4,8},{8,12},{12,14},{14,10},{10,6},{6,2},{2,0},{5,1},{9,5},... | collective-permute-start | bytes 1572872 | tf_op jit(solution)/shard_map/ppermute | solution.py:165
  77.7 12.4 %collective-permute-start.32 = (bf16[128,2048]{1,0:T(8,128)(2,1)S(1)}, bf16[128,2048]{1,0:T(8,128)(2,1)S(1)}, u32[]{:S(2)}, u32[]{:S(2)}) collective-permute-start(bf16[128,2048]{1,0:T(8,128)(2,1)S(1)} %get-tuple-element.82), channel_id=1, source_target_pairs={{0,1},{1,0},{2,3},{3,2},{4,5},{5,4},{6,7},{7,6},{8,9},{9,8},{10,11... | collective-permute-start | bytes 1572872 | tf_op jit(solution)/shard_map/ppermute | solution.py:168
  77.8 16.3 %collective-permute-start.28 = (bf16[128,2176]{1,0:T(8,128)(2,1)S(1)}, bf16[128,2176]{1,0:T(8,128)(2,1)S(1)}, u32[]{:S(2)}, u32[]{:S(2)}) collective-permute-start(bf16[128,2176]{1,0:T(8,128)(2,1)S(1)} %collective-permute-done.4.xa.refs_0_), channel_id=1, source_target_pairs={{0,1},{1,0},{2,3},{3,2},{4,5},{5,4},{6,7},{7,6},{8,9},{9,8},{10,11... | collective-permute-start | bytes 1671176 | tf_op jit(solution)/shard_map/ppermute | solution.py:168
  78.3 15.3 %collective-permute-start.25 = (bf16[128,2048]{1,0:T(8,128)(2,1)S(1)}, bf16[128,2048]{1,0:T(8,128)(2,1)S(1)}, u32[]{:S(2)}, u32[]{:S(2)}) collective-permute-start(bf16[128,2048]{1,0:T(8,128)(2,1)S(1)} %collective-permute-done.20.oa.refs_6_), channel_id=1, source_target_pairs={{0,4},{4,8},{8,12},{12,14},{14,10},{10,6},{6,2},{2,0},{5,1},{9,5},... | collective-permute-start | bytes 1572872 | tf_op jit(solution)/shard_map/ppermute | solution.py:165
  82.4 11.2 %collective-permute-start.29 = (bf16[128,2048]{1,0:T(8,128)(2,1)S(1)}, bf16[128,2048]{1,0:T(8,128)(2,1)S(1)}, u32[]{:S(2)}, u32[]{:S(2)}) collective-permute-start(bf16[128,2048]{1,0:T(8,128)(2,1)S(1)} %collective-permute-done.20.oa.refs_6_), channel_id=1, source_target_pairs={{0,1},{1,0},{2,3},{3,2},{4,5},{5,4},{6,7},{7,6},{8,9},{9,8},{10,11... | collective-permute-start | bytes 1572872 | tf_op jit(solution)/shard_map/ppermute | solution.py:168
  88.0 20.4 %collective-permute-start.6 = (bf16[128,2176]{1,0:T(8,128)(2,1)S(1)}, bf16[128,2176]{1,0:T(8,128)(2,1)S(1)}, u32[]{:S(2)}, u32[]{:S(2)}) collective-permute-start(bf16[128,2176]{1,0:T(8,128)(2,1)S(1)} %collective-permute-done.5.xa.refs_2_), channel_id=1, source_target_pairs={{0,4},{4,8},{8,12},{12,14},{14,10},{10,6},{6,2},{2,0},{5,1},{9,5},... | collective-permute-start | bytes 1671176 | tf_op jit(solution)/shard_map/ppermute | solution.py:165
  90.3 16.0 %collective-permute-start.33 = (bf16[128,2048]{1,0:T(8,128)(2,1)S(1)}, bf16[128,2048]{1,0:T(8,128)(2,1)S(1)}, u32[]{:S(2)}, u32[]{:S(2)}) collective-permute-start(bf16[128,2048]{1,0:T(8,128)(2,1)S(1)} %add_convert_fusion.2), channel_id=1, source_target_pairs={{0,4},{4,8},{8,12},{12,14},{14,10},{10,6},{6,2},{2,0},{5,1},{9,5},... | collective-permute-start | bytes 1572872 | tf_op jit(solution)/shard_map/ppermute | solution.py:165
  93.6 17.7 %collective-permute-start.38 = (bf16[128,2176]{1,0:T(8,128)(2,1)S(1)}, bf16[128,2176]{1,0:T(8,128)(2,1)S(1)}, u32[]{:S(2)}, u32[]{:S(2)}) collective-permute-start(bf16[128,2176]{1,0:T(8,128)(2,1)S(1)} %collective-permute-done.5.xa.refs_2_), channel_id=1, source_target_pairs={{0,1},{1,0},{2,3},{3,2},{4,5},{5,4},{6,7},{7,6},{8,9},{9,8},{10,11... | collective-permute-start | bytes 1671176 | tf_op jit(solution)/shard_map/ppermute | solution.py:168
  93.6 3.4 %collective-permute-start.39 = (bf16[128,2048]{1,0:T(8,128)(2,1)S(1)}, bf16[128,2048]{1,0:T(8,128)(2,1)S(1)}, u32[]{:S(2)}, u32[]{:S(2)}) collective-permute-start(bf16[128,2048]{1,0:T(8,128)(2,1)S(1)} %collective-permute-done.25.oa.refs_8_), channel_id=1, source_target_pairs={{0,1},{1,0},{2,3},{3,2},{4,5},{5,4},{6,7},{7,6},{8,9},{9,8},{10,11... | collective-permute-start | bytes 1572872 | tf_op jit(solution)/shard_map/ppermute | solution.py:168
  96.9 9.6 %collective-permute-start.34 = (bf16[128,2048]{1,0:T(8,128)(2,1)S(1)}, bf16[128,2048]{1,0:T(8,128)(2,1)S(1)}, u32[]{:S(2)}, u32[]{:S(2)}) collective-permute-start(bf16[128,2048]{1,0:T(8,128)(2,1)S(1)} %get-tuple-element.86), channel_id=1, source_target_pairs={{0,1},{1,0},{2,3},{3,2},{4,5},{5,4},{6,7},{7,6},{8,9},{9,8},{10,11... | collective-permute-start | bytes 1572872 | tf_op jit(solution)/shard_map/ppermute | solution.py:168
  97.0 13.8 %collective-permute-start.30 = (bf16[128,2048]{1,0:T(8,128)(2,1)S(1)}, bf16[128,2048]{1,0:T(8,128)(2,1)S(1)}, u32[]{:S(2)}, u32[]{:S(2)}) collective-permute-start(bf16[128,2048]{1,0:T(8,128)(2,1)S(1)} %collective-permute-done.25.oa.refs_8_), channel_id=1, source_target_pairs={{0,4},{4,8},{8,12},{12,14},{14,10},{10,6},{6,2},{2,0},{5,1},{9,5},... | collective-permute-start | bytes 1572872 | tf_op jit(solution)/shard_map/ppermute | solution.py:165
  106.4 28.6 %collective-permute-start.46 = (bf16[128,2048]{1,0:T(8,128)(2,1)S(1)}, bf16[128,2048]{1,0:T(8,128)(2,1)S(1)}, u32[]{:S(2)}, u32[]{:S(2)}) collective-permute-start(bf16[128,2048]{1,0:T(8,128)(2,1)S(1)} %get-tuple-element.68), channel_id=1, source_target_pairs={{0,1},{1,0},{2,3},{3,2},{4,5},{5,4},{6,7},{7,6},{8,9},{9,8},{10,11... | collective-permute-start | bytes 1572872 | tf_op jit(solution)/shard_map/ppermute | solution.py:168
  106.8 10.2 %collective-permute-start.37 = (bf16[128,2048]{1,0:T(8,128)(2,1)S(1)}, bf16[128,2048]{1,0:T(8,128)(2,1)S(1)}, u32[]{:S(2)}, u32[]{:S(2)}) collective-permute-start(bf16[128,2048]{1,0:T(8,128)(2,1)S(1)} %add_convert_fusion.1), channel_id=1, source_target_pairs={{0,4},{4,8},{8,12},{12,14},{14,10},{10,6},{6,2},{2,0},{5,1},{9,5},... | collective-permute-start | bytes 1572872 | tf_op jit(solution)/shard_map/ppermute | solution.py:165
  110.8 3.4 %collective-permute-start.35 = (bf16[128,2176]{1,0:T(8,128)(2,1)S(1)}, bf16[128,2176]{1,0:T(8,128)(2,1)S(1)}, u32[]{:S(2)}, u32[]{:S(2)}) collective-permute-start(bf16[128,2176]{1,0:T(8,128)(2,1)S(1)} %collective-permute-done.6.xa.refs_4_), channel_id=1, source_target_pairs={{0,1},{1,0},{2,3},{3,2},{4,5},{5,4},{6,7},{7,6},{8,9},{9,8},{10,11... | collective-permute-start | bytes 1671176 | tf_op jit(solution)/shard_map/ppermute | solution.py:168
  110.8 3.4 %collective-permute-start.36 = (bf16[128,2048]{1,0:T(8,128)(2,1)S(1)}, bf16[128,2048]{1,0:T(8,128)(2,1)S(1)}, u32[]{:S(2)}, u32[]{:S(2)}) collective-permute-start(bf16[128,2048]{1,0:T(8,128)(2,1)S(1)} %collective-permute-done.30.oa.refs_10_), channel_id=1, source_target_pairs={{0,1},{1,0},{2,3},{3,2},{4,5},{5,4},{6,7},{7,6},{8,9},{9,8},{10,11... | collective-permute-start | bytes 1572872 | tf_op jit(solution)/shard_map/ppermute | solution.py:168
  114.1 3.4 %collective-permute-start.40 = (bf16[128,2048]{1,0:T(8,128)(2,1)S(1)}, bf16[128,2048]{1,0:T(8,128)(2,1)S(1)}, u32[]{:S(2)}, u32[]{:S(2)}) collective-permute-start(bf16[128,2048]{1,0:T(8,128)(2,1)S(1)} %get-tuple-element.110), channel_id=1, source_target_pairs={{0,1},{1,0},{2,3},{3,2},{4,5},{5,4},{6,7},{7,6},{8,9},{9,8},{10,11... | collective-permute-start | bytes 1572872 | tf_op jit(solution)/shard_map/ppermute | solution.py:168
  117.0 4.5 %collective-permute-start.42 = (bf16[128,2048]{1,0:T(8,128)(2,1)S(1)}, bf16[128,2048]{1,0:T(8,128)(2,1)S(1)}, u32[]{:S(2)}, u32[]{:S(2)}) collective-permute-start(bf16[128,2048]{1,0:T(8,128)(2,1)S(1)} %get-tuple-element.112), channel_id=1, source_target_pairs={{0,1},{1,0},{2,3},{3,2},{4,5},{5,4},{6,7},{7,6},{8,9},{9,8},{10,11... | collective-permute-start | bytes 1572872 | tf_op jit(solution)/shard_map/ppermute | solution.py:168
  117.8 6.4 %collective-permute-start.41 = (bf16[64,2048]{1,0:T(8,128)(2,1)S(1)}, bf16[64,2048]{1,0:T(8,128)(2,1)S(1)}, u32[]{:S(2)}, u32[]{:S(2)}) collective-permute-start(bf16[64,2048]{1,0:T(8,128)(2,1)S(1)} %get-tuple-element.124), channel_id=1, source_target_pairs={{0,4},{4,8},{8,12},{12,14},{14,10},{10,6},{6,2},{2,0},{5,1},{9,5},... | collective-permute-start | bytes 786440 | tf_op jit(solution)/shard_map/ppermute | solution.py:165
  120.0 7.1 %collective-permute-start.44 = (bf16[64,2048]{1,0:T(8,128)(2,1)S(1)}, bf16[64,2048]{1,0:T(8,128)(2,1)S(1)}, u32[]{:S(2)}, u32[]{:S(2)}) collective-permute-start(bf16[64,2048]{1,0:T(8,128)(2,1)S(1)} %get-tuple-element.125), channel_id=1, source_target_pairs={{0,4},{4,8},{8,12},{12,14},{14,10},{10,6},{6,2},{2,0},{5,1},{9,5},... | collective-permute-start | bytes 786440 | tf_op jit(solution)/shard_map/ppermute | solution.py:165
  124.3 10.7 %collective-permute-start.43 = (bf16[64,2048]{1,0:T(8,128)(2,1)S(1)}, bf16[64,2048]{1,0:T(8,128)(2,1)S(1)}, u32[]{:S(2)}, u32[]{:S(2)}) collective-permute-start(bf16[64,2048]{1,0:T(8,128)(2,1)S(1)} %fusion.4), channel_id=1, source_target_pairs={{0,4},{4,8},{8,12},{12,14},{14,10},{10,6},{6,2},{2,0},{5,1},{9,5},... | collective-permute-start | bytes 786440 | tf_op jit(solution)/shard_map/ppermute | solution.py:165
  127.1 7.9 %collective-permute-start.45 = (bf16[64,2048]{1,0:T(8,128)(2,1)S(1)}, bf16[64,2048]{1,0:T(8,128)(2,1)S(1)}, u32[]{:S(2)}, u32[]{:S(2)}) collective-permute-start(bf16[64,2048]{1,0:T(8,128)(2,1)S(1)} %fusion.2), channel_id=1, source_target_pairs={{0,4},{4,8},{8,12},{12,14},{14,10},{10,6},{6,2},{2,0},{5,1},{9,5},... | collective-permute-start | bytes 786440 | tf_op jit(solution)/shard_map/ppermute | solution.py:165

commit v5 on v4

--- a/solution.py
+++ b/solution.py
@@ -21,7 +21,7 @@
 BLOCK_COST = 16
 WGRAD_COST = 1
 BLOCK_VMEM = 16 << 20
-WGRAD_VMEM = 24 << 20
+WGRAD_VMEM = 28 << 20
 
 
 def mm(a, b, dims):
@@ -90,7 +90,7 @@
     count, pairs = len(xs), len(grads)
     rows, width = os[0].shape
     ff = hiddens[0].shape[1]
-    chunk = 512 if resident else 256
+    chunk = 1024 if resident else 256
     has = acc is not None
 
     def body(*refs):

time: 136 us -> 136 us (level)
  starting transfers between devices: 50.6 us -> 49.1 us
  transfers between devices with their start and end apart: 47 -> 47, of which waited for: 15 -> 15; matrix products, arithmetic and copies ran while one was open for 3% -> 4% of each run, Pallas kernels for 26% -> 27%
where the time goes in v5:
time: 136 us
  starting transfers between devices  49.1 us (36%)
  waiting for transfers between devices  41.4 us (30%)
  Pallas kernels  36.2 us (27%)
  other arithmetic  7.73 us (6%)
    ppermute x23, starting transfers between devices, forward(): return lax.ppermute(v, 'expert', hop)  44.1 us
    ppermute x23, waiting for transfers between devices, forward(): return lax.ppermute(v, 'expert', hop)  41.3 us
    pallas_call x8, Pallas kernels, block_pair(): pl.pallas_call(body, in_specs=[pl.BlockSpec(memory_space=pltpu.SMEM)] + [...  23.2 us
    pallas_call x2, Pallas kernels, wgrad_group(): pl.pallas_call(body, grid=(width // chunk,), in_specs=specs + (acc_specs...  13 us
    ppermute x24, starting transfers between devices, other(): return lax.ppermute(v, 'expert', swap)  4.96 us
  transfers between devices with their start and end apart: 47, of which 15 were waited for; matrix products, arithmetic and copies ran while one was open for 4% of the time, Pallas kernels for 27%

profile of v5, /device:TPU:0, one launch (start us, length us, event | category | flops | bytes accessed | tf_op | source)
XLA Modules:
  0.0 135.5 jit_solution(11323686290841839745)
XLA Ops:
  0.6 0.7 select_reduce_fusion
  1.5 1.1 fusion.1.xa.refs_0_
  2.6 0.5 collective-permute-start.7
  3.1 2.6 %collective-permute-start = (bf16[128,2176]{1,0:T(8,128)(2,1)S(1)}, bf16[128,2176]{1,0:T(8,128)(2,1)S(1)}, u32[]{:S(2)}, u32[]{:S(2)}) collective-permute-start(bf16[128,2176]{1,0:T(8,128)(2,1)S(1)} %fusion.1.xa.refs_0_), channel_id=1, source_target_pairs={{0,4},{4,8},{8,12},{12,14},{14,10},{10,6},{6,2},{2,0},{5,1},{9,5},... | collective-permute-start | bytes 1671176 | tf_op jit(solution)/shard_map/ppermute | solution.py:165
  5.9 2.3 %pad_maximum_fusion.wgu = bf16[2048,768]{1,0:T(8,128)(2,1)S(1)} fusion(bf16[2048,384]{1,0:T(8,128)(2,1)} %bitcast.15, bf16[2048,384]{1,0:T(8,128)(2,1)} %bitcast.16), kind=kLoop, calls=%fused_computation | loop fusion | flops 6291456 | bytes 6291456 | tf_op jit(solution)/shard_map/concatenate | solution.py:209
  8.2 1.8 %collective-permute-start.8 = (bf16[128,2048]{1,0:T(8,128)(2,1)S(1)}, bf16[128,2048]{1,0:T(8,128)(2,1)S(1)}, u32[]{:S(2)}, u32[]{:S(2)}) collective-permute-start(bf16[128,2048]{1,0:T(8,128)(2,1)S(1)} %copy-done.1), channel_id=1, source_target_pairs={{0,4},{4,8},{8,12},{12,14},{14,10},{10,6},{6,2},{2,0},{5,1},{9,5},... | collective-permute-start | bytes 1572872 | tf_op jit(solution)/shard_map/ppermute | solution.py:165
  10.0 3.2 %collective-permute-done.xa.refs_2_ = bf16[128,2176]{1,0:T(8,128)(2,1)S(1)} collective-permute-done((bf16[128,2176]{1,0:T(8,128)(2,1)S(1)}, bf16[128,2176]{1,0:T(8,128)(2,1)S(1)}, u32[]{:S(2)}, u32[]{:S(2)}) %collective-permute-start) | collective-permute-done | bytes 557088 | tf_op jit(solution)/shard_map/ppermute | solution.py:165
  13.2 2.1 %collective-permute-start.1 = (bf16[128,2176]{1,0:T(8,128)(2,1)S(1)}, bf16[128,2176]{1,0:T(8,128)(2,1)S(1)}, u32[]{:S(2)}, u32[]{:S(2)}) collective-permute-start(bf16[128,2176]{1,0:T(8,128)(2,1)S(1)} %collective-permute-done.xa.refs_2_), channel_id=1, source_target_pairs={{0,4},{4,8},{8,12},{12,14},{14,10},{10,6},{6,2},{2,0},{5,1},{9,5},... | collective-permute-start | bytes 1671176 | tf_op jit(solution)/shard_map/ppermute | solution.py:165
  15.3 3.8 %block_pair.8 = (bf16[128,2048]{1,0:T(8,128)(2,1)S(1)}, bf16[128,2048]{1,0:T(8,128)(2,1)S(1)}, bf16[256,768]{1,0:T(8,128)(2,1)S(1)}, bf16[256,384]{1,0:T(8,128)(2,1)S(1)}) custom-call(s32[1]{0:T(128)} %bitcast.me, bf16[128,2176]{1,0:T(8,128)(2,1)S(1)} %fusion.1.xa.refs_0_, bf16[128,2176]{1,0:T(8,128)(2,1)S(1)} %collective-permute-done.7.xb.refs_1_, ...), custom_call_target="tpu_custom_call" | custom-call | flops 32212254720 | bytes 7864320 | tf_op jit(solution)/shard_map/block_pair/pallas_call | solution.py:69
  19.2 0.5 collective-permute-start.12
  19.7 1.7 %collective-permute-start.10 = (bf16[128,2048]{1,0:T(8,128)(2,1)S(1)}, bf16[128,2048]{1,0:T(8,128)(2,1)S(1)}, u32[]{:S(2)}, u32[]{:S(2)}) collective-permute-start(bf16[128,2048]{1,0:T(8,128)(2,1)S(1)} %collective-permute-done.8.oa.refs_12_), channel_id=1, source_target_pairs={{0,4},{4,8},{8,12},{12,14},{14,10},{10,6},{6,2},{2,0},{5,1},{9,5},... | collective-permute-start | bytes 1572872 | tf_op jit(solution)/shard_map/ppermute | solution.py:165
  21.4 3.4 %collective-permute-done.1.xa.refs_4_ = bf16[128,2176]{1,0:T(8,128)(2,1)S(1)} collective-permute-done((bf16[128,2176]{1,0:T(8,128)(2,1)S(1)}, bf16[128,2176]{1,0:T(8,128)(2,1)S(1)}, u32[]{:S(2)}, u32[]{:S(2)}) %collective-permute-start.1) | collective-permute-done | bytes 557088 | tf_op jit(solution)/shard_map/ppermute | solution.py:165
  24.8 2.1 %collective-permute-start.2 = (bf16[128,2176]{1,0:T(8,128)(2,1)S(1)}, bf16[128,2176]{1,0:T(8,128)(2,1)S(1)}, u32[]{:S(2)}, u32[]{:S(2)}) collective-permute-start(bf16[128,2176]{1,0:T(8,128)(2,1)S(1)} %collective-permute-done.1.xa.refs_4_), channel_id=1, source_target_pairs={{0,4},{4,8},{8,12},{12,14},{14,10},{10,6},{6,2},{2,0},{5,1},{9,5},... | collective-permute-start | bytes 1671176 | tf_op jit(solution)/shard_map/ppermute | solution.py:165
  26.9 2.8 %block_pair.9 = (bf16[128,2048]{1,0:T(8,128)(2,1)S(1)}, bf16[128,2048]{1,0:T(8,128)(2,1)S(1)}, bf16[256,768]{1,0:T(8,128)(2,1)S(1)}, bf16[256,384]{1,0:T(8,128)(2,1)S(1)}) custom-call(s32[1]{0:T(128)} %bitcast.me, bf16[128,2176]{1,0:T(8,128)(2,1)S(1)} %collective-permute-done.xa.refs_2_, bf16[128,2176]{1,0:T(8,128)(2,1)S(1)} %collective-permute-done.11.xb.refs_3_, ...), custom_call_target="tpu_custom_call" | custom-call | flops 32212254720 | bytes 7864320 | tf_op jit(solution)/shard_map/block_pair/pallas_call | solution.py:69
  29.7 0.7 collective-permute-done.10.oa.refs_14_
  30.4 0.5 collective-permute-start.15
  30.9 2.1 %collective-permute-start.13 = (bf16[128,2048]{1,0:T(8,128)(2,1)S(1)}, bf16[128,2048]{1,0:T(8,128)(2,1)S(1)}, u32[]{:S(2)}, u32[]{:S(2)}) collective-permute-start(bf16[128,2048]{1,0:T(8,128)(2,1)S(1)} %collective-permute-done.10.oa.refs_14_), channel_id=1, source_target_pairs={{0,4},{4,8},{8,12},{12,14},{14,10},{10,6},{6,2},{2,0},{5,1},{9,5},... | collective-permute-start | bytes 1572872 | tf_op jit(solution)/shard_map/ppermute | solution.py:165
  33.0 3.4 %collective-permute-done.2.xa.refs_6_ = bf16[128,2176]{1,0:T(8,128)(2,1)S(1)} collective-permute-done((bf16[128,2176]{1,0:T(8,128)(2,1)S(1)}, bf16[128,2176]{1,0:T(8,128)(2,1)S(1)}, u32[]{:S(2)}, u32[]{:S(2)}) %collective-permute-start.2) | collective-permute-done | bytes 557088 | tf_op jit(solution)/shard_map/ppermute | solution.py:165
  36.4 2.1 %collective-permute-start.3 = (bf16[128,2176]{1,0:T(8,128)(2,1)S(1)}, bf16[128,2176]{1,0:T(8,128)(2,1)S(1)}, u32[]{:S(2)}, u32[]{:S(2)}) collective-permute-start(bf16[128,2176]{1,0:T(8,128)(2,1)S(1)} %collective-permute-done.2.xa.refs_6_), channel_id=1, source_target_pairs={{0,4},{4,8},{8,12},{12,14},{14,10},{10,6},{6,2},{2,0},{5,1},{9,5},... | collective-permute-start | bytes 1671176 | tf_op jit(solution)/shard_map/ppermute | solution.py:165
  38.6 1.6 %collective-permute-start.21 = (bf16[128,2048]{1,0:T(8,128)(2,1)S(1)}, bf16[128,2048]{1,0:T(8,128)(2,1)S(1)}, u32[]{:S(2)}, u32[]{:S(2)}) collective-permute-start(bf16[128,2048]{1,0:T(8,128)(2,1)S(1)} %add_convert_fusion.5), channel_id=1, source_target_pairs={{0,4},{4,8},{8,12},{12,14},{14,10},{10,6},{6,2},{2,0},{5,1},{9,5},... | collective-permute-start | bytes 1572872 | tf_op jit(solution)/shard_map/ppermute | solution.py:165
  40.2 2.8 %block_pair.10 = (bf16[128,2048]{1,0:T(8,128)(2,1)S(1)}, bf16[128,2048]{1,0:T(8,128)(2,1)S(1)}, bf16[256,768]{1,0:T(8,128)(2,1)S(1)}, bf16[256,384]{1,0:T(8,128)(2,1)S(1)}) custom-call(s32[1]{0:T(128)} %bitcast.me, bf16[128,2176]{1,0:T(8,128)(2,1)S(1)} %collective-permute-done.1.xa.refs_4_, bf16[128,2176]{1,0:T(8,128)(2,1)S(1)} %collective-permute-done.14.xb.refs_5_, ...), custom_call_target="tpu_custom_call" | custom-call | flops 32212254720 | bytes 7864320 | tf_op jit(solution)/shard_map/block_pair/pallas_call | solution.py:69
  43.1 0.5 collective-permute-start.18
  43.7 4.3 %collective-permute-done.3.xa.refs_8_ = bf16[128,2176]{1,0:T(8,128)(2,1)S(1)} collective-permute-done((bf16[128,2176]{1,0:T(8,128)(2,1)S(1)}, bf16[128,2176]{1,0:T(8,128)(2,1)S(1)}, u32[]{:S(2)}, u32[]{:S(2)}) %collective-permute-start.3) | collective-permute-done | bytes 557088 | tf_op jit(solution)/shard_map/ppermute | solution.py:165
  48.0 2.1 %collective-permute-start.16 = (bf16[128,2048]{1,0:T(8,128)(2,1)S(1)}, bf16[128,2048]{1,0:T(8,128)(2,1)S(1)}, u32[]{:S(2)}, u32[]{:S(2)}) collective-permute-start(bf16[128,2048]{1,0:T(8,128)(2,1)S(1)} %collective-permute-done.13.oa.refs_16_), channel_id=1, source_target_pairs={{0,4},{4,8},{8,12},{12,14},{14,10},{10,6},{6,2},{2,0},{5,1},{9,5},... | collective-permute-start | bytes 1572872 | tf_op jit(solution)/shard_map/ppermute | solution.py:165
  50.0 3.5 %collective-permute-done.21 = bf16[128,2048]{1,0:T(8,128)(2,1)S(1)} collective-permute-done((bf16[128,2048]{1,0:T(8,128)(2,1)S(1)}, bf16[128,2048]{1,0:T(8,128)(2,1)S(1)}, u32[]{:S(2)}, u32[]{:S(2)}) %collective-permute-start.21) | collective-permute-done | bytes 524320 | tf_op jit(solution)/shard_map/ppermute | solution.py:165
  53.6 2.1 %collective-permute-start.4 = (bf16[128,2176]{1,0:T(8,128)(2,1)S(1)}, bf16[128,2176]{1,0:T(8,128)(2,1)S(1)}, u32[]{:S(2)}, u32[]{:S(2)}) collective-permute-start(bf16[128,2176]{1,0:T(8,128)(2,1)S(1)} %collective-permute-done.3.xa.refs_8_), channel_id=1, source_target_pairs={{0,4},{4,8},{8,12},{12,14},{14,10},{10,6},{6,2},{2,0},{5,1},{9,5},... | collective-permute-start | bytes 1671176 | tf_op jit(solution)/shard_map/ppermute | solution.py:165
  55.7 0.2 add_convert_fusion.4
  55.9 1.6 %collective-permute-start.26 = (bf16[128,2048]{1,0:T(8,128)(2,1)S(1)}, bf16[128,2048]{1,0:T(8,128)(2,1)S(1)}, u32[]{:S(2)}, u32[]{:S(2)}) collective-permute-start(bf16[128,2048]{1,0:T(8,128)(2,1)S(1)} %add_convert_fusion.4), channel_id=1, source_target_pairs={{0,4},{4,8},{8,12},{12,14},{14,10},{10,6},{6,2},{2,0},{5,1},{9,5},... | collective-permute-start | bytes 1572872 | tf_op jit(solution)/shard_map/ppermute | solution.py:165
  57.5 2.8 %block_pair.11 = (bf16[128,2048]{1,0:T(8,128)(2,1)S(1)}, bf16[128,2048]{1,0:T(8,128)(2,1)S(1)}, bf16[256,768]{1,0:T(8,128)(2,1)S(1)}, bf16[256,384]{1,0:T(8,128)(2,1)S(1)}) custom-call(s32[1]{0:T(128)} %bitcast.me, bf16[128,2176]{1,0:T(8,128)(2,1)S(1)} %collective-permute-done.2.xa.refs_6_, bf16[128,2176]{1,0:T(8,128)(2,1)S(1)} %collective-permute-done.18.xb.refs_7_, ...), custom_call_target="tpu_custom_call" | custom-call | flops 32212254720 | bytes 7864320 | tf_op jit(solution)/shard_map/block_pair/pallas_call | solution.py:69
  60.4 0.5 collective-permute-start.23
  61.0 4.2 %collective-permute-done.4.xa.refs_0_ = bf16[128,2176]{1,0:T(8,128)(2,1)S(1)} collective-permute-done((bf16[128,2176]{1,0:T(8,128)(2,1)S(1)}, bf16[128,2176]{1,0:T(8,128)(2,1)S(1)}, u32[]{:S(2)}, u32[]{:S(2)}) %collective-permute-start.4) | collective-permute-done | bytes 557088 | tf_op jit(solution)/shard_map/ppermute | solution.py:165
  65.2 2.1 %collective-permute-start.20 = (bf16[128,2048]{1,0:T(8,128)(2,1)S(1)}, bf16[128,2048]{1,0:T(8,128)(2,1)S(1)}, u32[]{:S(2)}, u32[]{:S(2)}) collective-permute-start(bf16[128,2048]{1,0:T(8,128)(2,1)S(1)} %collective-permute-done.16.oa.refs_18_), channel_id=1, source_target_pairs={{0,4},{4,8},{8,12},{12,14},{14,10},{10,6},{6,2},{2,0},{5,1},{9,5},... | collective-permute-start | bytes 1572872 | tf_op jit(solution)/shard_map/ppermute | solution.py:165
  67.2 3.5 %collective-permute-done.26 = bf16[128,2048]{1,0:T(8,128)(2,1)S(1)} collective-permute-done((bf16[128,2048]{1,0:T(8,128)(2,1)S(1)}, bf16[128,2048]{1,0:T(8,128)(2,1)S(1)}, u32[]{:S(2)}, u32[]{:S(2)}) %collective-permute-start.26) | collective-permute-done | bytes 524320 | tf_op jit(solution)/shard_map/ppermute | solution.py:165
  70.8 2.1 %collective-permute-start.5 = (bf16[128,2176]{1,0:T(8,128)(2,1)S(1)}, bf16[128,2176]{1,0:T(8,128)(2,1)S(1)}, u32[]{:S(2)}, u32[]{:S(2)}) collective-permute-start(bf16[128,2176]{1,0:T(8,128)(2,1)S(1)} %collective-permute-done.4.xa.refs_0_), channel_id=1, source_target_pairs={{0,4},{4,8},{8,12},{12,14},{14,10},{10,6},{6,2},{2,0},{5,1},{9,5},... | collective-permute-start | bytes 1671176 | tf_op jit(solution)/shard_map/ppermute | solution.py:165
  72.9 0.2 add_convert_fusion.3
  73.1 1.8 %collective-permute-start.31 = (bf16[128,2048]{1,0:T(8,128)(2,1)S(1)}, bf16[128,2048]{1,0:T(8,128)(2,1)S(1)}, u32[]{:S(2)}, u32[]{:S(2)}) collective-permute-start(bf16[128,2048]{1,0:T(8,128)(2,1)S(1)} %add_convert_fusion.3), channel_id=1, source_target_pairs={{0,4},{4,8},{8,12},{12,14},{14,10},{10,6},{6,2},{2,0},{5,1},{9,5},... | collective-permute-start | bytes 1572872 | tf_op jit(solution)/shard_map/ppermute | solution.py:165
  74.9 2.8 %block_pair.12 = (bf16[128,2048]{1,0:T(8,128)(2,1)S(1)}, bf16[128,2048]{1,0:T(8,128)(2,1)S(1)}, bf16[256,768]{1,0:T(8,128)(2,1)S(1)}, bf16[256,384]{1,0:T(8,128)(2,1)S(1)}) custom-call(s32[1]{0:T(128)} %bitcast.me, bf16[128,2176]{1,0:T(8,128)(2,1)S(1)} %collective-permute-done.3.xa.refs_8_, bf16[128,2176]{1,0:T(8,128)(2,1)S(1)} %collective-permute-done.23.xb.refs_9_, ...), custom_call_target="tpu_custom_call" | custom-call | flops 32212254720 | bytes 7864320 | tf_op jit(solution)/shard_map/block_pair/pallas_call | solution.py:69
  77.8 0.5 collective-permute-start.28
  78.3 1.6 %collective-permute-start.25 = (bf16[128,2048]{1,0:T(8,128)(2,1)S(1)}, bf16[128,2048]{1,0:T(8,128)(2,1)S(1)}, u32[]{:S(2)}, u32[]{:S(2)}) collective-permute-start(bf16[128,2048]{1,0:T(8,128)(2,1)S(1)} %collective-permute-done.20.oa.refs_6_), channel_id=1, source_target_pairs={{0,4},{4,8},{8,12},{12,14},{14,10},{10,6},{6,2},{2,0},{5,1},{9,5},... | collective-permute-start | bytes 1572872 | tf_op jit(solution)/shard_map/ppermute | solution.py:165
  79.9 2.5 %collective-permute-done.5.xa.refs_2_ = bf16[128,2176]{1,0:T(8,128)(2,1)S(1)} collective-permute-done((bf16[128,2176]{1,0:T(8,128)(2,1)S(1)}, bf16[128,2176]{1,0:T(8,128)(2,1)S(1)}, u32[]{:S(2)}, u32[]{:S(2)}) %collective-permute-start.5) | collective-permute-done | bytes 557088 | tf_op jit(solution)/shard_map/ppermute | solution.py:165
  82.4 5.6 %collective-permute-done.31 = bf16[128,2048]{1,0:T(8,128)(2,1)S(1)} collective-permute-done((bf16[128,2048]{1,0:T(8,128)(2,1)S(1)}, bf16[128,2048]{1,0:T(8,128)(2,1)S(1)}, u32[]{:S(2)}, u32[]{:S(2)}) %collective-permute-start.31) | collective-permute-done | bytes 524320 | tf_op jit(solution)/shard_map/ppermute | solution.py:165
  88.0 2.1 %collective-permute-start.6 = (bf16[128,2176]{1,0:T(8,128)(2,1)S(1)}, bf16[128,2176]{1,0:T(8,128)(2,1)S(1)}, u32[]{:S(2)}, u32[]{:S(2)}) collective-permute-start(bf16[128,2176]{1,0:T(8,128)(2,1)S(1)} %collective-permute-done.5.xa.refs_2_), channel_id=1, source_target_pairs={{0,4},{4,8},{8,12},{12,14},{14,10},{10,6},{6,2},{2,0},{5,1},{9,5},... | collective-permute-start | bytes 1671176 | tf_op jit(solution)/shard_map/ppermute | solution.py:165
  90.1 0.2 add_convert_fusion.2
  90.3 1.6 %collective-permute-start.33 = (bf16[128,2048]{1,0:T(8,128)(2,1)S(1)}, bf16[128,2048]{1,0:T(8,128)(2,1)S(1)}, u32[]{:S(2)}, u32[]{:S(2)}) collective-permute-start(bf16[128,2048]{1,0:T(8,128)(2,1)S(1)} %add_convert_fusion.2), channel_id=1, source_target_pairs={{0,4},{4,8},{8,12},{12,14},{14,10},{10,6},{6,2},{2,0},{5,1},{9,5},... | collective-permute-start | bytes 1572872 | tf_op jit(solution)/shard_map/ppermute | solution.py:165
  91.9 1.7 %collective-permute-done.25.oa.refs_8_ = bf16[128,2048]{1,0:T(8,128)(2,1)S(1)} collective-permute-done((bf16[128,2048]{1,0:T(8,128)(2,1)S(1)}, bf16[128,2048]{1,0:T(8,128)(2,1)S(1)}, u32[]{:S(2)}, u32[]{:S(2)}) %collective-permute-start.25) | collective-permute-done | bytes 524320 | tf_op jit(solution)/shard_map/ppermute | solution.py:165
  93.6 0.5 collective-permute-start.39
  94.1 2.8 %block_pair.13 = (bf16[128,2048]{1,0:T(8,128)(2,1)S(1)}, bf16[128,2048]{1,0:T(8,128)(2,1)S(1)}, bf16[256,768]{1,0:T(8,128)(2,1)S(1)}, bf16[256,384]{1,0:T(8,128)(2,1)S(1)}) custom-call(s32[1]{0:T(128)} %bitcast.me, bf16[128,2176]{1,0:T(8,128)(2,1)S(1)} %collective-permute-done.4.xa.refs_0_, bf16[128,2176]{1,0:T(8,128)(2,1)S(1)} %collective-permute-done.28.xb.refs_1_, ...), custom_call_target="tpu_custom_call" | custom-call | flops 32212254720 | bytes 7864320 | tf_op jit(solution)/shard_map/block_pair/pallas_call | solution.py:69
  97.0 2.1 %collective-permute-start.30 = (bf16[128,2048]{1,0:T(8,128)(2,1)S(1)}, bf16[128,2048]{1,0:T(8,128)(2,1)S(1)}, u32[]{:S(2)}, u32[]{:S(2)}) collective-permute-start(bf16[128,2048]{1,0:T(8,128)(2,1)S(1)} %collective-permute-done.25.oa.refs_8_), channel_id=1, source_target_pairs={{0,4},{4,8},{8,12},{12,14},{14,10},{10,6},{6,2},{2,0},{5,1},{9,5},... | collective-permute-start | bytes 1572872 | tf_op jit(solution)/shard_map/ppermute | solution.py:165
  99.1 7.8 %wgrad_group.2 = (f32[2048,384]{1,0:T(8,128)S(1)}, f32[2048,384]{1,0:T(8,128)S(1)}, f32[384,2048]{1,0:T(8,128)S(1)}) custom-call(bf16[128,2176]{1,0:T(8,128)(2,1)S(1)} %fusion.1.xa.refs_0_, bf16[128,2176]{1,0:T(8,128)(2,1)S(1)} %collective-permute-done.7.xb.refs_1_, bf16[128,2176]{1,0:T(8,128)(2,1)S(1)} %collective-permute-done.xa.refs_2_, ...), custom_call_target="tpu_custom_call" | custom-call | flops 6039797760 | bytes 19922944 | tf_op jit(solution)/shard_map/wgrad_group/pallas_call | solution.py:128
  107.1 1.3 add_convert_fusion.1
  108.4 1.8 %collective-permute-start.37 = (bf16[128,2048]{1,0:T(8,128)(2,1)S(1)}, bf16[128,2048]{1,0:T(8,128)(2,1)S(1)}, u32[]{:S(2)}, u32[]{:S(2)}) collective-permute-start(bf16[128,2048]{1,0:T(8,128)(2,1)S(1)} %add_convert_fusion.1), channel_id=1, source_target_pairs={{0,4},{4,8},{8,12},{12,14},{14,10},{10,6},{6,2},{2,0},{5,1},{9,5},... | collective-permute-start | bytes 1572872 | tf_op jit(solution)/shard_map/ppermute | solution.py:165
  110.1 0.7 collective-permute-done.30.oa.refs_10_
  110.8 0.5 collective-permute-start.36
  111.3 2.8 %block_pair.15 = (bf16[128,2048]{1,0:T(8,128)(2,1)S(1)}, bf16[128,2048]{1,0:T(8,128)(2,1)S(1)}, bf16[256,768]{1,0:T(8,128)(2,1)S(1)}, bf16[256,384]{1,0:T(8,128)(2,1)S(1)}) custom-call(s32[1]{0:T(128)} %bitcast.me, bf16[128,2176]{1,0:T(8,128)(2,1)S(1)} %collective-permute-done.5.xa.refs_2_, bf16[128,2176]{1,0:T(8,128)(2,1)S(1)} %collective-permute-done.38.xb.refs_3_, ...), custom_call_target="tpu_custom_call" | custom-call | flops 32212254720 | bytes 7864320 | tf_op jit(solution)/shard_map/block_pair/pallas_call | solution.py:69
  114.2 2.8 %block_pair.14 = (bf16[128,2048]{1,0:T(8,128)(2,1)S(1)}, bf16[128,2048]{1,0:T(8,128)(2,1)S(1)}, bf16[256,768]{1,0:T(8,128)(2,1)S(1)}, bf16[256,384]{1,0:T(8,128)(2,1)S(1)}) custom-call(s32[1]{0:T(128)} %bitcast.me, bf16[128,2176]{1,0:T(8,128)(2,1)S(1)} %collective-permute-done.6.xa.refs_4_, bf16[128,2176]{1,0:T(8,128)(2,1)S(1)} %collective-permute-done.35.xb.refs_5_, ...), custom_call_target="tpu_custom_call" | custom-call | flops 32212254720 | bytes 7864320 | tf_op jit(solution)/shard_map/block_pair/pallas_call | solution.py:69
  117.0 0.8 collective-permute-done.37
  118.1 1.8 %collective-permute-start.41 = (bf16[64,2048]{1,0:T(8,128)(2,1)S(1)}, bf16[64,2048]{1,0:T(8,128)(2,1)S(1)}, u32[]{:S(2)}, u32[]{:S(2)}) collective-permute-start(bf16[64,2048]{1,0:T(8,128)(2,1)S(1)} %get-tuple-element.124), channel_id=1, source_target_pairs={{0,4},{4,8},{8,12},{12,14},{14,10},{10,6},{6,2},{2,0},{5,1},{9,5},... | collective-permute-start | bytes 786440 | tf_op jit(solution)/shard_map/ppermute | solution.py:165
  119.9 1.6 %collective-permute-start.44 = (bf16[64,2048]{1,0:T(8,128)(2,1)S(1)}, bf16[64,2048]{1,0:T(8,128)(2,1)S(1)}, u32[]{:S(2)}, u32[]{:S(2)}) collective-permute-start(bf16[64,2048]{1,0:T(8,128)(2,1)S(1)} %get-tuple-element.125), channel_id=1, source_target_pairs={{0,4},{4,8},{8,12},{12,14},{14,10},{10,6},{6,2},{2,0},{5,1},{9,5},... | collective-permute-start | bytes 786440 | tf_op jit(solution)/shard_map/ppermute | solution.py:165
  121.6 2.9 %collective-permute-done.41 = bf16[64,2048]{1,0:T(8,128)(2,1)S(1)} collective-permute-done((bf16[64,2048]{1,0:T(8,128)(2,1)S(1)}, bf16[64,2048]{1,0:T(8,128)(2,1)S(1)}, u32[]{:S(2)}, u32[]{:S(2)}) %collective-permute-start.41) | collective-permute-done | bytes 262176 | tf_op jit(solution)/shard_map/ppermute | solution.py:165
  124.6 1.8 %collective-permute-start.43 = (bf16[64,2048]{1,0:T(8,128)(2,1)S(1)}, bf16[64,2048]{1,0:T(8,128)(2,1)S(1)}, u32[]{:S(2)}, u32[]{:S(2)}) collective-permute-start(bf16[64,2048]{1,0:T(8,128)(2,1)S(1)} %fusion.4), channel_id=1, source_target_pairs={{0,4},{4,8},{8,12},{12,14},{14,10},{10,6},{6,2},{2,0},{5,1},{9,5},... | collective-permute-start | bytes 786440 | tf_op jit(solution)/shard_map/ppermute | solution.py:165
  126.4 0.9 collective-permute-done.44
  127.4 1.8 %collective-permute-start.45 = (bf16[64,2048]{1,0:T(8,128)(2,1)S(1)}, bf16[64,2048]{1,0:T(8,128)(2,1)S(1)}, u32[]{:S(2)}, u32[]{:S(2)}) collective-permute-start(bf16[64,2048]{1,0:T(8,128)(2,1)S(1)} %fusion.2), channel_id=1, source_target_pairs={{0,4},{4,8},{8,12},{12,14},{14,10},{10,6},{6,2},{2,0},{5,1},{9,5},... | collective-permute-start | bytes 786440 | tf_op jit(solution)/shard_map/ppermute | solution.py:165
  129.2 5.3 %wgrad_group.3 = (bf16[2048,384]{1,0:T(8,128)(2,1)}, bf16[2048,384]{1,0:T(8,128)(2,1)}, bf16[384,2048]{1,0:T(8,128)(2,1)}) custom-call(bf16[128,2176]{1,0:T(8,128)(2,1)S(1)} %collective-permute-done.4.xa.refs_0_, bf16[128,2176]{1,0:T(8,128)(2,1)S(1)} %collective-permute-done.28.xb.refs_1_, bf16[128,2176]{1,0:T(8,128)(2,1)S(1)} %collective-permute-done.5.xa.refs_2_, ...), custom_call_target="tpu_custom_call" | custom-call | flops 3623878656 | bytes 15728640 | tf_op jit(solution)/shard_map/wgrad_group/pallas_call | solution.py:128
  134.5 1.0 add_convert_fusion
  (61 shorter events, 1.8 us)
Async XLA Ops:
  2.6 3.3 %collective-permute-start.7 = (bf16[128,2176]{1,0:T(8,128)(2,1)S(1)}, bf16[128,2176]{1,0:T(8,128)(2,1)S(1)}, u32[]{:S(2)}, u32[]{:S(2)}) collective-permute-start(bf16[128,2176]{1,0:T(8,128)(2,1)S(1)} %fusion.1.xa.refs_0_), channel_id=1, source_target_pairs={{0,1},{1,0},{2,3},{3,2},{4,5},{5,4},{6,7},{7,6},{8,9},{9,8},{10,11... | collective-permute-start | bytes 1671176 | tf_op jit(solution)/shard_map/ppermute | solution.py:168
  3.1 10.1 %collective-permute-start = (bf16[128,2176]{1,0:T(8,128)(2,1)S(1)}, bf16[128,2176]{1,0:T(8,128)(2,1)S(1)}, u32[]{:S(2)}, u32[]{:S(2)}) collective-permute-start(bf16[128,2176]{1,0:T(8,128)(2,1)S(1)} %fusion.1.xa.refs_0_), channel_id=1, source_target_pairs={{0,4},{4,8},{8,12},{12,14},{14,10},{10,6},{6,2},{2,0},{5,1},{9,5},... | collective-permute-start | bytes 1671176 | tf_op jit(solution)/shard_map/ppermute | solution.py:165
  5.7 9.5 %collective-permute-start.9 = (bf16[128,2048]{1,0:T(8,128)(2,1)}, bf16[128,2048]{1,0:T(8,128)(2,1)}, u32[]{:S(2)}, u32[]{:S(2)}) collective-permute-start(bf16[128,2048]{1,0:T(8,128)(2,1)} %refs_10_), channel_id=1, source_target_pairs={{0,1},{1,0},{2,3},{3,2},{4,5},{5,4},{6,7},{7,6},{8,9},{9,8},{10,11... | collective-permute-start | bytes 1572872 | tf_op jit(solution)/shard_map/ppermute | solution.py:168
  5.9 2.3 %copy-start.1 = (bf16[128,2048]{1,0:T(8,128)(2,1)S(1)}, bf16[128,2048]{1,0:T(8,128)(2,1)}, u32[]{:S(2)}) copy-start(bf16[128,2048]{1,0:T(8,128)(2,1)} %refs_10_) | copy-start | bytes 1572868
  5.9 9.4 %copy-start = (bf16[1,384,2048]{2,1,0:T(8,128)(2,1)S(1)}, bf16[1,384,2048]{2,1,0:T(8,128)(2,1)}, u32[]{:S(2)}) copy-start(bf16[1,384,2048]{2,1,0:T(8,128)(2,1)} %param.13) | copy-start | bytes 4718596
  8.2 11.0 %collective-permute-start.8 = (bf16[128,2048]{1,0:T(8,128)(2,1)S(1)}, bf16[128,2048]{1,0:T(8,128)(2,1)S(1)}, u32[]{:S(2)}, u32[]{:S(2)}) collective-permute-start(bf16[128,2048]{1,0:T(8,128)(2,1)S(1)} %copy-done.1), channel_id=1, source_target_pairs={{0,4},{4,8},{8,12},{12,14},{14,10},{10,6},{6,2},{2,0},{5,1},{9,5},... | collective-permute-start | bytes 1572872 | tf_op jit(solution)/shard_map/ppermute | solution.py:165
  13.2 11.6 %collective-permute-start.1 = (bf16[128,2176]{1,0:T(8,128)(2,1)S(1)}, bf16[128,2176]{1,0:T(8,128)(2,1)S(1)}, u32[]{:S(2)}, u32[]{:S(2)}) collective-permute-start(bf16[128,2176]{1,0:T(8,128)(2,1)S(1)} %collective-permute-done.xa.refs_2_), channel_id=1, source_target_pairs={{0,4},{4,8},{8,12},{12,14},{14,10},{10,6},{6,2},{2,0},{5,1},{9,5},... | collective-permute-start | bytes 1671176 | tf_op jit(solution)/shard_map/ppermute | solution.py:165
  19.1 7.8 %collective-permute-start.11 = (bf16[128,2176]{1,0:T(8,128)(2,1)S(1)}, bf16[128,2176]{1,0:T(8,128)(2,1)S(1)}, u32[]{:S(2)}, u32[]{:S(2)}) collective-permute-start(bf16[128,2176]{1,0:T(8,128)(2,1)S(1)} %collective-permute-done.xa.refs_2_), channel_id=1, source_target_pairs={{0,1},{1,0},{2,3},{3,2},{4,5},{5,4},{6,7},{7,6},{8,9},{9,8},{10,11... | collective-permute-start | bytes 1671176 | tf_op jit(solution)/shard_map/ppermute | solution.py:168
  19.2 7.7 %collective-permute-start.12 = (bf16[128,2048]{1,0:T(8,128)(2,1)S(1)}, bf16[128,2048]{1,0:T(8,128)(2,1)S(1)}, u32[]{:S(2)}, u32[]{:S(2)}) collective-permute-start(bf16[128,2048]{1,0:T(8,128)(2,1)S(1)} %collective-permute-done.8.oa.refs_12_), channel_id=1, source_target_pairs={{0,1},{1,0},{2,3},{3,2},{4,5},{5,4},{6,7},{7,6},{8,9},{9,8},{10,11... | collective-permute-start | bytes 1572872 | tf_op jit(solution)/shard_map/ppermute | solution.py:168
  19.7 10.7 %collective-permute-start.10 = (bf16[128,2048]{1,0:T(8,128)(2,1)S(1)}, bf16[128,2048]{1,0:T(8,128)(2,1)S(1)}, u32[]{:S(2)}, u32[]{:S(2)}) collective-permute-start(bf16[128,2048]{1,0:T(8,128)(2,1)S(1)} %collective-permute-done.8.oa.refs_12_), channel_id=1, source_target_pairs={{0,4},{4,8},{8,12},{12,14},{14,10},{10,6},{6,2},{2,0},{5,1},{9,5},... | collective-permute-start | bytes 1572872 | tf_op jit(solution)/shard_map/ppermute | solution.py:165
  24.8 11.6 %collective-permute-start.2 = (bf16[128,2176]{1,0:T(8,128)(2,1)S(1)}, bf16[128,2176]{1,0:T(8,128)(2,1)S(1)}, u32[]{:S(2)}, u32[]{:S(2)}) collective-permute-start(bf16[128,2176]{1,0:T(8,128)(2,1)S(1)} %collective-permute-done.1.xa.refs_4_), channel_id=1, source_target_pairs={{0,4},{4,8},{8,12},{12,14},{14,10},{10,6},{6,2},{2,0},{5,1},{9,5},... | collective-permute-start | bytes 1671176 | tf_op jit(solution)/shard_map/ppermute | solution.py:165
  29.7 8.8 %collective-permute-start.17 = (bf16[128,2048]{1,0:T(8,128)(2,1)S(1)}, bf16[128,2048]{1,0:T(8,128)(2,1)S(1)}, u32[]{:S(2)}, u32[]{:S(2)}) collective-permute-start(bf16[128,2048]{1,0:T(8,128)(2,1)S(1)} %get-tuple-element.71), channel_id=1, source_target_pairs={{0,1},{1,0},{2,3},{3,2},{4,5},{5,4},{6,7},{7,6},{8,9},{9,8},{10,11... | collective-permute-start | bytes 1572872 | tf_op jit(solution)/shard_map/ppermute | solution.py:168
  30.4 9.8 %collective-permute-start.14 = (bf16[128,2176]{1,0:T(8,128)(2,1)S(1)}, bf16[128,2176]{1,0:T(8,128)(2,1)S(1)}, u32[]{:S(2)}, u32[]{:S(2)}) collective-permute-start(bf16[128,2176]{1,0:T(8,128)(2,1)S(1)} %collective-permute-done.1.xa.refs_4_), channel_id=1, source_target_pairs={{0,1},{1,0},{2,3},{3,2},{4,5},{5,4},{6,7},{7,6},{8,9},{9,8},{10,11... | collective-permute-start | bytes 1671176 | tf_op jit(solution)/shard_map/ppermute | solution.py:168
  30.4 9.8 %collective-permute-start.15 = (bf16[128,2048]{1,0:T(8,128)(2,1)S(1)}, bf16[128,2048]{1,0:T(8,128)(2,1)S(1)}, u32[]{:S(2)}, u32[]{:S(2)}) collective-permute-start(bf16[128,2048]{1,0:T(8,128)(2,1)S(1)} %collective-permute-done.10.oa.refs_14_), channel_id=1, source_target_pairs={{0,1},{1,0},{2,3},{3,2},{4,5},{5,4},{6,7},{7,6},{8,9},{9,8},{10,11... | collective-permute-start | bytes 1572872 | tf_op jit(solution)/shard_map/ppermute | solution.py:168
  30.9 12.2 %collective-permute-start.13 = (bf16[128,2048]{1,0:T(8,128)(2,1)S(1)}, bf16[128,2048]{1,0:T(8,128)(2,1)S(1)}, u32[]{:S(2)}, u32[]{:S(2)}) collective-permute-start(bf16[128,2048]{1,0:T(8,128)(2,1)S(1)} %collective-permute-done.10.oa.refs_14_), channel_id=1, source_target_pairs={{0,4},{4,8},{8,12},{12,14},{14,10},{10,6},{6,2},{2,0},{5,1},{9,5},... | collective-permute-start | bytes 1572872 | tf_op jit(solution)/shard_map/ppermute | solution.py:165
  36.4 11.6 %collective-permute-start.3 = (bf16[128,2176]{1,0:T(8,128)(2,1)S(1)}, bf16[128,2176]{1,0:T(8,128)(2,1)S(1)}, u32[]{:S(2)}, u32[]{:S(2)}) collective-permute-start(bf16[128,2176]{1,0:T(8,128)(2,1)S(1)} %collective-permute-done.2.xa.refs_6_), channel_id=1, source_target_pairs={{0,4},{4,8},{8,12},{12,14},{14,10},{10,6},{6,2},{2,0},{5,1},{9,5},... | collective-permute-start | bytes 1671176 | tf_op jit(solution)/shard_map/ppermute | solution.py:165
  38.6 15.0 %collective-permute-start.21 = (bf16[128,2048]{1,0:T(8,128)(2,1)S(1)}, bf16[128,2048]{1,0:T(8,128)(2,1)S(1)}, u32[]{:S(2)}, u32[]{:S(2)}) collective-permute-start(bf16[128,2048]{1,0:T(8,128)(2,1)S(1)} %add_convert_fusion.5), channel_id=1, source_target_pairs={{0,4},{4,8},{8,12},{12,14},{14,10},{10,6},{6,2},{2,0},{5,1},{9,5},... | collective-permute-start | bytes 1572872 | tf_op jit(solution)/shard_map/ppermute | solution.py:165
  43.0 12.7 %collective-permute-start.22 = (bf16[128,2048]{1,0:T(8,128)(2,1)S(1)}, bf16[128,2048]{1,0:T(8,128)(2,1)S(1)}, u32[]{:S(2)}, u32[]{:S(2)}) collective-permute-start(bf16[128,2048]{1,0:T(8,128)(2,1)S(1)} %get-tuple-element.74), channel_id=1, source_target_pairs={{0,1},{1,0},{2,3},{3,2},{4,5},{5,4},{6,7},{7,6},{8,9},{9,8},{10,11... | collective-permute-start | bytes 1572872 | tf_op jit(solution)/shard_map/ppermute | solution.py:168
  43.1 14.5 %collective-permute-start.18 = (bf16[128,2176]{1,0:T(8,128)(2,1)S(1)}, bf16[128,2176]{1,0:T(8,128)(2,1)S(1)}, u32[]{:S(2)}, u32[]{:S(2)}) collective-permute-start(bf16[128,2176]{1,0:T(8,128)(2,1)S(1)} %collective-permute-done.2.xa.refs_6_), channel_id=1, source_target_pairs={{0,1},{1,0},{2,3},{3,2},{4,5},{5,4},{6,7},{7,6},{8,9},{9,8},{10,11... | collective-permute-start | bytes 1671176 | tf_op jit(solution)/shard_map/ppermute | solution.py:168
  43.6 14.0 %collective-permute-start.19 = (bf16[128,2048]{1,0:T(8,128)(2,1)S(1)}, bf16[128,2048]{1,0:T(8,128)(2,1)S(1)}, u32[]{:S(2)}, u32[]{:S(2)}) collective-permute-start(bf16[128,2048]{1,0:T(8,128)(2,1)S(1)} %collective-permute-done.13.oa.refs_16_), channel_id=1, source_target_pairs={{0,1},{1,0},{2,3},{3,2},{4,5},{5,4},{6,7},{7,6},{8,9},{9,8},{10,11... | collective-permute-start | bytes 1572872 | tf_op jit(solution)/shard_map/ppermute | solution.py:168
  48.0 12.4 %collective-permute-start.16 = (bf16[128,2048]{1,0:T(8,128)(2,1)S(1)}, bf16[128,2048]{1,0:T(8,128)(2,1)S(1)}, u32[]{:S(2)}, u32[]{:S(2)}) collective-permute-start(bf16[128,2048]{1,0:T(8,128)(2,1)S(1)} %collective-permute-done.13.oa.refs_16_), channel_id=1, source_target_pairs={{0,4},{4,8},{8,12},{12,14},{14,10},{10,6},{6,2},{2,0},{5,1},{9,5},... | collective-permute-start | bytes 1572872 | tf_op jit(solution)/shard_map/ppermute | solution.py:165
  53.6 11.6 %collective-permute-start.4 = (bf16[128,2176]{1,0:T(8,128)(2,1)S(1)}, bf16[128,2176]{1,0:T(8,128)(2,1)S(1)}, u32[]{:S(2)}, u32[]{:S(2)}) collective-permute-start(bf16[128,2176]{1,0:T(8,128)(2,1)S(1)} %collective-permute-done.3.xa.refs_8_), channel_id=1, source_target_pairs={{0,4},{4,8},{8,12},{12,14},{14,10},{10,6},{6,2},{2,0},{5,1},{9,5},... | collective-permute-start | bytes 1671176 | tf_op jit(solution)/shard_map/ppermute | solution.py:165
  55.9 14.9 %collective-permute-start.26 = (bf16[128,2048]{1,0:T(8,128)(2,1)S(1)}, bf16[128,2048]{1,0:T(8,128)(2,1)S(1)}, u32[]{:S(2)}, u32[]{:S(2)}) collective-permute-start(bf16[128,2048]{1,0:T(8,128)(2,1)S(1)} %add_convert_fusion.4), channel_id=1, source_target_pairs={{0,4},{4,8},{8,12},{12,14},{14,10},{10,6},{6,2},{2,0},{5,1},{9,5},... | collective-permute-start | bytes 1572872 | tf_op jit(solution)/shard_map/ppermute | solution.py:165
  60.3 12.5 %collective-permute-start.27 = (bf16[128,2048]{1,0:T(8,128)(2,1)S(1)}, bf16[128,2048]{1,0:T(8,128)(2,1)S(1)}, u32[]{:S(2)}, u32[]{:S(2)}) collective-permute-start(bf16[128,2048]{1,0:T(8,128)(2,1)S(1)} %get-tuple-element.78), channel_id=1, source_target_pairs={{0,1},{1,0},{2,3},{3,2},{4,5},{5,4},{6,7},{7,6},{8,9},{9,8},{10,11... | collective-permute-start | bytes 1572872 | tf_op jit(solution)/shard_map/ppermute | solution.py:168
  60.4 14.5 %collective-permute-start.23 = (bf16[128,2176]{1,0:T(8,128)(2,1)S(1)}, bf16[128,2176]{1,0:T(8,128)(2,1)S(1)}, u32[]{:S(2)}, u32[]{:S(2)}) collective-permute-start(bf16[128,2176]{1,0:T(8,128)(2,1)S(1)} %collective-permute-done.3.xa.refs_8_), channel_id=1, source_target_pairs={{0,1},{1,0},{2,3},{3,2},{4,5},{5,4},{6,7},{7,6},{8,9},{9,8},{10,11... | collective-permute-start | bytes 1671176 | tf_op jit(solution)/shard_map/ppermute | solution.py:168
  60.9 14.0 %collective-permute-start.24 = (bf16[128,2048]{1,0:T(8,128)(2,1)S(1)}, bf16[128,2048]{1,0:T(8,128)(2,1)S(1)}, u32[]{:S(2)}, u32[]{:S(2)}) collective-permute-start(bf16[128,2048]{1,0:T(8,128)(2,1)S(1)} %collective-permute-done.16.oa.refs_18_), channel_id=1, source_target_pairs={{0,1},{1,0},{2,3},{3,2},{4,5},{5,4},{6,7},{7,6},{8,9},{9,8},{10,11... | collective-permute-start | bytes 1572872 | tf_op jit(solution)/shard_map/ppermute | solution.py:168
  65.2 12.6 %collective-permute-start.20 = (bf16[128,2048]{1,0:T(8,128)(2,1)S(1)}, bf16[128,2048]{1,0:T(8,128)(2,1)S(1)}, u32[]{:S(2)}, u32[]{:S(2)}) collective-permute-start(bf16[128,2048]{1,0:T(8,128)(2,1)S(1)} %collective-permute-done.16.oa.refs_18_), channel_id=1, source_target_pairs={{0,4},{4,8},{8,12},{12,14},{14,10},{10,6},{6,2},{2,0},{5,1},{9,5},... | collective-permute-start | bytes 1572872 | tf_op jit(solution)/shard_map/ppermute | solution.py:165
  70.8 11.6 %collective-permute-start.5 = (bf16[128,2176]{1,0:T(8,128)(2,1)S(1)}, bf16[128,2176]{1,0:T(8,128)(2,1)S(1)}, u32[]{:S(2)}, u32[]{:S(2)}) collective-permute-start(bf16[128,2176]{1,0:T(8,128)(2,1)S(1)} %collective-permute-done.4.xa.refs_0_), channel_id=1, source_target_pairs={{0,4},{4,8},{8,12},{12,14},{14,10},{10,6},{6,2},{2,0},{5,1},{9,5},... | collective-permute-start | bytes 1671176 | tf_op jit(solution)/shard_map/ppermute | solution.py:165
  73.1 14.9 %collective-permute-start.31 = (bf16[128,2048]{1,0:T(8,128)(2,1)S(1)}, bf16[128,2048]{1,0:T(8,128)(2,1)S(1)}, u32[]{:S(2)}, u32[]{:S(2)}) collective-permute-start(bf16[128,2048]{1,0:T(8,128)(2,1)S(1)} %add_convert_fusion.3), channel_id=1, source_target_pairs={{0,4},{4,8},{8,12},{12,14},{14,10},{10,6},{6,2},{2,0},{5,1},{9,5},... | collective-permute-start | bytes 1572872 | tf_op jit(solution)/shard_map/ppermute | solution.py:165
  77.7 12.4 %collective-permute-start.32 = (bf16[128,2048]{1,0:T(8,128)(2,1)S(1)}, bf16[128,2048]{1,0:T(8,128)(2,1)S(1)}, u32[]{:S(2)}, u32[]{:S(2)}) collective-permute-start(bf16[128,2048]{1,0:T(8,128)(2,1)S(1)} %get-tuple-element.82), channel_id=1, source_target_pairs={{0,1},{1,0},{2,3},{3,2},{4,5},{5,4},{6,7},{7,6},{8,9},{9,8},{10,11... | collective-permute-start | bytes 1572872 | tf_op jit(solution)/shard_map/ppermute | solution.py:168
  77.8 16.3 %collective-permute-start.28 = (bf16[128,2176]{1,0:T(8,128)(2,1)S(1)}, bf16[128,2176]{1,0:T(8,128)(2,1)S(1)}, u32[]{:S(2)}, u32[]{:S(2)}) collective-permute-start(bf16[128,2176]{1,0:T(8,128)(2,1)S(1)} %collective-permute-done.4.xa.refs_0_), channel_id=1, source_target_pairs={{0,1},{1,0},{2,3},{3,2},{4,5},{5,4},{6,7},{7,6},{8,9},{9,8},{10,11... | collective-permute-start | bytes 1671176 | tf_op jit(solution)/shard_map/ppermute | solution.py:168
  78.3 15.3 %collective-permute-start.25 = (bf16[128,2048]{1,0:T(8,128)(2,1)S(1)}, bf16[128,2048]{1,0:T(8,128)(2,1)S(1)}, u32[]{:S(2)}, u32[]{:S(2)}) collective-permute-start(bf16[128,2048]{1,0:T(8,128)(2,1)S(1)} %collective-permute-done.20.oa.refs_6_), channel_id=1, source_target_pairs={{0,4},{4,8},{8,12},{12,14},{14,10},{10,6},{6,2},{2,0},{5,1},{9,5},... | collective-permute-start | bytes 1572872 | tf_op jit(solution)/shard_map/ppermute | solution.py:165
  82.4 11.2 %collective-permute-start.29 = (bf16[128,2048]{1,0:T(8,128)(2,1)S(1)}, bf16[128,2048]{1,0:T(8,128)(2,1)S(1)}, u32[]{:S(2)}, u32[]{:S(2)}) collective-permute-start(bf16[128,2048]{1,0:T(8,128)(2,1)S(1)} %collective-permute-done.20.oa.refs_6_), channel_id=1, source_target_pairs={{0,1},{1,0},{2,3},{3,2},{4,5},{5,4},{6,7},{7,6},{8,9},{9,8},{10,11... | collective-permute-start | bytes 1572872 | tf_op jit(solution)/shard_map/ppermute | solution.py:168
  88.0 22.2 %collective-permute-start.6 = (bf16[128,2176]{1,0:T(8,128)(2,1)S(1)}, bf16[128,2176]{1,0:T(8,128)(2,1)S(1)}, u32[]{:S(2)}, u32[]{:S(2)}) collective-permute-start(bf16[128,2176]{1,0:T(8,128)(2,1)S(1)} %collective-permute-done.5.xa.refs_2_), channel_id=1, source_target_pairs={{0,4},{4,8},{8,12},{12,14},{14,10},{10,6},{6,2},{2,0},{5,1},{9,5},... | collective-permute-start | bytes 1671176 | tf_op jit(solution)/shard_map/ppermute | solution.py:165
  90.3 16.6 %collective-permute-start.33 = (bf16[128,2048]{1,0:T(8,128)(2,1)S(1)}, bf16[128,2048]{1,0:T(8,128)(2,1)S(1)}, u32[]{:S(2)}, u32[]{:S(2)}) collective-permute-start(bf16[128,2048]{1,0:T(8,128)(2,1)S(1)} %add_convert_fusion.2), channel_id=1, source_target_pairs={{0,4},{4,8},{8,12},{12,14},{14,10},{10,6},{6,2},{2,0},{5,1},{9,5},... | collective-permute-start | bytes 1572872 | tf_op jit(solution)/shard_map/ppermute | solution.py:165
  93.6 17.7 %collective-permute-start.38 = (bf16[128,2176]{1,0:T(8,128)(2,1)S(1)}, bf16[128,2176]{1,0:T(8,128)(2,1)S(1)}, u32[]{:S(2)}, u32[]{:S(2)}) collective-permute-start(bf16[128,2176]{1,0:T(8,128)(2,1)S(1)} %collective-permute-done.5.xa.refs_2_), channel_id=1, source_target_pairs={{0,1},{1,0},{2,3},{3,2},{4,5},{5,4},{6,7},{7,6},{8,9},{9,8},{10,11... | collective-permute-start | bytes 1671176 | tf_op jit(solution)/shard_map/ppermute | solution.py:168
  93.6 3.4 %collective-permute-start.39 = (bf16[128,2048]{1,0:T(8,128)(2,1)S(1)}, bf16[128,2048]{1,0:T(8,128)(2,1)S(1)}, u32[]{:S(2)}, u32[]{:S(2)}) collective-permute-start(bf16[128,2048]{1,0:T(8,128)(2,1)S(1)} %collective-permute-done.25.oa.refs_8_), channel_id=1, source_target_pairs={{0,1},{1,0},{2,3},{3,2},{4,5},{5,4},{6,7},{7,6},{8,9},{9,8},{10,11... | collective-permute-start | bytes 1572872 | tf_op jit(solution)/shard_map/ppermute | solution.py:168
  96.9 10.2 %collective-permute-start.34 = (bf16[128,2048]{1,0:T(8,128)(2,1)S(1)}, bf16[128,2048]{1,0:T(8,128)(2,1)}, u32[]{:S(2)}, u32[]{:S(2)}) collective-permute-start(bf16[128,2048]{1,0:T(8,128)(2,1)S(1)} %get-tuple-element.86), channel_id=1, source_target_pairs={{0,1},{1,0},{2,3},{3,2},{4,5},{5,4},{6,7},{7,6},{8,9},{9,8},{10,11... | collective-permute-start | bytes 1572872 | tf_op jit(solution)/shard_map/ppermute | solution.py:168
  97.0 13.8 %collective-permute-start.30 = (bf16[128,2048]{1,0:T(8,128)(2,1)S(1)}, bf16[128,2048]{1,0:T(8,128)(2,1)S(1)}, u32[]{:S(2)}, u32[]{:S(2)}) collective-permute-start(bf16[128,2048]{1,0:T(8,128)(2,1)S(1)} %collective-permute-done.25.oa.refs_8_), channel_id=1, source_target_pairs={{0,4},{4,8},{8,12},{12,14},{14,10},{10,6},{6,2},{2,0},{5,1},{9,5},... | collective-permute-start | bytes 1572872 | tf_op jit(solution)/shard_map/ppermute | solution.py:165
  106.9 27.5 %collective-permute-start.46 = (bf16[128,2048]{1,0:T(8,128)(2,1)S(1)}, bf16[128,2048]{1,0:T(8,128)(2,1)S(1)}, u32[]{:S(2)}, u32[]{:S(2)}) collective-permute-start(bf16[128,2048]{1,0:T(8,128)(2,1)S(1)} %get-tuple-element.68), channel_id=1, source_target_pairs={{0,1},{1,0},{2,3},{3,2},{4,5},{5,4},{6,7},{7,6},{8,9},{9,8},{10,11... | collective-permute-start | bytes 1572872 | tf_op jit(solution)/shard_map/ppermute | solution.py:168
  108.4 9.5 %collective-permute-start.37 = (bf16[128,2048]{1,0:T(8,128)(2,1)S(1)}, bf16[128,2048]{1,0:T(8,128)(2,1)S(1)}, u32[]{:S(2)}, u32[]{:S(2)}) collective-permute-start(bf16[128,2048]{1,0:T(8,128)(2,1)S(1)} %add_convert_fusion.1), channel_id=1, source_target_pairs={{0,4},{4,8},{8,12},{12,14},{14,10},{10,6},{6,2},{2,0},{5,1},{9,5},... | collective-permute-start | bytes 1572872 | tf_op jit(solution)/shard_map/ppermute | solution.py:165
  110.8 3.4 %collective-permute-start.35 = (bf16[128,2176]{1,0:T(8,128)(2,1)S(1)}, bf16[128,2176]{1,0:T(8,128)(2,1)S(1)}, u32[]{:S(2)}, u32[]{:S(2)}) collective-permute-start(bf16[128,2176]{1,0:T(8,128)(2,1)S(1)} %collective-permute-done.6.xa.refs_4_), channel_id=1, source_target_pairs={{0,1},{1,0},{2,3},{3,2},{4,5},{5,4},{6,7},{7,6},{8,9},{9,8},{10,11... | collective-permute-start | bytes 1671176 | tf_op jit(solution)/shard_map/ppermute | solution.py:168
  110.8 3.4 %collective-permute-start.36 = (bf16[128,2048]{1,0:T(8,128)(2,1)S(1)}, bf16[128,2048]{1,0:T(8,128)(2,1)S(1)}, u32[]{:S(2)}, u32[]{:S(2)}) collective-permute-start(bf16[128,2048]{1,0:T(8,128)(2,1)S(1)} %collective-permute-done.30.oa.refs_10_), channel_id=1, source_target_pairs={{0,1},{1,0},{2,3},{3,2},{4,5},{5,4},{6,7},{7,6},{8,9},{9,8},{10,11... | collective-permute-start | bytes 1572872 | tf_op jit(solution)/shard_map/ppermute | solution.py:168
  114.1 3.7 %collective-permute-start.40 = (bf16[128,2048]{1,0:T(8,128)(2,1)S(1)}, bf16[128,2048]{1,0:T(8,128)(2,1)S(1)}, u32[]{:S(2)}, u32[]{:S(2)}) collective-permute-start(bf16[128,2048]{1,0:T(8,128)(2,1)S(1)} %get-tuple-element.110), channel_id=1, source_target_pairs={{0,1},{1,0},{2,3},{3,2},{4,5},{5,4},{6,7},{7,6},{8,9},{9,8},{10,11... | collective-permute-start | bytes 1572872 | tf_op jit(solution)/shard_map/ppermute | solution.py:168
  117.8 3.7 %collective-permute-start.42 = (bf16[128,2048]{1,0:T(8,128)(2,1)S(1)}, bf16[128,2048]{1,0:T(8,128)(2,1)S(1)}, u32[]{:S(2)}, u32[]{:S(2)}) collective-permute-start(bf16[128,2048]{1,0:T(8,128)(2,1)S(1)} %get-tuple-element.112), channel_id=1, source_target_pairs={{0,1},{1,0},{2,3},{3,2},{4,5},{5,4},{6,7},{7,6},{8,9},{9,8},{10,11... | collective-permute-start | bytes 1572872 | tf_op jit(solution)/shard_map/ppermute | solution.py:168
  118.1 6.4 %collective-permute-start.41 = (bf16[64,2048]{1,0:T(8,128)(2,1)S(1)}, bf16[64,2048]{1,0:T(8,128)(2,1)S(1)}, u32[]{:S(2)}, u32[]{:S(2)}) collective-permute-start(bf16[64,2048]{1,0:T(8,128)(2,1)S(1)} %get-tuple-element.124), channel_id=1, source_target_pairs={{0,4},{4,8},{8,12},{12,14},{14,10},{10,6},{6,2},{2,0},{5,1},{9,5},... | collective-permute-start | bytes 786440 | tf_op jit(solution)/shard_map/ppermute | solution.py:165
  119.9 7.4 %collective-permute-start.44 = (bf16[64,2048]{1,0:T(8,128)(2,1)S(1)}, bf16[64,2048]{1,0:T(8,128)(2,1)S(1)}, u32[]{:S(2)}, u32[]{:S(2)}) collective-permute-start(bf16[64,2048]{1,0:T(8,128)(2,1)S(1)} %get-tuple-element.125), channel_id=1, source_target_pairs={{0,4},{4,8},{8,12},{12,14},{14,10},{10,6},{6,2},{2,0},{5,1},{9,5},... | collective-permute-start | bytes 786440 | tf_op jit(solution)/shard_map/ppermute | solution.py:165
  124.6 9.9 %collective-permute-start.43 = (bf16[64,2048]{1,0:T(8,128)(2,1)S(1)}, bf16[64,2048]{1,0:T(8,128)(2,1)S(1)}, u32[]{:S(2)}, u32[]{:S(2)}) collective-permute-start(bf16[64,2048]{1,0:T(8,128)(2,1)S(1)} %fusion.4), channel_id=1, source_target_pairs={{0,4},{4,8},{8,12},{12,14},{14,10},{10,6},{6,2},{2,0},{5,1},{9,5},... | collective-permute-start | bytes 786440 | tf_op jit(solution)/shard_map/ppermute | solution.py:165
  127.4 7.1 %collective-permute-start.45 = (bf16[64,2048]{1,0:T(8,128)(2,1)S(1)}, bf16[64,2048]{1,0:T(8,128)(2,1)S(1)}, u32[]{:S(2)}, u32[]{:S(2)}) collective-permute-start(bf16[64,2048]{1,0:T(8,128)(2,1)S(1)} %fusion.2), channel_id=1, source_target_pairs={{0,4},{4,8},{8,12},{12,14},{14,10},{10,6},{6,2},{2,0},{5,1},{9,5},... | collective-permute-start | bytes 786440 | tf_op jit(solution)/shard_map/ppermute | solution.py:165
